TPU v7x, 32 devices: a whole 2x2x4 slice. The times are simulated.
32 devices in a mesh: brick: 2 (over core), chain: 16 (over z, y, x).
Axes of the slice: x: 2, y: 2, z: 4, core: 2. Of those that a mesh axis runs over, the one named last changes fastest.
Arguments:
- populations: float32 [19, 4, 512, 128], P(None, 'brick', 'chain'), may hold values from 0.5 to 1.5
- positions: float32 [2, 16, 3, 64, 256], P('brick', 'chain'), may hold values from -0.4 to 0.4
- bead_site: int32 [2, 16, 64, 256], P('brick', 'chain'), may hold values from 0 to 127
- chain_slots: int32 [2, 16, 4, 256], P('brick', 'chain'), may hold values from 0 to 2047, as said below
- send_rows: int32 [2, 16, 16, 128], P('brick', 'chain'), may hold values from 0 to 63
- send_count: int32 [2, 16, 16], P('brick', 'chain'), may hold values from 32 to 128, as said below
- migrate_list: int32 [2, 16, 2, 8], P('brick', 'chain'), may hold values from 0 to 255
- migrate_count: int32 [2, 16, 2], P('brick', 'chain'), may hold values from 0 to 8, as said below
Outputs:
- read: float32 [19, 4, 512, 128], P(None, 'brick', 'chain')
- new_positions: float32 [2, 16, 3, 64, 256], P('brick', 'chain')
- arrivals: float32 [2, 16, 2, 1536], P('brick', 'chain')
Inputs may be any that keep to these rules, and one draw needn't show every extreme that they name: `send_count`: in every brick one group receives 128 live slots from every group of that brick. `chain_slots`: each entry is p * 128 + s for a group p of the same brick and a slot s below send_count[b, p, c] of this device's brick b and group c. `migrate_count`: no chain leaves for its own brick; for every group one brick receives 8 chains from every other brick.
All inputs are finite; a program needn't handle non-finite values.
Results may differ from a plain program's by a relative error of at most 0.00086.
Values may be sent and summed in bfloat16 or wider, within the bound.
No kernel may reach another device: no remote copies, remote signals or barrier semaphores. Data moves between devices by JAX's collectives and lax.ppermute only.
A program may use at most 64 MiB of HBM per device.

v0:
```python
import math

import jax
import jax.numpy as jnp
import numpy as np
from jax import lax
from jax.sharding import PartitionSpec as P

LATTICE_VECTORS = np.array(
    [
        [0, 0, 0],
        [1, 0, 0],
        [-1, 0, 0],
        [0, 1, 0],
        [0, -1, 0],
        [0, 0, 1],
        [0, 0, -1],
        [1, 1, 0],
        [-1, -1, 0],
        [1, -1, 0],
        [-1, 1, 0],
        [1, 0, 1],
        [-1, 0, -1],
        [1, 0, -1],
        [-1, 0, 1],
        [0, 1, 1],
        [0, -1, -1],
        [0, 1, -1],
        [0, -1, 1],
    ],
    np.int32,
)
WEIGHT_TABLE = np.array([1.0 / 3.0] + [1.0 / 18.0] * 6 + [1.0 / 36.0] * 12)
TAU_RELAX = 0.8
SPRING = 0.5
MAX_STRETCH = 4.0
highest = lax.Precision.HIGHEST


def with_halo(value, sides, width):
    for axis, dim in sides:
        peers, length = (lax.axis_size(axis), value.shape[dim])
        up = [(i, (i + 1) % peers) for i in range(peers)]
        down = [(j, i) for i, j in up]
        last = lax.slice_in_dim(value, length - width, length, axis=dim)
        first = lax.slice_in_dim(value, 0, width, axis=dim)
        before = lax.ppermute(last, axis, up)
        after = lax.ppermute(first, axis, down)
        value = jnp.concatenate([before, value, after], axis=dim)
    return value


def lattice_tables():
    return (jnp.array(LATTICE_VECTORS, jnp.float32), jnp.array(WEIGHT_TABLE, jnp.float32))


def moments(populations):
    vectors, weights = lattice_tables()
    density = jnp.einsum("i,ixyz->xyz", weights, populations, precision=highest)
    momentum = jnp.einsum(
        "ic,ixyz->cxyz", weights[:, None] * vectors, populations, precision=highest
    )
    return (density, momentum)


def collide(populations, density, momentum, force_field):
    vectors, weights = lattice_tables()
    velocity = (momentum + TAU_RELAX * force_field) / density
    projected = jnp.einsum("ic,cxyz->ixyz", vectors, velocity, precision=highest)
    square = jnp.sum(velocity * velocity, axis=0)
    balance = density * (1.0 + 3.0 * projected + 4.5 * projected * projected - 1.5 * square)
    return populations - (populations - balance) / TAU_RELAX


def stream(padded, size_x, size_y):
    outputs = []
    for direction in range(19):
        shift_x, shift_y, shift_z = [int(value) for value in LATTICE_VECTORS[direction]]
        rolled = jnp.roll(padded[direction], shift_z, axis=-1)
        outputs.append(
            rolled[1 - shift_x : 1 - shift_x + size_x, 1 - shift_y : 1 - shift_y + size_y]
        )
    return jnp.stack(outputs)


def rouse_tables(bead_count):
    mode_index = jnp.arange(bead_count).astype(jnp.float32)
    mode_basis = math.sqrt(2.0 / bead_count) * jnp.cos(
        math.pi * mode_index[:, None] * (mode_index[None, :] + 0.5) / bead_count
    )
    first_row = jnp.full((1, bead_count), math.sqrt(1.0 / bead_count), jnp.float32)
    mode_basis = jnp.concatenate([first_row, mode_basis[1:]], axis=0)
    spectrum = 4.0 * jnp.sin(math.pi * mode_index / (2.0 * bead_count)) ** 2
    return (mode_basis, spectrum)


def onehot_sum(index, values, count):
    table = (index[:, None] == jnp.arange(count)[None, :]).astype(values.dtype)
    if values.dtype == jnp.float32:
        return lax.dot_general(
            table,
            values,
            (((0,), (0,)), ((), ())),
            precision=highest,
            preferred_element_type=jnp.float32,
        )
    return lax.dot_general(
        table, values, (((0,), (0,)), ((), ())), preferred_element_type=jnp.float32
    )


def chain_step(received, positions, sites, slots):
    row_length = received.shape[-1]
    bead_count = positions.shape[1]
    chains = positions.shape[2]
    slot_count = slots.shape[0]
    per_slot = bead_count // slot_count
    centre = sites.reshape(slot_count, per_slot, chains)[..., None]
    site_axis = jnp.arange(row_length)[None, None, None, :]
    kernel = 0.5 * (site_axis == centre).astype(jnp.float32)
    kernel = kernel + 0.25 * (site_axis == (centre + 1) % row_length).astype(jnp.float32)
    kernel = kernel + 0.25 * (site_axis == (centre + row_length - 1) % row_length).astype(
        jnp.float32
    )
    slot_rows = received[slots]
    bead_velocity = jnp.einsum(
        "rjns,rncs->crjn",
        kernel.astype(jnp.bfloat16),
        slot_rows,
        preferred_element_type=jnp.float32,
    ).reshape(3, bead_count, chains)
    bond_vectors = positions[:, 1:, :] - positions[:, :-1, :]
    stretch = jnp.sum(bond_vectors * bond_vectors, axis=(0, 1)) / (bead_count - 1)
    stiffness = SPRING / (1.0 - stretch / MAX_STRETCH)
    mode_basis, spectrum = rouse_tables(bead_count)
    mode_amps = jnp.einsum("pj,cjn->cpn", mode_basis, positions + bead_velocity, precision=highest)
    mode_amps = mode_amps / (1.0 + stiffness[None, None, :] * spectrum[None, :, None])
    moved_beads = jnp.einsum("pj,cpn->cjn", mode_basis, mode_amps, precision=highest)
    bead_force = bead_velocity - (moved_beads - positions)
    spread = -jnp.einsum(
        "rjns,crjn->rncs",
        kernel,
        bead_force.reshape(3, slot_count, per_slot, chains),
        precision=highest,
    )
    slot_force = onehot_sum(
        slots.reshape(-1), spread.reshape(-1, 3 * row_length), received.shape[0]
    )
    return (moved_beads, slot_force.reshape(received.shape[0], 3, row_length).astype(jnp.bfloat16))


def local(
    populations,
    positions,
    bead_site,
    chain_slots,
    send_rows,
    send_count,
    migrate_list,
    migrate_count,
):
    size_x = populations.shape[1]
    size_y = populations.shape[2]
    length = populations.shape[3]
    row_count = size_x * size_y
    groups = lax.axis_size("chain")
    capacity = send_rows.shape[-1]
    density, momentum = moments(populations)
    velocity = momentum / density
    row_field = velocity.transpose(1, 2, 0, 3).reshape(row_count, 3, length).astype(jnp.bfloat16)
    slot_range = jnp.arange(capacity)
    own_rows = send_rows[0, 0]
    own_counts = send_count[0, 0]
    live_slot = slot_range[None, :] < own_counts[:, None]
    packed = jnp.where(
        live_slot[:, :, None, None], row_field[own_rows], jnp.zeros((), jnp.bfloat16)
    )
    arrived = lax.all_to_all(packed, "chain", split_axis=0, concat_axis=0, tiled=True)
    received = arrived.reshape(groups * capacity, 3, length)
    moved_beads, slot_force = chain_step(
        received, positions[0, 0], bead_site[0, 0], chain_slots[0, 0]
    )
    returned = lax.all_to_all(
        slot_force.reshape(groups, capacity, 3, length),
        "chain",
        split_axis=0,
        concat_axis=0,
        tiled=True,
    )
    slot_values = jnp.where(live_slot[:, :, None, None], returned, jnp.zeros((), jnp.bfloat16))
    force_rows = onehot_sum(
        own_rows.reshape(-1), slot_values.reshape(-1, 3 * length), row_count
    ).reshape(row_count, 3, length)
    force_field = force_rows.reshape(size_x, size_y, 3, length).transpose(2, 0, 1, 3)
    collided = with_halo(
        collide(populations, density, momentum, force_field), (("brick", 1), ("chain", 2)), 1
    )
    read = stream(collided, size_x, size_y)
    targets = migrate_list[0, 0]
    bricks = targets.shape[0]
    slots_out = targets.shape[1]
    chosen = (
        moved_beads[:, :, targets.reshape(-1)]
        .reshape(3, moved_beads.shape[1], bricks, slots_out)
        .transpose(2, 3, 0, 1)
    )
    kept_slot = jnp.arange(slots_out)[None, :] < migrate_count[0, 0][:, None]
    outgoing = jnp.where(kept_slot[:, :, None, None], chosen, jnp.zeros((), jnp.float32)).reshape(
        bricks, -1
    )
    arrivals = lax.all_to_all(outgoing, "brick", split_axis=0, concat_axis=0, tiled=True)
    return (read, moved_beads[None, None], arrivals[None, None])


def solution(mesh):
    placed = (
        P(None, "brick", "chain", None),
        P("brick", "chain", None, None, None),
        P("brick", "chain", None, None),
        P("brick", "chain", None, None),
        P("brick", "chain", None, None),
        P("brick", "chain", None),
        P("brick", "chain", None, None),
        P("brick", "chain", None),
    )
    return jax.shard_map(
        local,
        mesh=mesh,
        in_specs=placed,
        out_specs=(
            P(None, "brick", "chain", None),
            P("brick", "chain", None, None, None),
            P("brick", "chain", None, None),
        ),
        check_vma=False,
    )
```

profile of v0, /device:TPU:0, one launch (start us, length us, event | category | flops | bytes accessed | tf_op | source)
XLA Modules:
  0.0 176.0 jit_solution(3439130432045923648)
XLA Ops:
  0.6 1.9 %fusion.27 = f32[1,2,32,128]{3,0,2,1:T(1,128)S(1)} fusion(f32[19,1,1,1]{0,1,3,2:T(1,128)} %constant.102, f32[19,2,32,128]{3,2,1,0:T(8,128)} %param.11), kind=kOutput, calls=%fused_computation.36 | convolution fusion | flops 1867776 | bytes 655436 | tf_op jit(solution)/shard_map/i,ixyz->xyz/dot_general | solution.py:59
  2.6 1.9 %fusion.25 = f32[3,2,32,128]{3,0,2,1:T(4,128)S(1)} fusion(f32[19,3,1,1]{0,1,3,2:T(4,128)} %constant.104, f32[19,2,32,128]{3,2,1,0:T(8,128)} %param.11), kind=kOutput, calls=%fused_computation.34 | convolution fusion | flops 5603328 | bytes 721124 | tf_op jit(solution)/shard_map/ic,ixyz->cxyz/dot_general | solution.py:60
  4.6 6.9 %gather_fusion = bf16[2048,3,128]{2,1,0:T(4,128)(2,1)S(1)} fusion(bf16[64,3,128]{2,1,0:T(4,128)(2,1)S(1)} %copy.1176, s32[2048]{0:T(1024)S(1)} %fusion.60), kind=kCustom, calls=%fused_computation | custom fusion | bytes 3153920 | tf_op jit(solution)/shard_map/gather | solution.py:176
  11.5 0.2 copy.1177
  11.8 0.4 copy-done.8
  12.2 0.4 broadcast_select_fusion.1
  12.7 1.6 copy.1178
  14.3 8.5 %all-to-all-start = ((bf16[16,128,3,128]{1,3,2,0:T(8,128)(2,1)}), bf16[16,128,3,128]{1,3,2,0:T(8,128)(2,1)S(1)}, u32[]{:S(2)}, u32[]{:S(2)}) async-start(bf16[16,128,3,128]{1,3,2,0:T(8,128)(2,1)} %copy.1178), calls=%async_computation | async-start | bytes 3145728 | tf_op jit(solution)/shard_map/all_to_all | solution.py:178
  22.8 1.0 copy.1180
  23.9 1.0 copy.1181
  24.9 1.0 copy.1182
  26.1 0.2 cosine_multiply_fusion
  26.3 0.7 multiply_add_fusion
  27.0 29.9 %all-to-all-done = bf16[16,128,3,128]{1,3,2,0:T(8,128)(2,1)S(1)} async-done(((bf16[16,128,3,128]{1,3,2,0:T(8,128)(2,1)}), bf16[16,128,3,128]{1,3,2,0:T(8,128)(2,1)S(1)}, u32[]{:S(2)}, u32[]{:S(2)}) %all-to-all-start) | async-done | bytes 1572896 | tf_op jit(solution)/shard_map/all_to_all | solution.py:178
  56.9 2.5 %copy.1179 = bf16[16,128,3,128]{3,2,1,0:T(4,128)(2,1)} copy(bf16[16,128,3,128]{1,3,2,0:T(8,128)(2,1)S(1)} %all-to-all-done) | data formatting | bytes 3145728 | tf_op jit(solution)/shard_map/all_to_all | solution.py:178
  59.4 5.1 %gather_fusion.1 = bf16[1024,3,128]{2,1,0:T(4,128)(2,1)S(1)} fusion(bf16[2048,3,128]{2,1,0:T(4,128)(2,1)} %bitcast.256, s32[1024]{0:T(1024)S(1)} %broadcast_clamp_fusion), kind=kCustom, calls=%fused_computation.1 | custom fusion | bytes 1576960 | tf_op jit(solution)/shard_map/gather | solution.py:125
  64.5 13.5 %fusion.17 = f32[3,4,16,256]{2,0,3,1:T(4,128)S(1)} fusion(bf16[4,256,3,128]{3,2,1,0:T(4,128)(2,1)S(1)} %bitcast.261, s32[4,16,256]{1,2,0:T(8,128)} %copy.1182, s32[4,16,256]{1,2,0:T(8,128)} %copy.1181, s32[4,16,256]{1,2,0:T(8,128)} %copy.1180), kind=kOutput, calls=%fused_computation.21 | convolution fusion | flops 31457280 | bytes 1179648 | tf_op jit(solution)/shard_map/rjns,rncs->crjn/dot_general | solution.py:126
  78.0 0.6 copy.1183
  78.7 0.2 copy-done.5
  78.9 0.3 fusion.21
  79.2 0.4 bitcast_subtract_fusion
  79.6 0.8 copy.1185
  80.4 20.6 %fusion.20 = f32[4,256,3,128]{3,2,1,0:T(4,128)S(1)} fusion(f32[3,4,16,256]{2,0,3,1:T(4,128)S(1)} %copy.1185, s32[4,16,256]{1,2,0:T(8,128)} %copy.1182, s32[4,16,256]{1,2,0:T(8,128)} %copy.1181, s32[4,16,256]{1,2,0:T(8,128)S(1)} %copy-done.3), kind=kOutput, calls=%fused_computation.26 | convolution fusion | flops 92667904 | bytes 1966080 | tf_op jit(solution)/shard_map/rjns,crjn->rncs/dot_general | solution.py:140
  101.2 0.5 copy.1226
  101.6 6.7 %fusion.14 = bf16[2048,3,128]{2,0,1:T(8,128)(2,1)S(1)} fusion(f32[3,128,1024]{2,1,0:T(8,128)S(1)} %bitcast.259, s32[1024]{0:T(1024)S(1)} %bitcast.293), kind=kOutput, calls=%fused_computation.20 | convolution fusion | flops 9666560000 | bytes 3149824 | tf_op jit(solution)/shard_map/dot_general | solution.py:100
  108.4 1.6 copy.1187
  110.0 7.9 %all-to-all-start.1 = ((bf16[16,128,3,128]{1,3,2,0:T(8,128)(2,1)}), bf16[16,128,3,128]{1,3,2,0:T(8,128)(2,1)S(1)}, u32[]{:S(2)}, u32[]{:S(2)}) async-start(bf16[16,128,3,128]{1,3,2,0:T(8,128)(2,1)} %copy.1187), calls=%async_computation.1 | async-start | bytes 3145728 | tf_op jit(solution)/shard_map/all_to_all | solution.py:183
  118.0 33.4 %all-to-all-done.1 = bf16[16,128,3,128]{1,3,2,0:T(8,128)(2,1)S(1)} async-done(((bf16[16,128,3,128]{1,3,2,0:T(8,128)(2,1)}), bf16[16,128,3,128]{1,3,2,0:T(8,128)(2,1)S(1)}, u32[]{:S(2)}, u32[]{:S(2)}) %all-to-all-start.1) | async-done | bytes 1572896 | tf_op jit(solution)/shard_map/all_to_all | solution.py:183
  151.4 0.9 copy.1188
  152.3 1.4 broadcast_select_fusion
  153.7 2.1 %copy.1189 = bf16[16,128,3,128]{1,0,3,2:T(8,128)(2,1)S(1)} copy(bf16[16,128,3,128]{3,1,0,2:T(8,128)(2,1)} %broadcast_select_fusion) | data formatting | bytes 3145728 | tf_op jit(solution)/shard_map/jit(_where)/select_n | solution.py:190
  155.9 0.4 copy.1269
  156.3 0.6 multiply_reduce_fusion
  157.0 1.3 copy_subtract_fusion.1
  158.4 0.5 collective-permute-start.1
  159.0 0.2 copy.1213
  159.2 0.6 gather_fusion.2
  159.8 0.3 collective-permute-done
  160.1 0.6 collective-permute-done.1
  160.7 0.7 collective-permute-start.2
  161.4 5.2 %collective-permute-start.3 = (f32[19,4,1,128]{3,0,2,1:T(8,128)S(1)}, f32[19,4,1,128]{3,0,2,1:T(8,128)S(1)}, u32[]{:S(2)}, u32[]{:S(2)}) collective-permute-start(f32[19,4,1,128]{3,0,2,1:T(8,128)S(1)} %get-tuple-element.40), channel_id=1, source_target_pairs={{1,0},{2,1},{3,2},{4,3},{5,4},{6,5},{7,6},{8,7},{9,8},{10,9},{11,1... | collective-permute-start | bytes 116744 | tf_op jit(solution)/shard_map/ppermute | solution.py:48
  166.8 3.7 %all_to_all.20 = f32[2,1,1536]{2,1,0:T(1,128)S(1)} all-to-all(f32[2,1,1536]{2,1,0:T(1,128)S(1)} %all_to_all.16), channel_id=1, replica_groups=mesh['brick'=2,'chain'=16] {'brick'}, dimensions={0} | all-to-all | bytes 24576 | tf_op jit(solution)/shard_map/all_to_all | solution.py:211
  170.5 0.6 copy.1218
  171.1 0.1 pad_maximum_fusion
  171.5 0.2 pad_maximum_fusion.6
  172.0 0.2 pad_maximum_fusion.9
  172.8 0.2 pad_maximum_fusion.18
  175.1 0.9 copy.1217
  (99 shorter events, 4.2 us)
Async XLA Ops:
  0.6 4.0 %copy-start.6 = (s32[1,1,16,128]{3,2,1,0:T(8,128)S(1)}, s32[1,1,16,128]{3,2,1,0:T(8,128)}, u32[]{:S(2)}) copy-start(s32[1,1,16,128]{3,2,1,0:T(8,128)} %param.15) | copy-start | bytes 24580
  11.5 0.7 copy-start.8
  14.3 8.5 %copy-start.7 = (s32[1,1,4,256]{3,2,1,0:T(4,128)S(1)}, s32[1,1,4,256]{3,2,1,0:T(4,128)}, u32[]{:S(2)}) copy-start(s32[1,1,4,256]{3,2,1,0:T(4,128)} %param.14) | copy-start | bytes 12292
  14.3 8.5 %copy-start.4 = (s32[1,1,64,256]{3,2,1,0:T(8,128)S(1)}, s32[1,1,64,256]{3,2,1,0:T(8,128)}, u32[]{:S(2)}) copy-start(s32[1,1,64,256]{3,2,1,0:T(8,128)} %param.13) | copy-start | bytes 196612
  14.3 11.7 %copy-start.1 = (f32[1,1,3,64,256]{4,3,2,1,0:T(8,128)S(1)}, f32[1,1,3,64,256]{4,3,2,1,0:T(8,128)}, u32[]{:S(2)}) copy-start(f32[1,1,3,64,256]{4,3,2,1,0:T(8,128)} %param.12) | copy-start | bytes 589828
  14.3 42.6 %all-to-all-start = ((bf16[16,128,3,128]{1,3,2,0:T(8,128)(2,1)}), bf16[16,128,3,128]{1,3,2,0:T(8,128)(2,1)S(1)}, u32[]{:S(2)}, u32[]{:S(2)}) async-start(bf16[16,128,3,128]{1,3,2,0:T(8,128)(2,1)} %copy.1178), calls=%async_computation | async-start | bytes 3145728 | tf_op jit(solution)/shard_map/all_to_all | solution.py:178
  78.0 0.8 copy-start.5
  78.9 1.6 copy-start.3
  79.6 79.4 %copy-start.2 = (f32[3,256,64]{1,2,0:T(8,128)}, f32[3,256,64]{1,2,0:T(8,128)S(1)}, u32[]{:S(2)}) copy-start(f32[3,256,64]{1,2,0:T(8,128)S(1)} %get-tuple-element.46) | copy-start | bytes 589828
  110.0 7.9 %copy-start.9 = (s32[1,1,2,8]{3,2,1,0:T(2,128)S(1)}, s32[1,1,2,8]{3,2,1,0:T(2,128)}, u32[]{:S(2)}) copy-start(s32[1,1,2,8]{3,2,1,0:T(2,128)} %param.17) | copy-start | bytes 196
  110.0 41.4 %all-to-all-start.1 = ((bf16[16,128,3,128]{1,3,2,0:T(8,128)(2,1)}), bf16[16,128,3,128]{1,3,2,0:T(8,128)(2,1)S(1)}, u32[]{:S(2)}, u32[]{:S(2)}) async-start(bf16[16,128,3,128]{1,3,2,0:T(8,128)(2,1)} %copy.1187), calls=%async_computation.1 | async-start | bytes 3145728 | tf_op jit(solution)/shard_map/all_to_all | solution.py:183
  155.9 1.1 copy-start
  155.9 1.1 copy-start.11
  156.9 2.0 %copy-start.10 = (s32[1,1,2]{2,1,0:T(1,128)S(1)}, s32[1,1,2]{2,1,0:T(1,128)}, u32[]{:S(2)}) copy-start(s32[1,1,2]{2,1,0:T(1,128)} %param.18) | copy-start | bytes 28
  158.3 1.8 %collective-permute-start = (f32[19,1,32,128]{3,0,2,1:T(8,128)S(1)}, f32[19,1,32,128]{3,0,2,1:T(8,128)S(1)}, u32[]{:S(2)}, u32[]{:S(2)}) collective-permute-start(f32[19,1,32,128]{3,0,2,1:T(8,128)S(1)} %get-tuple-element.41), channel_id=1, source_target_pairs={{0,16},{16,0},{1,17},{17,1},{2,18},{18,2},{3,19},{19,3},{4,20},{20... | collective-permute-start | bytes 933896 | tf_op jit(solution)/shard_map/ppermute | solution.py:47
  158.4 2.3 %collective-permute-start.1 = (f32[19,1,32,128]{3,0,2,1:T(8,128)S(1)}, f32[19,1,32,128]{3,0,2,1:T(8,128)S(1)}, u32[]{:S(2)}, u32[]{:S(2)}) collective-permute-start(f32[19,1,32,128]{3,0,2,1:T(8,128)S(1)} %get-tuple-element.42), channel_id=1, source_target_pairs={{16,0},{0,16},{17,1},{1,17},{18,2},{2,18},{19,3},{3,19},{20,4},{4,... | collective-permute-start | bytes 933896 | tf_op jit(solution)/shard_map/ppermute | solution.py:48
  160.7 10.4 %collective-permute-start.2 = (f32[19,4,1,128]{3,0,2,1:T(8,128)S(1)}, f32[19,4,1,128]{3,0,2,1:T(8,128)S(1)}, u32[]{:S(2)}, u32[]{:S(2)}) collective-permute-start(f32[19,4,1,128]{3,0,2,1:T(8,128)S(1)} %get-tuple-element.39), channel_id=1, source_target_pairs={{0,1},{1,2},{2,3},{3,4},{4,5},{5,6},{6,7},{7,8},{8,9},{9,10},{10,1... | collective-permute-start | bytes 116744 | tf_op jit(solution)/shard_map/ppermute | solution.py:47
  161.4 9.7 %collective-permute-start.3 = (f32[19,4,1,128]{3,0,2,1:T(8,128)S(1)}, f32[19,4,1,128]{3,0,2,1:T(8,128)S(1)}, u32[]{:S(2)}, u32[]{:S(2)}) collective-permute-start(f32[19,4,1,128]{3,0,2,1:T(8,128)S(1)} %get-tuple-element.40), channel_id=1, source_target_pairs={{1,0},{2,1},{3,2},{4,3},{5,4},{6,5},{7,6},{8,7},{9,8},{10,9},{11,1... | collective-permute-start | bytes 116744 | tf_op jit(solution)/shard_map/ppermute | solution.py:48
where the time goes:
time: 177 us; the launch traced here: 176 us
  waiting for transfers between devices  64.1 us (36%)
  matrix products  47.2 us (27%)
  local copies, waits for them, and re-layouts  31.4 us (18%)
  starting transfers between devices  22.9 us (13%)
  other arithmetic  5.37 us (3%)
  blocking collectives  3.72 us (2%)
    all_to_all x1, waiting for transfers between devices, local(): lax.all_to_all(slot_force.reshape(groups, capacity, 3, length), 'chain',...  33.4 us
    all_to_all x1, waiting for transfers between devices, local(): lax.all_to_all(packed, 'chain', split_axis=0, concat_axis=0, tiled=True)  29.9 us
    dot_general x1, matrix products, chain_step(): jnp.einsum('rjns,crjn->rncs', kernel, bead_force.reshape(3, slot_count, p...  20.6 us
    dot_general x1, matrix products, chain_step(): jnp.einsum('rjns,rncs->crjn', kernel.astype(jnp.bfloat16), slot_rows, pre...  13.5 us
    all_to_all x1, starting transfers between devices, local(): lax.all_to_all(packed, 'chain', split_axis=0, concat_axis=0, tiled=True)  8.47 us
    all_to_all x1, starting transfers between devices, local(): lax.all_to_all(slot_force.reshape(groups, capacity, 3, length), 'chain',...  7.89 us
    gather x2, local copies, waits for them, and re-layouts, local(): row_field[own_rows]  7.08 us
    dot_general x1, matrix products, onehot_sum(): lax.dot_general(table, values, (((0,), (0,)), ((), ())), precision=highes...  6.73 us
  transfers between devices with their start and end apart: 6, of which 4 were waited for; matrix products, arithmetic and copies ran while one was open for 3% of the time, Pallas kernels for 0%

commit v1 on v0

v1 whole, which is shorter than its diff:
```python
import functools
import math

import jax
import jax.numpy as jnp
import numpy as np
from jax import lax
from jax.experimental import pallas as pl
from jax.experimental.pallas import tpu as pltpu
from jax.sharding import PartitionSpec as P

LATTICE_VECTORS = np.array(
    [
        [0, 0, 0],
        [1, 0, 0],
        [-1, 0, 0],
        [0, 1, 0],
        [0, -1, 0],
        [0, 0, 1],
        [0, 0, -1],
        [1, 1, 0],
        [-1, -1, 0],
        [1, -1, 0],
        [-1, 1, 0],
        [1, 0, 1],
        [-1, 0, -1],
        [1, 0, -1],
        [-1, 0, 1],
        [0, 1, 1],
        [0, -1, -1],
        [0, 1, -1],
        [0, -1, 1],
    ],
    np.int32,
)
WEIGHT_TABLE = [1.0 / 3.0] + [1.0 / 18.0] * 6 + [1.0 / 36.0] * 12
DIRECTIONS = len(WEIGHT_TABLE)
VECTORS = [tuple(int(v) for v in row) for row in LATTICE_VECTORS]
MOVES_UP = [i for i in range(DIRECTIONS) if VECTORS[i][1] == 1]
MOVES_DOWN = [i for i in range(DIRECTIONS) if VECTORS[i][1] == -1]
CROSSING = [i for i in range(DIRECTIONS) if VECTORS[i][0] != 0]
TAU_RELAX = 0.8
SPRING = 0.5
MAX_STRETCH = 4.0
f32 = jnp.float32
bf16 = jnp.bfloat16
highest = lax.Precision.HIGHEST
NT = (((1,), (1,)), ((), ()))
VMEM = pl.BlockSpec(memory_space=pltpu.VMEM)
SMEM = pl.BlockSpec(memory_space=pltpu.SMEM)
ANY = pl.BlockSpec(memory_space=pl.ANY)


class Plan:
    def __init__(self, groups, rows, size_y):
        self.groups = groups
        self.outer = 4
        self.inner = groups // self.outer
        self.rows = rows
        self.size_y = size_y
        self.size_x = rows // size_y
        extra = max(self.inner, 2 * self.size_x)
        self.stride = (rows + extra + 7) // 8 * 8
        self.block = self.outer * self.stride

    def outer_shift(self, k):
        z_count, w_count = self.outer, self.inner
        return [
            (z * w_count + w, (z + k) % z_count * w_count + w)
            for z in range(z_count)
            for w in range(w_count)
        ]

    def inner_swap(self, m):
        z_count, w_count = self.outer, self.inner
        return [
            (z * w_count + w, z * w_count + (w ^ m))
            for z in range(z_count)
            for w in range(w_count)
        ]


def rouse_tables(bead_count):
    mode = np.arange(bead_count, dtype=np.float64)
    basis = math.sqrt(2.0 / bead_count) * np.cos(
        math.pi * mode[:, None] * (mode[None, :] + 0.5) / bead_count
    )
    basis[0] = math.sqrt(1.0 / bead_count)
    spectrum = 4.0 * np.sin(math.pi * mode / (2.0 * bead_count)) ** 2
    return (basis.astype(np.float32), spectrum.astype(np.float32)[:, None])


def weighted_sums(get):
    density = None
    momentum = [None, None, None]
    for i in range(DIRECTIONS):
        value = get(i) * np.float32(WEIGHT_TABLE[i])
        density = value if density is None else density + value
        for k in range(3):
            sign = VECTORS[i][k]
            if sign == 0:
                continue
            term = value if sign > 0 else -value
            momentum[k] = term if momentum[k] is None else momentum[k] + term
    return (density, momentum)


def moment_kernel(plan, pop_ref, rows_ref, count_ref, *outs):
    msg_refs = outs[: plan.outer]
    up_ref, down_ref = outs[plan.outer :]
    length = pop_ref.shape[3]
    size_y = plan.size_y
    for x in range(plan.size_x):
        density, momentum = weighted_sums(lambda i: pop_ref[i, x])
        first = slice(x * size_y, (x + 1) * size_y)
        for k in range(3):
            velocity = (momentum[k] / density).astype(bf16)
            for msg in msg_refs:
                msg[first, k * length : (k + 1) * length] = velocity
        for out, moves, row in ((up_ref, MOVES_UP, size_y - 1), (down_ref, MOVES_DOWN, 0)):
            for slot, i in enumerate(moves):
                out[slot, x : x + 1, :] = pop_ref[i, x, row : row + 1, :]
            at = len(moves)
            for slot, value in enumerate([density] + momentum):
                out[at + slot, x : x + 1, :] = value[row : row + 1]
    me = lax.axis_index("chain")
    z = me // plan.inner
    w = me % plan.inner
    lane = lax.broadcasted_iota(jnp.int32, (1, length), 1)
    extra = plan.stride - plan.rows
    for k, msg in enumerate(msg_refs):
        tables = []
        for m in range(plan.inner):
            target = (z + plan.outer - k) % plan.outer * plan.inner + (w ^ m)
            row = rows_ref[pl.ds(target, 1), :]
            tables.append(jnp.where(lane < count_ref[target], row, -1).astype(f32))
        if extra > plan.inner:
            tables.append(jnp.zeros((extra - plan.inner, length), f32))
        block = jnp.concatenate(tables, axis=0).astype(bf16)
        msg[plan.rows :, :length] = block
        msg[plan.rows :, length:] = jnp.zeros((extra, 2 * length), bf16)


def chain_kernel(plan, capacity, *refs):
    block_refs = refs[: plan.inner]
    (
        pos_ref,
        site_ref,
        slot_ref,
        list_ref,
        live_ref,
        basis_ref,
        spectrum_ref,
        own_ref,
    ) = refs[plan.inner : plan.inner + 8]
    send_refs = refs[plan.inner + 8 : 2 * plan.inner + 7]
    (
        moved_ref,
        stay_ref,
        leave_ref,
        table,
        turned,
        onehot,
        smooth,
        velocity,
        force,
        spread_hi,
        spread_lo,
        sums,
    ) = refs[2 * plan.inner + 7 :]
    inner, outer, rows, stride = plan.inner, plan.outer, plan.rows, plan.stride
    groups = plan.groups
    total = inner * plan.block
    length = table.shape[1] // 3
    slots, chains = slot_ref.shape
    beads = pos_ref.shape[1]
    per_slot = beads // slots
    extra = stride - rows
    me = lax.axis_index("chain")
    z = me // inner
    w = me % inner

    table_rows = []
    for m in range(inner):
        for k in range(outer):
            base = k * stride
            to = (m * outer + k) * stride
            table[to : to + rows, :] = block_refs[m][base : base + rows, :]
            table[to + rows : to + stride, :] = jnp.zeros((extra, 3 * length), bf16)
            names = block_refs[m][base + rows : base + stride, :length].astype(f32)
            table_rows.append(names[m : m + 1])
    names = jnp.concatenate(table_rows, axis=0).astype(bf16)

    eye = (
        lax.broadcasted_iota(jnp.int32, (length, length), 0)
        == lax.broadcasted_iota(jnp.int32, (length, length), 1)
    )
    eye = jnp.where(eye, 1.0, 0.0).astype(bf16)
    for k in range(3):
        part = slice(k * length, (k + 1) * length)
        turned[part, :] = lax.dot_general(
            eye, table[:, part], NT, preferred_element_type=f32
        ).astype(bf16)

    site_iota = lax.broadcasted_iota(jnp.int32, (length, chains), 0)
    group_iota = lax.broadcasted_iota(jnp.int32, (groups, chains), 0)
    row_iota = lax.broadcasted_iota(jnp.int32, (rows, chains), 0)
    extra_iota = lax.broadcasted_iota(jnp.int32, (extra, chains), 0)

    def group_of(p):
        return ((p % inner) ^ w) * outer + (p // inner - z + outer) % outer

    for r in range(slots):
        slot = slot_ref[r : r + 1, :]
        p = slot // capacity
        s = slot % capacity
        group = group_of(p)
        pick = jnp.where(site_iota == s, 1.0, 0.0).astype(bf16)
        looked = jnp.dot(names, pick, preferred_element_type=f32)
        row = jnp.sum(jnp.where(group_iota == group, looked, 0.0), axis=0, keepdims=True)
        row = row.astype(jnp.int32)
        live = row >= 0
        y = row % plan.size_y
        x = row // plan.size_y
        first = jnp.where(live, group * stride + row, -1)
        above = group_of((p + 1) % groups) * stride + x
        below = group_of((p + groups - 1) % groups) * stride + plan.size_x + x
        second = jnp.where(y == plan.size_y - 1, above, jnp.where(y == 0, below, -stride))
        second = jnp.where(live, second, -stride)
        lanes = slice(r * chains, (r + 1) * chains)
        for g in range(groups):
            base = g * stride
            onehot[base : base + rows, lanes] = jnp.where(
                row_iota == first - base, 1.0, 0.0
            ).astype(bf16)
            onehot[base + rows : base + stride, lanes] = jnp.where(
                extra_iota == second - base, 1.0, 0.0
            ).astype(bf16)

    picked = jnp.dot(turned[...], onehot[...], preferred_element_type=f32).astype(bf16)
    near = lax.broadcasted_iota(jnp.int32, (length, length), 0)
    near = near - lax.broadcasted_iota(jnp.int32, (length, length), 1)
    around = (near == 1) | (near == -1) | (near == length - 1) | (near == 1 - length)
    kernel = jnp.where(near == 0, 0.5, jnp.where(around, 0.25, 0.0)).astype(bf16)
    for k in range(3):
        part = slice(k * length, (k + 1) * length)
        smooth[part, :] = jnp.dot(kernel, picked[part], preferred_element_type=f32)

    for r in range(slots):
        for octet in range(per_slot // 8):
            for tile in range(chains // 128):
                at = slice(r * per_slot + octet * 8, r * per_slot + octet * 8 + 8)
                lanes = slice(tile * 128, tile * 128 + 128)
                wide = slice(r * chains + tile * 128, r * chains + tile * 128 + 128)
                site = site_ref[at, lanes]
                inside = site & 7
                which = site >> 3
                for k in range(3):
                    value = jnp.zeros((8, 128), f32)
                    for t in range(length // 8):
                        rows8 = slice(k * length + t * 8, k * length + t * 8 + 8)
                        got = jnp.take_along_axis(
                            smooth[rows8, wide], inside, axis=0, mode="promise_in_bounds"
                        )
                        value = jnp.where(which == t, got, value)
                    velocity[k, at, lanes] = value

    stretch = None
    for k in range(3):
        bond = pos_ref[k, 1:, :] - pos_ref[k, : beads - 1, :]
        part = jnp.sum(bond * bond, axis=0, keepdims=True)
        stretch = part if stretch is None else stretch + part
    stretch = stretch / (beads - 1)
    stiffness = SPRING / (1.0 - stretch / MAX_STRETCH)
    damping = 1.0 / (1.0 + spectrum_ref[...] * stiffness)
    basis = basis_ref[...]
    for k in range(3):
        amps = jnp.dot(
            basis, pos_ref[k] + velocity[k], precision=highest, preferred_element_type=f32
        )
        moved = lax.dot_general(
            basis,
            amps * damping,
            (((0,), (0,)), ((), ())),
            precision=highest,
            preferred_element_type=f32,
        )
        moved_ref[k] = moved
        force[k] = (moved - pos_ref[k]) - velocity[k]

    brick = lax.axis_index("brick")
    chain_iota = lax.broadcasted_iota(jnp.int32, (1, chains), 1)
    leaving = list_ref.shape[1]
    for i, out in enumerate((stay_ref, leave_ref)):
        target = brick ^ i
        chosen = []
        for s in range(leaving):
            number = jnp.where(s < live_ref[target], list_ref[target, s], -1)
            chosen.append(jnp.where(chain_iota == number, 1.0, 0.0))
        chosen = jnp.concatenate(chosen, axis=0)
        for k in range(3):
            out[:, k * beads : (k + 1) * beads] = lax.dot_general(
                chosen, moved_ref[k], NT, precision=highest, preferred_element_type=f32
            )

    step = 32
    step_iota = lax.broadcasted_iota(jnp.int32, (step, 128), 0)
    for r in range(slots):
        for tile in range(chains // 128):
            lanes = slice(tile * 128, tile * 128 + 128)
            wide = slice(r * chains + tile * 128, r * chains + tile * 128 + 128)
            for start in range(0, length, step):
                parts = [jnp.zeros((step, 128), f32) for _ in range(3)]
                for j in range(per_slot):
                    at = slice(r * per_slot + j, r * per_slot + j + 1)
                    here = step_iota == site_ref[at, lanes] - start
                    for k in range(3):
                        parts[k] = parts[k] + jnp.where(here, force[k, at, lanes], 0.0)
                for k in range(3):
                    out = slice(k * length + start, k * length + start + step)
                    hi = parts[k].astype(bf16)
                    spread_hi[out, wide] = hi
                    spread_lo[out, wide] = (parts[k] - hi.astype(f32)).astype(bf16)

    sums[...] = lax.dot_general(
        onehot[...], spread_hi[...], NT, preferred_element_type=f32
    ) + lax.dot_general(onehot[...], spread_lo[...], NT, preferred_element_type=f32)
    own_ref[...] = sums[: plan.block, :]
    for m in range(1, inner):
        send_refs[m - 1][...] = sums[m * plan.block : (m + 1) * plan.block, :].astype(bf16)


def equilibrium(i, density, velocity, square):
    projected = None
    for k in range(3):
        sign = VECTORS[i][k]
        if sign == 0:
            continue
        term = velocity[k] if sign > 0 else -velocity[k]
        projected = term if projected is None else projected + term
    if projected is None:
        return density * (1.0 - 1.5 * square)
    return density * (1.0 + 3.0 * projected + 4.5 * projected * projected - 1.5 * square)


def collide_kernel(plan, pop_ref, *refs):
    kept_ref = refs[0]
    came_refs = refs[1 : plan.outer]
    low_ref, high_ref, read_ref, send_ref = refs[plan.outer :]
    length = pop_ref.shape[3]
    size_x, size_y, rows = plan.size_x, plan.size_y, plan.rows
    total = kept_ref[...]
    for came in came_refs:
        total = total + came[...].astype(f32)
    force = []
    for k in range(3):
        value = total[:, k * length : (k + 1) * length]
        near = pltpu.roll(value, 1, axis=1) + pltpu.roll(value, length - 1, axis=1)
        force.append(0.5 * value + 0.25 * near)

    def flow(density, momentum, field):
        velocity = [(momentum[k] + TAU_RELAX * field[k]) / density for k in range(3)]
        square = velocity[0] * velocity[0] + velocity[1] * velocity[1] + velocity[2] * velocity[2]
        return (density, velocity, square)

    def relax(i, value, state):
        return value - (value - equilibrium(i, *state)) / TAU_RELAX

    edges = {}
    for side, (ref, moves) in enumerate(((low_ref, MOVES_UP), (high_ref, MOVES_DOWN))):
        at = len(moves)
        first = rows + side * size_x
        state = flow(
            ref[at],
            [ref[at + 1], ref[at + 2], ref[at + 3]],
            [force[k][first : first + size_x] for k in range(3)],
        )
        for slot, i in enumerate(moves):
            edges[i] = relax(i, ref[slot], state)

    y_iota = lax.broadcasted_iota(jnp.int32, (size_y, length), 0)
    for x in range(size_x):
        density, momentum = weighted_sums(lambda i: pop_ref[i, x])
        state = flow(
            density, momentum, [force[k][x * size_y : (x + 1) * size_y] for k in range(3)]
        )
        for i in range(DIRECTIONS):
            shift_x, shift_y, shift_z = VECTORS[i]
            value = relax(i, pop_ref[i, x], state)
            if shift_y != 0:
                value = pltpu.roll(value, shift_y % size_y, axis=0)
                edge = jnp.broadcast_to(edges[i][x : x + 1], (size_y, length))
                value = jnp.where(y_iota == (0 if shift_y > 0 else size_y - 1), edge, value)
            if shift_z != 0:
                value = pltpu.roll(value, shift_z % length, axis=1)
            target = x + shift_x
            if 0 <= target < size_x:
                read_ref[i, target] = value
            else:
                send_ref[CROSSING.index(i)] = value


def merge_kernel(plan, came_ref, part_ref, read_ref, sem):
    del part_ref
    copies = []
    for slot, i in enumerate(CROSSING):
        target = 0 if VECTORS[i][0] > 0 else plan.size_x - 1
        copies.append(
            pltpu.make_async_copy(came_ref.at[slot], read_ref.at[i, target], sem.at[slot])
        )
    for copy in copies:
        copy.start()
    for copy in copies:
        copy.wait()


def local(
    populations,
    positions,
    bead_site,
    chain_slots,
    send_rows,
    send_count,
    migrate_list,
    migrate_count,
):
    size_x, size_y, length = populations.shape[1:]
    groups = lax.axis_size("chain")
    bricks = lax.axis_size("brick")
    capacity = send_rows.shape[-1]
    plan = Plan(groups, size_x * size_y, size_y)
    inner, outer = plan.inner, plan.outer
    beads, chains = positions.shape[3:]
    slots = chain_slots.shape[2]
    shape = jax.ShapeDtypeStruct
    width = 3 * length
    edge = shape((len(MOVES_UP) + 4, size_x, length), f32)

    first = pl.pallas_call(
        functools.partial(moment_kernel, plan),
        out_shape=[shape((plan.stride, width), bf16)] * outer + [edge, edge],
        in_specs=[VMEM, VMEM, SMEM],
        out_specs=[VMEM] * (outer + 2),
        name="moments",
    )(populations, send_rows[0, 0], send_count[0, 0])
    msgs, (edge_up, edge_down) = first[:outer], first[outer:]
    parts = [msgs[0]] + [
        lax.ppermute(msgs[k], "chain", plan.outer_shift(-k)) for k in range(1, outer)
    ]
    near = jnp.concatenate(parts, axis=0)
    blocks = [near] + [lax.ppermute(near, "chain", plan.inner_swap(m)) for m in range(1, inner)]
    up = [(i, (i + 1) % groups) for i in range(groups)]
    down = [(j, i) for i, j in up]
    low = lax.ppermute(edge_up, "chain", up)
    high = lax.ppermute(edge_down, "chain", down)

    basis, spectrum = rouse_tables(beads)
    total = inner * plan.block
    leaving = migrate_list.shape[-1]
    second = pl.pallas_call(
        functools.partial(chain_kernel, plan, capacity),
        out_shape=[shape((plan.block, width), f32)]
        + [shape((plan.block, width), bf16)] * (inner - 1)
        + [shape((3, beads, chains), f32)]
        + [shape((leaving, 3 * beads), f32)] * 2,
        in_specs=[VMEM] * (inner + 3) + [SMEM, SMEM] + [VMEM, VMEM],
        out_specs=[VMEM] * (inner + 3),
        scratch_shapes=[
            pltpu.VMEM((total, width), bf16),
            pltpu.VMEM((width, total), bf16),
            pltpu.VMEM((total, slots * chains), bf16),
            pltpu.VMEM((width, slots * chains), f32),
            pltpu.VMEM((3, beads, chains), f32),
            pltpu.VMEM((3, beads, chains), f32),
            pltpu.VMEM((width, slots * chains), bf16),
            pltpu.VMEM((width, slots * chains), bf16),
            pltpu.VMEM((total, width), f32),
        ],
        name="chains",
    )(
        *blocks,
        positions[0, 0],
        bead_site[0, 0],
        chain_slots[0, 0],
        migrate_list[0, 0],
        migrate_count[0, 0],
        basis,
        spectrum,
    )
    own, sends = second[0], second[1:inner]
    moved, stay, leave = second[inner:]
    total_force = own
    for m in range(1, inner):
        total_force = total_force + lax.ppermute(sends[m - 1], "chain", plan.inner_swap(m)).astype(
            f32
        )
    swap = [(i, (i + 1) % bricks) for i in range(bricks)]
    arrived = lax.ppermute(leave, "brick", swap)
    stride = plan.stride
    kept = total_force[:stride]
    came = [
        lax.ppermute(
            total_force[k * stride : (k + 1) * stride].astype(bf16), "chain", plan.outer_shift(k)
        )
        for k in range(1, outer)
    ]
    partial, crossing = pl.pallas_call(
        functools.partial(collide_kernel, plan),
        out_shape=[
            shape(populations.shape, f32),
            shape((len(CROSSING), size_y, length), f32),
        ],
        in_specs=[VMEM] * (outer + 3),
        out_specs=[VMEM, VMEM],
        name="collide",
    )(populations, kept, *came, low, high)
    crossed = lax.ppermute(crossing, "brick", swap)
    read = pl.pallas_call(
        functools.partial(merge_kernel, plan),
        out_shape=shape(populations.shape, f32),
        in_specs=[VMEM, ANY],
        out_specs=ANY,
        scratch_shapes=[pltpu.SemaphoreType.DMA((len(CROSSING),))],
        input_output_aliases={1: 0},
        name="merge",
    )(crossed, partial)
    here = lax.axis_index("brick")
    stay = stay.reshape(1, -1)
    arrived = arrived.reshape(1, -1)
    arrivals = jnp.where(
        here == 0,
        jnp.concatenate([stay, arrived], axis=0),
        jnp.concatenate([arrived, stay], axis=0),
    )
    return (read, moved[None, None], arrivals[None, None])


def solution(mesh):
    placed = (
        P(None, "brick", "chain", None),
        P("brick", "chain", None, None, None),
        P("brick", "chain", None, None),
        P("brick", "chain", None, None),
        P("brick", "chain", None, None),
        P("brick", "chain", None),
        P("brick", "chain", None, None),
        P("brick", "chain", None),
    )
    return jax.shard_map(
        local,
        mesh=mesh,
        in_specs=placed,
        out_specs=(
            P(None, "brick", "chain", None),
            P("brick", "chain", None, None, None),
            P("brick", "chain", None, None),
        ),
        check_vma=False,
    )
```

time: 177 us -> 70.3 us (0.40)
  matrix products: 47.2 us -> 0 us
  waiting for transfers between devices: 64.1 us -> 21.8 us
  local copies, waits for them, and re-layouts: 31.4 us -> 4.36 us
  Pallas kernels: 0 us -> 16.7 us
  blocking collectives: 3.72 us -> 0 us
  other arithmetic: 5.37 us -> 1.75 us
    all_to_all x2 -> x0, waiting for transfers between devices: 63.3 us -> none  [the longest x1 33.4 us: local(): lax.all_to_all(slot_force.reshape(groups, capacity, 3, length), 'chain',...]
    dot_general x9 -> x0, matrix products: 47.2 us -> none  [the longest x1 20.6 us: chain_step(): jnp.einsum('rjns,crjn->rncs', kernel, bead_force.reshape(3, slot_count, p...]
    ppermute x4 -> x16, waiting for transfers between devices: 0.87 us -> 21.8 us  [the longest x3 8.24 us: local(): lax.ppermute(near, 'chain', plan.inner_swap(m))]
    ppermute x4 -> x16, starting transfers between devices: 6.49 us -> 24.6 us  [the longest x3 6.34 us: local(): lax.ppermute(total_force[k * stride:(k + 1) * stride].astype(bf16), 'chai...]
    pallas_call x0 -> x4, Pallas kernels: none -> 16.7 us  [the longest x1 10.6 us: local(): pl.pallas_call(functools.partial(chain_kernel, plan, capacity), out_shape...]
    all_to_all x2 -> x0, starting transfers between devices: 16.4 us -> none  [the longest x1 8.47 us: local(): lax.all_to_all(packed, 'chain', split_axis=0, concat_axis=0, tiled=True)]
    gather x4 -> x0, local copies, waits for them, and re-layouts: 12.8 us -> none  [the longest x2 7.08 us: local(): row_field[own_rows]]
    select_n x5 -> x0, local copies, waits for them, and re-layouts: 5.8 us -> none  [the longest x1 2.14 us: local(): jnp.where(live_slot[:, :, None, None], returned, jnp.zeros((), jnp.bfloat...]
  transfers between devices with their start and end apart: 6 -> 16, of which waited for: 4 -> 10; matrix products, arithmetic and copies ran while one was open for 3% -> 3% of each run, Pallas kernels for 0% -> 0%
where the time goes in v1:
time: 70.3 us; the launch traced here: 70 us
  starting transfers between devices  24.6 us (35%)
  waiting for transfers between devices  21.8 us (31%)
  Pallas kernels  16.7 us (24%)
  local copies, waits for them, and re-layouts  4.36 us (6%)
  other arithmetic  1.75 us (2%)
  between operations  0.76 us (1%)
    pallas_call x1, Pallas kernels, local(): pl.pallas_call(functools.partial(chain_kernel, plan, capacity), out_shape...  10.6 us
    ppermute x3, waiting for transfers between devices, local(): lax.ppermute(near, 'chain', plan.inner_swap(m))  8.24 us
    ppermute x3, waiting for transfers between devices, local(): lax.ppermute(sends[m - 1], 'chain', plan.inner_swap(m)).astype(f32)  6.9 us
    ppermute x3, starting transfers between devices, local(): lax.ppermute(total_force[k * stride:(k + 1) * stride].astype(bf16), 'chai...  6.34 us
    ppermute x3, starting transfers between devices, local(): lax.ppermute(msgs[k], 'chain', plan.outer_shift(-k))  6.09 us
    ppermute x1, starting transfers between devices, local(): high = lax.ppermute(edge_down, 'chain', down)  4.51 us
    ppermute x3, waiting for transfers between devices, local(): lax.ppermute(msgs[k], 'chain', plan.outer_shift(-k))  4.31 us
    ppermute x3, starting transfers between devices, local(): lax.ppermute(near, 'chain', plan.inner_swap(m))  3.55 us
  transfers between devices with their start and end apart: 16, of which 10 were waited for; matrix products, arithmetic and copies ran while one was open for 3% of the time, Pallas kernels for 0%

profile of v1, /device:TPU:0, one launch (start us, length us, event | category | flops | bytes accessed | tf_op | source)
XLA Modules:
  0.0 70.0 jit_solution(17567926175267995229)
XLA Ops:
  0.6 1.9 %moments.1 = (bf16[72,384]{1,0:T(8,128)(2,1)}, bf16[72,384]{1,0:T(8,128)(2,1)}, bf16[72,384]{1,0:T(8,128)(2,1)}, bf16[72,384]{1,0:T(8,128)(2,1)}, f32[9,2,128]{2,1,0:T(2,128)}, /*index=5*/f32[9,2,128]{2,1,0:T(2,128)}) custom-call(f32[19,2,32,128]{3,2,1,0:T(8,128)} %pop_ref.3, s32[16,128]{1,0:T(8,128)} %bitcast.10, s32[16]{0:T(128)} %bitcast.14), custom_call_target="tpu_custom_call" | custom-call | tf_op jit(solution)/shard_map/moments/pallas_call | solution.py:439
  2.5 5.1 %collective-permute-start = (bf16[72,384]{1,0:T(8,128)(2,1)}, bf16[72,384]{1,0:T(8,128)(2,1)S(1)}, u32[]{:S(2)}, u32[]{:S(2)}) collective-permute-start(bf16[72,384]{1,0:T(8,128)(2,1)} %get-tuple-element.19), channel_id=1, source_target_pairs={{0,12},{1,13},{2,14},{3,15},{4,0},{5,1},{6,2},{7,3},{8,4},{9,5},{1... | collective-permute-start | bytes 165896 | tf_op jit(solution)/shard_map/ppermute | solution.py:448
  7.6 0.0 collective-permute-start.1
  7.6 1.0 %collective-permute-start.2 = (bf16[72,384]{1,0:T(8,128)(2,1)}, bf16[72,384]{1,0:T(8,128)(2,1)S(1)}, u32[]{:S(2)}, u32[]{:S(2)}) collective-permute-start(bf16[72,384]{1,0:T(8,128)(2,1)} %get-tuple-element.21), channel_id=1, source_target_pairs={{0,4},{1,5},{2,6},{3,7},{4,8},{5,9},{6,10},{7,11},{8,12},{9,13},{1... | collective-permute-start | bytes 165896 | tf_op jit(solution)/shard_map/ppermute | solution.py:448
  8.6 0.8 %constant_dynamic-update-slice_fusion.3 = bf16[288,384]{1,0:T(8,128)(2,1)S(1)} fusion(bf16[72,384]{1,0:T(8,128)(2,1)} %get-tuple-element.18), kind=kLoop, calls=%fused_computation.5 | loop fusion | bytes 110592
  9.4 0.7 %collective-permute-done = bf16[72,384]{1,0:T(8,128)(2,1)S(1)} collective-permute-done((bf16[72,384]{1,0:T(8,128)(2,1)}, bf16[72,384]{1,0:T(8,128)(2,1)S(1)}, u32[]{:S(2)}, u32[]{:S(2)}) %collective-permute-start) | collective-permute-done | bytes 55328 | tf_op jit(solution)/shard_map/ppermute | solution.py:448
  10.2 2.8 %collective-permute-done.1 = bf16[72,384]{1,0:T(8,128)(2,1)S(1)} collective-permute-done((bf16[72,384]{1,0:T(8,128)(2,1)}, bf16[72,384]{1,0:T(8,128)(2,1)S(1)}, u32[]{:S(2)}, u32[]{:S(2)}) %collective-permute-start.1) | collective-permute-done | bytes 55328 | tf_op jit(solution)/shard_map/ppermute | solution.py:448
  13.0 0.8 %collective-permute-done.2 = bf16[72,384]{1,0:T(8,128)(2,1)S(1)} collective-permute-done((bf16[72,384]{1,0:T(8,128)(2,1)}, bf16[72,384]{1,0:T(8,128)(2,1)S(1)}, u32[]{:S(2)}, u32[]{:S(2)}) %collective-permute-start.2) | collective-permute-done | bytes 55328 | tf_op jit(solution)/shard_map/ppermute | solution.py:448
  13.8 1.6 %collective-permute-start.3 = (bf16[288,384]{1,0:T(8,128)(2,1)S(1)}, bf16[288,384]{1,0:T(8,128)(2,1)S(1)}, u32[]{:S(2)}, u32[]{:S(2)}) collective-permute-start(bf16[288,384]{1,0:T(8,128)(2,1)S(1)} %constant_dynamic-update-slice_fusion.refs_0_), channel_id=1, source_target_pairs={{0,1},{1,0},{2,3},{3,2},{4,5},{5,4},{6,7},{7,6},{8,9},{9,8},{10,11... | collective-permute-start | bytes 663560 | tf_op jit(solution)/shard_map/ppermute | solution.py:451
  15.4 1.5 %collective-permute-start.4 = (bf16[288,384]{1,0:T(8,128)(2,1)S(1)}, bf16[288,384]{1,0:T(8,128)(2,1)S(1)}, u32[]{:S(2)}, u32[]{:S(2)}) collective-permute-start(bf16[288,384]{1,0:T(8,128)(2,1)S(1)} %constant_dynamic-update-slice_fusion.refs_0_), channel_id=1, source_target_pairs={{0,2},{1,3},{2,0},{3,1},{4,6},{5,7},{6,4},{7,5},{8,10},{9,11},{10,... | collective-permute-start | bytes 663560 | tf_op jit(solution)/shard_map/ppermute | solution.py:451
  16.9 0.5 collective-permute-start.5
  17.4 4.6 %collective-permute-done.3.refs_1_ = bf16[288,384]{1,0:T(8,128)(2,1)S(1)} collective-permute-done((bf16[288,384]{1,0:T(8,128)(2,1)S(1)}, bf16[288,384]{1,0:T(8,128)(2,1)S(1)}, u32[]{:S(2)}, u32[]{:S(2)}) %collective-permute-start.3) | collective-permute-done | bytes 221216 | tf_op jit(solution)/shard_map/ppermute | solution.py:451
  22.0 3.6 %collective-permute-done.4.refs_2_ = bf16[288,384]{1,0:T(8,128)(2,1)S(1)} collective-permute-done((bf16[288,384]{1,0:T(8,128)(2,1)S(1)}, bf16[288,384]{1,0:T(8,128)(2,1)S(1)}, u32[]{:S(2)}, u32[]{:S(2)}) %collective-permute-start.4) | collective-permute-done | bytes 221216 | tf_op jit(solution)/shard_map/ppermute | solution.py:451
  25.6 0.0 collective-permute-done.5.refs_3_
  25.6 0.7 copy-done.2
  26.3 0.1 copy-done.3
  26.4 10.6 %chains.1 = (f32[288,384]{1,0:T(8,128)}, bf16[288,384]{1,0:T(8,128)(2,1)}, bf16[288,384]{1,0:T(8,128)(2,1)}, bf16[288,384]{1,0:T(8,128)(2,1)}, f32[3,64,256]{2,1...) custom-call(bf16[288,384]{1,0:T(8,128)(2,1)} %copy-done, bf16[288,384]{1,0:T(8,128)(2,1)} %copy-done.1, ...), custom_call_target="tpu_custom_call" | custom-call | tf_op jit(solution)/shard_map/chains/pallas_call | solution.py:460
  37.0 1.1 %collective-permute-start.6 = (bf16[288,384]{1,0:T(8,128)(2,1)}, bf16[288,384]{1,0:T(8,128)(2,1)S(1)}, u32[]{:S(2)}, u32[]{:S(2)}) collective-permute-start(bf16[288,384]{1,0:T(8,128)(2,1)} %get-tuple-element.23), channel_id=1, source_target_pairs={{0,1},{1,0},{2,3},{3,2},{4,5},{5,4},{6,7},{7,6},{8,9},{9,8},{10,11... | collective-permute-start | bytes 663560 | tf_op jit(solution)/shard_map/ppermute | solution.py:494
  38.1 0.9 %collective-permute-start.7 = (bf16[288,384]{1,0:T(8,128)(2,1)}, bf16[288,384]{1,0:T(8,128)(2,1)S(1)}, u32[]{:S(2)}, u32[]{:S(2)}) collective-permute-start(bf16[288,384]{1,0:T(8,128)(2,1)} %get-tuple-element.24), channel_id=1, source_target_pairs={{0,2},{1,3},{2,0},{3,1},{4,6},{5,7},{6,4},{7,5},{8,10},{9,11},{10,... | collective-permute-start | bytes 663560 | tf_op jit(solution)/shard_map/ppermute | solution.py:494
  39.0 1.5 %collective-permute-start.8 = (bf16[288,384]{1,0:T(8,128)(2,1)}, bf16[288,384]{1,0:T(8,128)(2,1)S(1)}, u32[]{:S(2)}, u32[]{:S(2)}) collective-permute-start(bf16[288,384]{1,0:T(8,128)(2,1)} %get-tuple-element.25), channel_id=1, source_target_pairs={{0,3},{1,2},{2,1},{3,0},{4,7},{5,6},{6,5},{7,4},{8,11},{9,10},{10,... | collective-permute-start | bytes 663560 | tf_op jit(solution)/shard_map/ppermute | solution.py:494
  40.5 3.4 %collective-permute-done.6 = bf16[288,384]{1,0:T(8,128)(2,1)S(1)} collective-permute-done((bf16[288,384]{1,0:T(8,128)(2,1)}, bf16[288,384]{1,0:T(8,128)(2,1)S(1)}, u32[]{:S(2)}, u32[]{:S(2)}) %collective-permute-start.6) | collective-permute-done | bytes 221216 | tf_op jit(solution)/shard_map/ppermute | solution.py:494
  43.9 3.5 %collective-permute-done.7 = bf16[288,384]{1,0:T(8,128)(2,1)S(1)} collective-permute-done((bf16[288,384]{1,0:T(8,128)(2,1)}, bf16[288,384]{1,0:T(8,128)(2,1)S(1)}, u32[]{:S(2)}, u32[]{:S(2)}) %collective-permute-start.7) | collective-permute-done | bytes 221216 | tf_op jit(solution)/shard_map/ppermute | solution.py:494
  47.4 0.0 collective-permute-done.8
  47.4 1.1 %fusion = (bf16[288,384]{1,0:T(8,128)(2,1)S(1)}, f32[288,384]{1,0:T(8,128)S(1)}) fusion(bf16[288,384]{1,0:T(8,128)(2,1)S(1)} %collective-permute-done.8, bf16[288,384]{1,0:T(8,128)(2,1)S(1)} %collective-permute-done.7, f32[288,384]{1,0:T(8,128)} %get-tuple-element.22, bf16[288,384]{1,0:T(8,128)(2,1)S(1)} %collective-permute-done.6), kind=kLoop, calls=%fused_computation.6 | loop fusion | flops 774144 | bytes 1769472 | tf_op jit(solution)/shard_map/convert.2
  48.5 0.0 copy-start.12
  48.6 4.3 %collective-permute-start.10 = (bf16[72,384]{1,0:T(8,128)(2,1)S(1)}, bf16[72,384]{1,0:T(8,128)(2,1)S(1)}, u32[]{:S(2)}, u32[]{:S(2)}) collective-permute-start(bf16[72,384]{1,0:T(8,128)(2,1)S(1)} %get-tuple-element.36), channel_id=1, source_target_pairs={{0,8},{1,9},{2,10},{3,11},{4,12},{5,13},{6,14},{7,15},{8,0},{9,1},... | collective-permute-start | bytes 165896 | tf_op jit(solution)/shard_map/ppermute | solution.py:502
  52.9 0.1 collective-permute-start.11
  53.0 1.9 %collective-permute-start.9 = (bf16[72,384]{1,0:T(8,128)(2,1)S(1)}, bf16[72,384]{1,0:T(8,128)(2,1)S(1)}, u32[]{:S(2)}, u32[]{:S(2)}) collective-permute-start(bf16[72,384]{1,0:T(8,128)(2,1)S(1)} %get-tuple-element.37), channel_id=1, source_target_pairs={{0,4},{1,5},{2,6},{3,7},{4,8},{5,9},{6,10},{7,11},{8,12},{9,13},{1... | collective-permute-start | bytes 165896 | tf_op jit(solution)/shard_map/ppermute | solution.py:502
  54.9 0.0 collective-permute-start.15
  54.9 0.6 collective-permute-start.12
  55.6 0.5 collective-permute-done.15
  56.1 4.5 %collective-permute-start.13 = (f32[9,2,128]{2,1,0:T(2,128)S(1)}, f32[9,2,128]{2,1,0:T(2,128)S(1)}, u32[]{:S(2)}, u32[]{:S(2)}) collective-permute-start(f32[9,2,128]{2,1,0:T(2,128)S(1)} %copy-done.11), channel_id=1, source_target_pairs={{1,0},{2,1},{3,2},{4,3},{5,4},{6,5},{7,6},{8,7},{9,8},{10,9},{11,1... | collective-permute-start | bytes 27656 | tf_op jit(solution)/shard_map/ppermute | solution.py:455
  60.6 0.1 concatenate.28
  60.7 0.1 concatenate.29
  60.8 0.7 slice.19.refs_0_
  61.4 0.8 %collective-permute-done.12.refs_4_ = f32[9,2,128]{2,1,0:T(2,128)S(1)} collective-permute-done((f32[9,2,128]{2,1,0:T(2,128)S(1)}, f32[9,2,128]{2,1,0:T(2,128)S(1)}, u32[]{:S(2)}, u32[]{:S(2)}) %collective-permute-start.12) | collective-permute-done | bytes 9248 | tf_op jit(solution)/shard_map/ppermute | solution.py:454
  62.3 0.0 collective-permute-done.13.refs_5_
  62.3 0.0 collective-permute-done.10.refs_2_
  62.3 0.0 collective-permute-done.11.refs_3_
  62.3 0.5 copy-done.8
  62.9 0.0 copy-done.5
  62.9 0.0 copy-done.6
  62.9 0.6 copy-done.7
  63.5 2.5 %collide.1 = (f32[19,2,32,128]{3,2,1,0:T(8,128)}, f32[10,32,128]{2,1,0:T(8,128)}) custom-call(f32[19,2,32,128]{3,2,1,0:T(8,128)} %pop_ref.3, f32[72,384]{1,0:T(8,128)} %slice.19.refs_0_, bf16[72,384]{1,0:T(8,128)(2,1)} %copy-done.7, bf16[72,384]{1,0:T(8,128)(2,1)} %copy-done.5, bf16[72,384]{1,0:T(8,128)(2,1)} %copy-done.6, f32[9,2,128]{2,1,0:T(2,128)} %copy-done.8, ...), custom_call_target="tpu_custom_call" | custom-call | tf_op jit(solution)/shard_map/collide/pallas_call | solution.py:507
  66.1 0.6 maximum_select_fusion
  66.7 1.0 %collective-permute-done.14.came_ref = f32[10,32,128]{2,1,0:T(8,128)S(1)} collective-permute-done((f32[10,32,128]{2,1,0:T(8,128)}, f32[10,32,128]{2,1,0:T(8,128)S(1)}, u32[]{:S(2)}, u32[]{:S(2)}) %collective-permute-start.14) | collective-permute-done | bytes 163872 | tf_op jit(solution)/shard_map/ppermute | solution.py:517
  67.7 0.7 copy-done.4
  68.4 1.7 %merge.1 = f32[19,2,32,128]{3,2,1,0:T(8,128)} custom-call(f32[10,32,128]{2,1,0:T(8,128)} %copy-done.4, f32[19,2,32,128]{3,2,1,0:T(8,128)} %get-tuple-element.29.part_ref), custom_call_target="tpu_custom_call", output_to_operand_aliasing={{}: (1, {})} | custom-call | tf_op jit(solution)/shard_map/merge/pallas_call | solution.py:518
  (26 shorter events, 0.1 us)
Async XLA Ops:
  2.5 7.7 %collective-permute-start = (bf16[72,384]{1,0:T(8,128)(2,1)}, bf16[72,384]{1,0:T(8,128)(2,1)S(1)}, u32[]{:S(2)}, u32[]{:S(2)}) collective-permute-start(bf16[72,384]{1,0:T(8,128)(2,1)} %get-tuple-element.19), channel_id=1, source_target_pairs={{0,12},{1,13},{2,14},{3,15},{4,0},{5,1},{6,2},{7,3},{8,4},{9,5},{1... | collective-permute-start | bytes 165896 | tf_op jit(solution)/shard_map/ppermute | solution.py:448
  7.6 5.3 %collective-permute-start.1 = (bf16[72,384]{1,0:T(8,128)(2,1)}, bf16[72,384]{1,0:T(8,128)(2,1)S(1)}, u32[]{:S(2)}, u32[]{:S(2)}) collective-permute-start(bf16[72,384]{1,0:T(8,128)(2,1)} %get-tuple-element.20), channel_id=1, source_target_pairs={{0,8},{1,9},{2,10},{3,11},{4,12},{5,13},{6,14},{7,15},{8,0},{9,1},... | collective-permute-start | bytes 165896 | tf_op jit(solution)/shard_map/ppermute | solution.py:448
  7.6 6.2 %collective-permute-start.2 = (bf16[72,384]{1,0:T(8,128)(2,1)}, bf16[72,384]{1,0:T(8,128)(2,1)S(1)}, u32[]{:S(2)}, u32[]{:S(2)}) collective-permute-start(bf16[72,384]{1,0:T(8,128)(2,1)} %get-tuple-element.21), channel_id=1, source_target_pairs={{0,4},{1,5},{2,6},{3,7},{4,8},{5,9},{6,10},{7,11},{8,12},{9,13},{1... | collective-permute-start | bytes 165896 | tf_op jit(solution)/shard_map/ppermute | solution.py:448
  13.8 11.8 %copy-start = (bf16[288,384]{1,0:T(8,128)(2,1)}, bf16[288,384]{1,0:T(8,128)(2,1)S(1)}, u32[]{:S(2)}) copy-start(bf16[288,384]{1,0:T(8,128)(2,1)S(1)} %constant_dynamic-update-slice_fusion.refs_0_) | copy-start | bytes 663556
  13.8 8.2 %collective-permute-start.3 = (bf16[288,384]{1,0:T(8,128)(2,1)S(1)}, bf16[288,384]{1,0:T(8,128)(2,1)S(1)}, u32[]{:S(2)}, u32[]{:S(2)}) collective-permute-start(bf16[288,384]{1,0:T(8,128)(2,1)S(1)} %constant_dynamic-update-slice_fusion.refs_0_), channel_id=1, source_target_pairs={{0,1},{1,0},{2,3},{3,2},{4,5},{5,4},{6,7},{7,6},{8,9},{9,8},{10,11... | collective-permute-start | bytes 663560 | tf_op jit(solution)/shard_map/ppermute | solution.py:451
  15.4 10.2 %collective-permute-start.4 = (bf16[288,384]{1,0:T(8,128)(2,1)S(1)}, bf16[288,384]{1,0:T(8,128)(2,1)S(1)}, u32[]{:S(2)}, u32[]{:S(2)}) collective-permute-start(bf16[288,384]{1,0:T(8,128)(2,1)S(1)} %constant_dynamic-update-slice_fusion.refs_0_), channel_id=1, source_target_pairs={{0,2},{1,3},{2,0},{3,1},{4,6},{5,7},{6,4},{7,5},{8,10},{9,11},{10,... | collective-permute-start | bytes 663560 | tf_op jit(solution)/shard_map/ppermute | solution.py:451
  16.9 8.7 %collective-permute-start.5 = (bf16[288,384]{1,0:T(8,128)(2,1)S(1)}, bf16[288,384]{1,0:T(8,128)(2,1)S(1)}, u32[]{:S(2)}, u32[]{:S(2)}) collective-permute-start(bf16[288,384]{1,0:T(8,128)(2,1)S(1)} %constant_dynamic-update-slice_fusion.refs_0_), channel_id=1, source_target_pairs={{0,3},{1,2},{2,1},{3,0},{4,7},{5,6},{6,5},{7,4},{8,11},{9,10},{10,... | collective-permute-start | bytes 663560 | tf_op jit(solution)/shard_map/ppermute | solution.py:451
  22.0 3.6 %copy-start.1 = (bf16[288,384]{1,0:T(8,128)(2,1)}, bf16[288,384]{1,0:T(8,128)(2,1)S(1)}, u32[]{:S(2)}) copy-start(bf16[288,384]{1,0:T(8,128)(2,1)S(1)} %collective-permute-done.3.refs_1_) | copy-start | bytes 663556
  25.6 0.7 %copy-start.2 = (bf16[288,384]{1,0:T(8,128)(2,1)}, bf16[288,384]{1,0:T(8,128)(2,1)S(1)}, u32[]{:S(2)}) copy-start(bf16[288,384]{1,0:T(8,128)(2,1)S(1)} %collective-permute-done.4.refs_2_) | copy-start | bytes 663556
  25.6 0.8 %copy-start.3 = (bf16[288,384]{1,0:T(8,128)(2,1)}, bf16[288,384]{1,0:T(8,128)(2,1)S(1)}, u32[]{:S(2)}) copy-start(bf16[288,384]{1,0:T(8,128)(2,1)S(1)} %collective-permute-done.5.refs_3_) | copy-start | bytes 663556
  37.0 6.9 %collective-permute-start.6 = (bf16[288,384]{1,0:T(8,128)(2,1)}, bf16[288,384]{1,0:T(8,128)(2,1)S(1)}, u32[]{:S(2)}, u32[]{:S(2)}) collective-permute-start(bf16[288,384]{1,0:T(8,128)(2,1)} %get-tuple-element.23), channel_id=1, source_target_pairs={{0,1},{1,0},{2,3},{3,2},{4,5},{5,4},{6,7},{7,6},{8,9},{9,8},{10,11... | collective-permute-start | bytes 663560 | tf_op jit(solution)/shard_map/ppermute | solution.py:494
  38.1 9.3 %collective-permute-start.7 = (bf16[288,384]{1,0:T(8,128)(2,1)}, bf16[288,384]{1,0:T(8,128)(2,1)S(1)}, u32[]{:S(2)}, u32[]{:S(2)}) collective-permute-start(bf16[288,384]{1,0:T(8,128)(2,1)} %get-tuple-element.24), channel_id=1, source_target_pairs={{0,2},{1,3},{2,0},{3,1},{4,6},{5,7},{6,4},{7,5},{8,10},{9,11},{10,... | collective-permute-start | bytes 663560 | tf_op jit(solution)/shard_map/ppermute | solution.py:494
  39.0 8.4 %collective-permute-start.8 = (bf16[288,384]{1,0:T(8,128)(2,1)}, bf16[288,384]{1,0:T(8,128)(2,1)S(1)}, u32[]{:S(2)}, u32[]{:S(2)}) collective-permute-start(bf16[288,384]{1,0:T(8,128)(2,1)} %get-tuple-element.25), channel_id=1, source_target_pairs={{0,3},{1,2},{2,1},{3,0},{4,7},{5,6},{6,5},{7,4},{8,11},{9,10},{10,... | collective-permute-start | bytes 663560 | tf_op jit(solution)/shard_map/ppermute | solution.py:494
  48.5 6.4 %copy-start.13 = (f32[8,192]{1,0:T(8,128)S(1)}, f32[8,192]{1,0:T(8,128)}, u32[]{:S(2)}) copy-start(f32[8,192]{1,0:T(8,128)} %get-tuple-element.32) | copy-start | bytes 18436
  48.5 6.4 %copy-start.12 = (f32[9,2,128]{2,1,0:T(2,128)S(1)}, f32[9,2,128]{2,1,0:T(2,128)}, u32[]{:S(2)}) copy-start(f32[9,2,128]{2,1,0:T(2,128)} %get-tuple-element.26) | copy-start | bytes 27652
  48.6 7.5 %copy-start.11 = (f32[9,2,128]{2,1,0:T(2,128)S(1)}, f32[9,2,128]{2,1,0:T(2,128)}, u32[]{:S(2)}) copy-start(f32[9,2,128]{2,1,0:T(2,128)} %get-tuple-element.27) | copy-start | bytes 27652
  48.6 13.7 %collective-permute-start.10 = (bf16[72,384]{1,0:T(8,128)(2,1)S(1)}, bf16[72,384]{1,0:T(8,128)(2,1)S(1)}, u32[]{:S(2)}, u32[]{:S(2)}) collective-permute-start(bf16[72,384]{1,0:T(8,128)(2,1)S(1)} %get-tuple-element.36), channel_id=1, source_target_pairs={{0,8},{1,9},{2,10},{3,11},{4,12},{5,13},{6,14},{7,15},{8,0},{9,1},... | collective-permute-start | bytes 165896 | tf_op jit(solution)/shard_map/ppermute | solution.py:502
  52.9 9.4 %collective-permute-start.11 = (bf16[72,384]{1,0:T(8,128)(2,1)S(1)}, bf16[72,384]{1,0:T(8,128)(2,1)S(1)}, u32[]{:S(2)}, u32[]{:S(2)}) collective-permute-start(bf16[72,384]{1,0:T(8,128)(2,1)S(1)} %get-tuple-element.35), channel_id=1, source_target_pairs={{0,12},{1,13},{2,14},{3,15},{4,0},{5,1},{6,2},{7,3},{8,4},{9,5},{1... | collective-permute-start | bytes 165896 | tf_op jit(solution)/shard_map/ppermute | solution.py:502
  53.0 9.3 %collective-permute-start.9 = (bf16[72,384]{1,0:T(8,128)(2,1)S(1)}, bf16[72,384]{1,0:T(8,128)(2,1)S(1)}, u32[]{:S(2)}, u32[]{:S(2)}) collective-permute-start(bf16[72,384]{1,0:T(8,128)(2,1)S(1)} %get-tuple-element.37), channel_id=1, source_target_pairs={{0,4},{1,5},{2,6},{3,7},{4,8},{5,9},{6,10},{7,11},{8,12},{9,13},{1... | collective-permute-start | bytes 165896 | tf_op jit(solution)/shard_map/ppermute | solution.py:502
  54.9 5.7 %copy-start.10 = (f32[8,192]{1,0:T(8,128)S(1)}, f32[8,192]{1,0:T(8,128)}, u32[]{:S(2)}) copy-start(f32[8,192]{1,0:T(8,128)} %get-tuple-element.31) | copy-start | bytes 18436
  54.9 1.2 %collective-permute-start.15 = (f32[8,192]{1,0:T(8,128)S(1)}, f32[8,192]{1,0:T(8,128)S(1)}, u32[]{:S(2)}, u32[]{:S(2)}) collective-permute-start(f32[8,192]{1,0:T(8,128)S(1)} %copy-done.13), channel_id=1, source_target_pairs={{0,16},{16,0},{1,17},{17,1},{2,18},{18,2},{3,19},{19,3},{4,20},{20... | collective-permute-start | bytes 18440 | tf_op jit(solution)/shard_map/ppermute | solution.py:498
  54.9 7.3 %collective-permute-start.12 = (f32[9,2,128]{2,1,0:T(2,128)S(1)}, f32[9,2,128]{2,1,0:T(2,128)S(1)}, u32[]{:S(2)}, u32[]{:S(2)}) collective-permute-start(f32[9,2,128]{2,1,0:T(2,128)S(1)} %copy-done.12), channel_id=1, source_target_pairs={{0,1},{1,2},{2,3},{3,4},{4,5},{5,6},{6,7},{7,8},{8,9},{9,10},{10,1... | collective-permute-start | bytes 27656 | tf_op jit(solution)/shard_map/ppermute | solution.py:454
  56.1 6.1 %collective-permute-start.13 = (f32[9,2,128]{2,1,0:T(2,128)S(1)}, f32[9,2,128]{2,1,0:T(2,128)S(1)}, u32[]{:S(2)}, u32[]{:S(2)}) collective-permute-start(f32[9,2,128]{2,1,0:T(2,128)S(1)} %copy-done.11), channel_id=1, source_target_pairs={{1,0},{2,1},{3,2},{4,3},{5,4},{6,5},{7,6},{8,7},{9,8},{10,9},{11,1... | collective-permute-start | bytes 27656 | tf_op jit(solution)/shard_map/ppermute | solution.py:455
  62.3 0.6 copy-start.8
  62.3 0.6 copy-start.9
  62.3 0.6 copy-start.5
  62.3 0.6 copy-start.6
  62.9 0.6 copy-start.7
  66.1 1.6 %collective-permute-start.14 = (f32[10,32,128]{2,1,0:T(8,128)}, f32[10,32,128]{2,1,0:T(8,128)S(1)}, u32[]{:S(2)}, u32[]{:S(2)}) collective-permute-start(f32[10,32,128]{2,1,0:T(8,128)} %get-tuple-element.28), channel_id=1, source_target_pairs={{0,16},{16,0},{1,17},{17,1},{2,18},{18,2},{3,19},{19,3},{4,20},{20... | collective-permute-start | bytes 491528 | tf_op jit(solution)/shard_map/ppermute | solution.py:517
  67.7 0.7 copy-start.4

commit v2 on v1

--- a/solution.py
+++ b/solution.py
@@ -49,6 +49,7 @@
 VMEM = pl.BlockSpec(memory_space=pltpu.VMEM)
 SMEM = pl.BlockSpec(memory_space=pltpu.SMEM)
 ANY = pl.BlockSpec(memory_space=pl.ANY)
+HBM = pl.BlockSpec(memory_space=pltpu.HBM)
 
 
 class Plan:
@@ -59,9 +60,10 @@
         self.rows = rows
         self.size_y = size_y
         self.size_x = rows // size_y
-        extra = max(self.inner, 2 * self.size_x)
-        self.stride = (rows + extra + 7) // 8 * 8
-        self.block = self.outer * self.stride
+        self.extra = max(self.inner, 2 * self.size_x)
+        self.stride = (rows + self.extra + 7) // 8 * 8
+        self.main = self.outer * rows
+        self.block = (self.main + self.outer * self.extra + 15) // 16 * 16
 
     def outer_shift(self, k):
         z_count, w_count = self.outer, self.inner
@@ -105,14 +107,30 @@
     return (density, momentum)
 
 
-def moment_kernel(plan, pop_ref, rows_ref, count_ref, *outs):
+def moment_kernel(plan, pop_hbm, rows_hbm, count_hbm, slots_hbm, *outs):
     msg_refs = outs[: plan.outer]
-    up_ref, down_ref = outs[plan.outer :]
+    up_ref, down_ref, state_ref, slots_ref, pop_ref, rows_ref, count_ref, sem = outs[
+        plan.outer :
+    ]
     length = pop_ref.shape[3]
-    size_y = plan.size_y
-    for x in range(plan.size_x):
+    size_x, size_y = plan.size_x, plan.size_y
+    loads = [
+        pltpu.make_async_copy(pop_hbm.at[:, x], pop_ref.at[:, x], sem.at[x])
+        for x in range(size_x)
+    ]
+    others = [
+        pltpu.make_async_copy(rows_hbm, rows_ref, sem.at[size_x]),
+        pltpu.make_async_copy(count_hbm, count_ref, sem.at[size_x + 1]),
+        pltpu.make_async_copy(slots_hbm, slots_ref, sem.at[size_x + 2]),
+    ]
+    for copy in loads + others:
+        copy.start()
+    for x in range(size_x):
+        loads[x].wait()
         density, momentum = weighted_sums(lambda i: pop_ref[i, x])
         first = slice(x * size_y, (x + 1) * size_y)
+        for slot, value in enumerate([density] + momentum):
+            state_ref[slot, first, :] = value
         for k in range(3):
             velocity = (momentum[k] / density).astype(bf16)
             for msg in msg_refs:
@@ -123,6 +141,8 @@
             at = len(moves)
             for slot, value in enumerate([density] + momentum):
                 out[at + slot, x : x + 1, :] = value[row : row + 1]
+    for copy in others:
+        copy.wait()
     me = lax.axis_index("chain")
     z = me // plan.inner
     w = me % plan.inner
@@ -141,14 +161,27 @@
         msg[plan.rows :, length:] = jnp.zeros((extra, 2 * length), bf16)
 
 
+def pack_kernel(plan, *refs):
+    part_refs, out_ref = refs[:-1], refs[-1]
+    rows, extra = plan.rows, plan.extra
+    tails = []
+    for k, part in enumerate(part_refs):
+        out_ref[k * rows : (k + 1) * rows, :] = part[:rows, :]
+        tails.append(part[rows:, :].astype(f32)[:extra])
+    spare = plan.block - plan.main - plan.outer * extra
+    if spare:
+        tails.append(jnp.zeros((spare, out_ref.shape[1]), f32))
+    out_ref[plan.main :, :] = jnp.concatenate(tails, axis=0).astype(bf16)
+
+
 def chain_kernel(plan, capacity, *refs):
     block_refs = refs[: plan.inner]
     (
         pos_ref,
         site_ref,
         slot_ref,
-        list_ref,
-        live_ref,
+        list_hbm,
+        live_hbm,
         basis_ref,
         spectrum_ref,
         own_ref,
@@ -164,31 +197,38 @@
         smooth,
         velocity,
         force,
-        spread_hi,
-        spread_lo,
+        spread,
         sums,
+        list_ref,
+        live_ref,
+        sem,
     ) = refs[2 * plan.inner + 7 :]
-    inner, outer, rows, stride = plan.inner, plan.outer, plan.rows, plan.stride
-    groups = plan.groups
-    total = inner * plan.block
+    inner, outer, rows, extra = plan.inner, plan.outer, plan.rows, plan.extra
+    main, block, groups = plan.main, plan.block, plan.groups
     length = table.shape[1] // 3
     slots, chains = slot_ref.shape
     beads = pos_ref.shape[1]
     per_slot = beads // slots
-    extra = stride - rows
     me = lax.axis_index("chain")
     z = me // inner
     w = me % inner
 
+    loads = [
+        pltpu.make_async_copy(list_hbm, list_ref, sem.at[0]),
+        pltpu.make_async_copy(live_hbm, live_ref, sem.at[1]),
+    ]
+    for copy in loads:
+        copy.start()
+
     table_rows = []
     for m in range(inner):
+        table[m * block : m * block + main, :] = block_refs[m][:main, :]
+        table[m * block + main : (m + 1) * block, :] = jnp.zeros(
+            (block - main, 3 * length), bf16
+        )
+        names = block_refs[m][main:, :length].astype(f32)
         for k in range(outer):
-            base = k * stride
-            to = (m * outer + k) * stride
-            table[to : to + rows, :] = block_refs[m][base : base + rows, :]
-            table[to + rows : to + stride, :] = jnp.zeros((extra, 3 * length), bf16)
-            names = block_refs[m][base + rows : base + stride, :length].astype(f32)
-            table_rows.append(names[m : m + 1])
+            table_rows.append(names[k * extra + m : k * extra + m + 1])
     names = jnp.concatenate(table_rows, axis=0).astype(bf16)
 
     eye = (
@@ -204,36 +244,40 @@
 
     site_iota = lax.broadcasted_iota(jnp.int32, (length, chains), 0)
     group_iota = lax.broadcasted_iota(jnp.int32, (groups, chains), 0)
-    row_iota = lax.broadcasted_iota(jnp.int32, (rows, chains), 0)
-    extra_iota = lax.broadcasted_iota(jnp.int32, (extra, chains), 0)
-
-    def group_of(p):
-        return ((p % inner) ^ w) * outer + (p // inner - z + outer) % outer
+    main_iota = lax.broadcasted_iota(jnp.int32, (main, chains), 0)
+    extra_iota = lax.broadcasted_iota(jnp.int32, (block - main, chains), 0)
+
+    def place_of(p):
+        return ((p % inner) ^ w, (p // inner - z + outer) % outer)
 
     for r in range(slots):
         slot = slot_ref[r : r + 1, :]
         p = slot // capacity
         s = slot % capacity
-        group = group_of(p)
+        m, k = place_of(p)
         pick = jnp.where(site_iota == s, 1.0, 0.0).astype(bf16)
         looked = jnp.dot(names, pick, preferred_element_type=f32)
-        row = jnp.sum(jnp.where(group_iota == group, looked, 0.0), axis=0, keepdims=True)
+        row = jnp.sum(
+            jnp.where(group_iota == m * outer + k, looked, 0.0), axis=0, keepdims=True
+        )
         row = row.astype(jnp.int32)
         live = row >= 0
         y = row % plan.size_y
         x = row // plan.size_y
-        first = jnp.where(live, group * stride + row, -1)
-        above = group_of((p + 1) % groups) * stride + x
-        below = group_of((p + groups - 1) % groups) * stride + plan.size_x + x
-        second = jnp.where(y == plan.size_y - 1, above, jnp.where(y == 0, below, -stride))
-        second = jnp.where(live, second, -stride)
+        first = jnp.where(live, m * block + k * rows + row, -1)
+        m, k = place_of((p + 1) % groups)
+        above = m * block + k * extra + x
+        m, k = place_of((p + groups - 1) % groups)
+        below = m * block + k * extra + plan.size_x + x
+        second = jnp.where(y == plan.size_y - 1, above, jnp.where(y == 0, below, -1))
+        second = jnp.where(live, second, -1)
         lanes = slice(r * chains, (r + 1) * chains)
-        for g in range(groups):
-            base = g * stride
-            onehot[base : base + rows, lanes] = jnp.where(
-                row_iota == first - base, 1.0, 0.0
+        for m in range(inner):
+            base = m * block
+            onehot[base : base + main, lanes] = jnp.where(
+                main_iota == first - base, 1.0, 0.0
             ).astype(bf16)
-            onehot[base + rows : base + stride, lanes] = jnp.where(
+            onehot[base + main : base + block, lanes] = jnp.where(
                 extra_iota == second - base, 1.0, 0.0
             ).astype(bf16)
 
@@ -288,6 +332,8 @@
         moved_ref[k] = moved
         force[k] = (moved - pos_ref[k]) - velocity[k]
 
+    for copy in loads:
+        copy.wait()
     brick = lax.axis_index("brick")
     chain_iota = lax.broadcasted_iota(jnp.int32, (1, chains), 1)
     leaving = list_ref.shape[1]
@@ -318,16 +364,32 @@
                         parts[k] = parts[k] + jnp.where(here, force[k, at, lanes], 0.0)
                 for k in range(3):
                     out = slice(k * length + start, k * length + start + step)
-                    hi = parts[k].astype(bf16)
-                    spread_hi[out, wide] = hi
-                    spread_lo[out, wide] = (parts[k] - hi.astype(f32)).astype(bf16)
-
-    sums[...] = lax.dot_general(
-        onehot[...], spread_hi[...], NT, preferred_element_type=f32
-    ) + lax.dot_general(onehot[...], spread_lo[...], NT, preferred_element_type=f32)
-    own_ref[...] = sums[: plan.block, :]
+                    spread[out, wide] = parts[k].astype(bf16)
+
+    sums[...] = lax.dot_general(onehot[...], spread[...], NT, preferred_element_type=f32)
+    own_ref[...] = sums[:block, :]
     for m in range(1, inner):
-        send_refs[m - 1][...] = sums[m * plan.block : (m + 1) * plan.block, :].astype(bf16)
+        send_refs[m - 1][...] = sums[m * block : (m + 1) * block, :].astype(bf16)
+
+
+def sum_kernel(plan, own_ref, *refs):
+    came_refs = refs[: plan.inner - 1]
+    kept_ref, *send_refs = refs[plan.inner - 1 :]
+    rows, extra, main = plan.rows, plan.extra, plan.main
+    spare = plan.stride - rows - extra
+    tails = own_ref[main:, :]
+    for came in came_refs:
+        tails = tails + came[main:, :].astype(f32)
+    for k, out in enumerate([kept_ref] + send_refs):
+        part = slice(k * rows, (k + 1) * rows)
+        value = own_ref[part, :]
+        for came in came_refs:
+            value = value + came[part, :].astype(f32)
+        out[:rows, :] = value.astype(out.dtype)
+        tail = tails[k * extra : (k + 1) * extra]
+        if spare:
+            tail = jnp.concatenate([tail, jnp.zeros((spare, tail.shape[1]), f32)], axis=0)
+        out[rows:, :] = tail.astype(out.dtype)
 
 
 def equilibrium(i, density, velocity, square):
@@ -343,10 +405,27 @@
     return density * (1.0 + 3.0 * projected + 4.5 * projected * projected - 1.5 * square)
 
 
-def collide_kernel(plan, pop_ref, *refs):
+def relax(i, value, state):
+    return value - (value - equilibrium(i, *state)) / TAU_RELAX
+
+
+def shifted(i, value, edge):
+    _, shift_y, shift_z = VECTORS[i]
+    size_y, length = value.shape
+    if shift_y != 0:
+        y_iota = lax.broadcasted_iota(jnp.int32, value.shape, 0)
+        value = pltpu.roll(value, shift_y % size_y, axis=0)
+        edge = jnp.broadcast_to(edge, value.shape)
+        value = jnp.where(y_iota == (0 if shift_y > 0 else size_y - 1), edge, value)
+    if shift_z != 0:
+        value = pltpu.roll(value, shift_z % length, axis=1)
+    return value
+
+
+def cross_kernel(plan, pop_ref, sites_ref, *refs):
     kept_ref = refs[0]
     came_refs = refs[1 : plan.outer]
-    low_ref, high_ref, read_ref, send_ref = refs[plan.outer :]
+    low_ref, high_ref, send_ref, state_ref, edge_ref = refs[plan.outer :]
     length = pop_ref.shape[3]
     size_x, size_y, rows = plan.size_x, plan.size_y, plan.rows
     total = kept_ref[...]
@@ -363,9 +442,6 @@
         square = velocity[0] * velocity[0] + velocity[1] * velocity[1] + velocity[2] * velocity[2]
         return (density, velocity, square)
 
-    def relax(i, value, state):
-        return value - (value - equilibrium(i, *state)) / TAU_RELAX
-
     edges = {}
     for side, (ref, moves) in enumerate(((low_ref, MOVES_UP), (high_ref, MOVES_DOWN))):
         at = len(moves)
@@ -377,27 +453,38 @@
         )
         for slot, i in enumerate(moves):
             edges[i] = relax(i, ref[slot], state)
-
-    y_iota = lax.broadcasted_iota(jnp.int32, (size_y, length), 0)
+            edge_ref[i] = edges[i]
+
     for x in range(size_x):
-        density, momentum = weighted_sums(lambda i: pop_ref[i, x])
+        part = slice(x * size_y, (x + 1) * size_y)
         state = flow(
-            density, momentum, [force[k][x * size_y : (x + 1) * size_y] for k in range(3)]
+            sites_ref[0, part, :],
+            [sites_ref[k + 1, part, :] for k in range(3)],
+            [force[k][part] for k in range(3)],
+        )
+        density, velocity, square = state
+        for slot, value in enumerate([density] + velocity + [square]):
+            state_ref[slot, part, :] = value
+        for slot, i in enumerate(CROSSING):
+            if not 0 <= x + VECTORS[i][0] < size_x:
+                edge = edges[i][x : x + 1] if i in edges else None
+                send_ref[slot] = shifted(i, relax(i, pop_ref[i, x], state), edge)
+
+
+def collide_kernel(plan, pop_ref, state_ref, edge_ref, read_ref):
+    size_x, size_y = plan.size_x, plan.size_y
+    for x in range(size_x):
+        part = slice(x * size_y, (x + 1) * size_y)
+        state = (
+            state_ref[0, part, :],
+            [state_ref[k + 1, part, :] for k in range(3)],
+            state_ref[4, part, :],
         )
         for i in range(DIRECTIONS):
-            shift_x, shift_y, shift_z = VECTORS[i]
-            value = relax(i, pop_ref[i, x], state)
-            if shift_y != 0:
-                value = pltpu.roll(value, shift_y % size_y, axis=0)
-                edge = jnp.broadcast_to(edges[i][x : x + 1], (size_y, length))
-                value = jnp.where(y_iota == (0 if shift_y > 0 else size_y - 1), edge, value)
-            if shift_z != 0:
-                value = pltpu.roll(value, shift_z % length, axis=1)
-            target = x + shift_x
+            target = x + VECTORS[i][0]
             if 0 <= target < size_x:
-                read_ref[i, target] = value
-            else:
-                send_ref[CROSSING.index(i)] = value
+                edge = edge_ref[i, x : x + 1, :]
+                read_ref[i, target] = shifted(i, relax(i, pop_ref[i, x], state), edge)
 
 
 def merge_kernel(plan, came_ref, part_ref, read_ref, sem):
@@ -436,23 +523,42 @@
     width = 3 * length
     edge = shape((len(MOVES_UP) + 4, size_x, length), f32)
 
+    params = pltpu.CompilerParams
     first = pl.pallas_call(
         functools.partial(moment_kernel, plan),
-        out_shape=[shape((plan.stride, width), bf16)] * outer + [edge, edge],
-        in_specs=[VMEM, VMEM, SMEM],
-        out_specs=[VMEM] * (outer + 2),
+        out_shape=[shape((plan.stride, width), bf16)] * outer
+        + [edge, edge, shape((4, plan.rows, length), f32), shape((slots, chains), jnp.int32)],
+        in_specs=[HBM] * 4,
+        out_specs=[VMEM] * (outer + 4),
+        scratch_shapes=[
+            pltpu.VMEM(populations.shape, f32),
+            pltpu.VMEM((groups, capacity), jnp.int32),
+            pltpu.SMEM((groups,), jnp.int32),
+            pltpu.SemaphoreType.DMA((size_x + 3,)),
+        ],
+        compiler_params=params(vmem_limit_bytes=6 << 20),
         name="moments",
-    )(populations, send_rows[0, 0], send_count[0, 0])
-    msgs, (edge_up, edge_down) = first[:outer], first[outer:]
-    parts = [msgs[0]] + [
-        lax.ppermute(msgs[k], "chain", plan.outer_shift(-k)) for k in range(1, outer)
-    ]
-    near = jnp.concatenate(parts, axis=0)
-    blocks = [near] + [lax.ppermute(near, "chain", plan.inner_swap(m)) for m in range(1, inner)]
+    )(populations, send_rows[0, 0], send_count[0, 0], chain_slots[0, 0])
+    msgs, (edge_up, edge_down, sites, slot_list) = first[:outer], first[outer:]
+    parts = [msgs[0]]
+    for k in range(1, outer):
+        parts.append(lax.ppermute(msgs[k], "chain", plan.outer_shift(-k)))
+    near = pl.pallas_call(
+        functools.partial(pack_kernel, plan),
+        out_shape=shape((plan.block, width), bf16),
+        in_specs=[VMEM] * outer,
+        out_specs=VMEM,
+        compiler_params=params(vmem_limit_bytes=4 << 20),
+        name="pack",
+    )(*parts)
+    blocks = [near]
+    for m in range(1, inner):
+        blocks.append(lax.ppermute(blocks[0], "chain", plan.inner_swap(m)))
     up = [(i, (i + 1) % groups) for i in range(groups)]
     down = [(j, i) for i, j in up]
     low = lax.ppermute(edge_up, "chain", up)
     high = lax.ppermute(edge_down, "chain", down)
+    blocks, low, high = lax.optimization_barrier((blocks, low, high))
 
     basis, spectrum = rouse_tables(beads)
     total = inner * plan.block
@@ -463,7 +569,7 @@
         + [shape((plan.block, width), bf16)] * (inner - 1)
         + [shape((3, beads, chains), f32)]
         + [shape((leaving, 3 * beads), f32)] * 2,
-        in_specs=[VMEM] * (inner + 3) + [SMEM, SMEM] + [VMEM, VMEM],
+        in_specs=[VMEM] * (inner + 3) + [HBM, HBM] + [VMEM, VMEM],
         out_specs=[VMEM] * (inner + 3),
         scratch_shapes=[
             pltpu.VMEM((total, width), bf16),
@@ -473,15 +579,18 @@
             pltpu.VMEM((3, beads, chains), f32),
             pltpu.VMEM((3, beads, chains), f32),
             pltpu.VMEM((width, slots * chains), bf16),
-            pltpu.VMEM((width, slots * chains), bf16),
             pltpu.VMEM((total, width), f32),
+            pltpu.SMEM((bricks, leaving), jnp.int32),
+            pltpu.SMEM((bricks,), jnp.int32),
+            pltpu.SemaphoreType.DMA((2,)),
         ],
+        compiler_params=params(vmem_limit_bytes=(12 << 20) + total * 8192),
         name="chains",
     )(
         *blocks,
         positions[0, 0],
         bead_site[0, 0],
-        chain_slots[0, 0],
+        slot_list,
         migrate_list[0, 0],
         migrate_count[0, 0],
         basis,
@@ -489,32 +598,45 @@
     )
     own, sends = second[0], second[1:inner]
     moved, stay, leave = second[inner:]
-    total_force = own
+    came = []
     for m in range(1, inner):
-        total_force = total_force + lax.ppermute(sends[m - 1], "chain", plan.inner_swap(m)).astype(
-            f32
-        )
+        came.append(lax.ppermute(sends[m - 1], "chain", plan.inner_swap(m)))
     swap = [(i, (i + 1) % bricks) for i in range(bricks)]
     arrived = lax.ppermute(leave, "brick", swap)
-    stride = plan.stride
-    kept = total_force[:stride]
-    came = [
-        lax.ppermute(
-            total_force[k * stride : (k + 1) * stride].astype(bf16), "chain", plan.outer_shift(k)
-        )
-        for k in range(1, outer)
-    ]
-    partial, crossing = pl.pallas_call(
+    came, arrived = lax.optimization_barrier((came, arrived))
+    kept, *outgoing = pl.pallas_call(
+        functools.partial(sum_kernel, plan),
+        out_shape=[shape((plan.stride, width), f32)]
+        + [shape((plan.stride, width), bf16)] * (outer - 1),
+        in_specs=[VMEM] * inner,
+        out_specs=[VMEM] * outer,
+        compiler_params=params(vmem_limit_bytes=8 << 20),
+        name="sums",
+    )(own, *came)
+    came = []
+    for k in range(1, outer):
+        came.append(lax.ppermute(outgoing[k - 1], "chain", plan.outer_shift(k)))
+    crossing, state, edges = pl.pallas_call(
+        functools.partial(cross_kernel, plan),
+        out_shape=[
+            shape((len(CROSSING), size_y, length), f32),
+            shape((5, plan.rows, length), f32),
+            shape((DIRECTIONS, size_x, length), f32),
+        ],
+        in_specs=[VMEM] * (outer + 4),
+        out_specs=[VMEM] * 3,
+        compiler_params=params(vmem_limit_bytes=6 << 20),
+        name="cross",
+    )(populations, sites, kept, *came, low, high)
+    crossed = lax.ppermute(crossing, "brick", swap)
+    partial = pl.pallas_call(
         functools.partial(collide_kernel, plan),
-        out_shape=[
-            shape(populations.shape, f32),
-            shape((len(CROSSING), size_y, length), f32),
-        ],
-        in_specs=[VMEM] * (outer + 3),
-        out_specs=[VMEM, VMEM],
+        out_shape=shape(populations.shape, f32),
+        in_specs=[VMEM] * 3,
+        out_specs=VMEM,
+        compiler_params=params(vmem_limit_bytes=6 << 20),
         name="collide",
-    )(populations, kept, *came, low, high)
-    crossed = lax.ppermute(crossing, "brick", swap)
+    )(populations, state, edges)
     read = pl.pallas_call(
         functools.partial(merge_kernel, plan),
         out_shape=shape(populations.shape, f32),
@@ -522,6 +644,7 @@
         out_specs=ANY,
         scratch_shapes=[pltpu.SemaphoreType.DMA((len(CROSSING),))],
         input_output_aliases={1: 0},
+        compiler_params=params(vmem_limit_bytes=4 << 20),
         name="merge",
     )(crossed, partial)
     here = lax.axis_index("brick")
@@ -546,6 +669,7 @@
         P("brick", "chain", None, None),
         P("brick", "chain", None),
     )
+
     return jax.shard_map(
         local,
         mesh=mesh,

time: 70.3 us -> 56.4 us (0.80)
  Pallas kernels: 16.7 us -> 9.94 us
  waiting for transfers between devices: 21.8 us -> 15.3 us
  starting transfers between devices: 24.6 us -> 26.2 us
  other arithmetic: 1.75 us -> 0.63 us
  local copies, waits for them, and re-layouts: 4.36 us -> 3.27 us
    ppermute x12, waiting for transfers between devices: 19.5 us -> 12.4 us  [the longest x3 5.14 us: local(): came.append(lax.ppermute(sends[m - 1], 'chain', plan.inner_swap(m)))]
    pallas_call x1, Pallas kernels: 10.6 us -> 7.03 us  [local(): pl.pallas_call(functools.partial(chain_kernel, plan, capacity), out_shape...]
    pallas_call x1, Pallas kernels: 1.9 us -> 0.68 us  [local(): pl.pallas_call(functools.partial(moment_kernel, plan), out_shape=[shape((...]
    another operation x1 -> x0, other arithmetic: 1.13 us -> none
    pallas_call x1 -> x4, Pallas kernels: 2.54 us -> 1.5 us  [the longest x1 1.08 us: local(): pl.pallas_call(functools.partial(collide_kernel, plan), out_shape=shape(p...]
    ppermute x12, starting transfers between devices: 19.5 us -> 20.5 us  [the longest x3 7.24 us: local(): came.append(lax.ppermute(outgoing[k - 1], 'chain', plan.outer_shift(k)))]
    ppermute x1, waiting for transfers between devices: 0.98 us -> 0.01 us  [local(): crossed = lax.ppermute(crossing, 'brick', swap)]
    ppermute x1, waiting for transfers between devices: 0.81 us -> 1.74 us  [local(): low = lax.ppermute(edge_up, 'chain', up)]
  transfers between devices with their start and end apart: 16 -> 16, of which waited for: 10 -> 9; matrix products, arithmetic and copies ran while one was open for 3% -> 1% of each run, Pallas kernels for 0% -> 2%
where the time goes in v2:
time: 56.4 us; the launch traced here: 56.1 us
  starting transfers between devices  26.2 us (46%)
  waiting for transfers between devices  15.3 us (27%)
  Pallas kernels  9.94 us (18%)
  local copies, waits for them, and re-layouts  3.27 us (6%)
  between operations  0.75 us (1%)
  other arithmetic  0.63 us (1%)
    ppermute x3, starting transfers between devices, local(): came.append(lax.ppermute(outgoing[k - 1], 'chain', plan.outer_shift(k)))  7.24 us
    pallas_call x1, Pallas kernels, local(): pl.pallas_call(functools.partial(chain_kernel, plan, capacity), out_shape...  7.03 us
    ppermute x3, starting transfers between devices, local(): parts.append(lax.ppermute(msgs[k], 'chain', plan.outer_shift(-k)))  6.14 us
    ppermute x3, waiting for transfers between devices, local(): came.append(lax.ppermute(sends[m - 1], 'chain', plan.inner_swap(m)))  5.14 us
    ppermute x3, waiting for transfers between devices, local(): parts.append(lax.ppermute(msgs[k], 'chain', plan.outer_shift(-k)))  4.94 us
    ppermute x1, starting transfers between devices, local(): high = lax.ppermute(edge_down, 'chain', down)  4.13 us
    ppermute x3, starting transfers between devices, local(): blocks.append(lax.ppermute(blocks[0], 'chain', plan.inner_swap(m)))  3.55 us
    ppermute x3, starting transfers between devices, local(): came.append(lax.ppermute(sends[m - 1], 'chain', plan.inner_swap(m)))  3.55 us
  transfers between devices with their start and end apart: 16, of which 9 were waited for; matrix products, arithmetic and copies ran while one was open for 1% of the time, Pallas kernels for 2%

profile of v2, /device:TPU:0, one launch (start us, length us, event | category | flops | bytes accessed | tf_op | source)
XLA Modules:
  0.0 56.1 jit_solution(15459609186417832203)
XLA Ops:
  0.6 0.0 copy-start.7
  0.6 0.0 copy-start.10
  0.7 0.7 %copy-done.7 = s32[1,1,4,256]{3,2,1,0:T(4,128)S(1)} copy-done((s32[1,1,4,256]{3,2,1,0:T(4,128)S(1)}, s32[1,1,4,256]{3,2,1,0:T(4,128)}, u32[]{:S(2)}) %copy-start.7) | copy-done | bytes 4120
  1.3 1.1 %copy-done = f32[19,2,32,128]{3,2,1,0:T(8,128)S(1)} copy-done((f32[19,2,32,128]{3,2,1,0:T(8,128)S(1)}, f32[19,2,32,128]{3,2,1,0:T(8,128)}, u32[]{:S(2)}) %copy-start) | copy-done | bytes 622616
  2.4 0.7 %copy-done.6 = s32[1,1,16,128]{3,2,1,0:T(8,128)S(1)} copy-done((s32[1,1,16,128]{3,2,1,0:T(8,128)S(1)}, s32[1,1,16,128]{3,2,1,0:T(8,128)}, u32[]{:S(2)}) %copy-start.6) | copy-done | bytes 8216
  3.1 0.7 %moments.1 = (bf16[72,384]{1,0:T(8,128)(2,1)S(1)}, bf16[72,384]{1,0:T(8,128)(2,1)S(1)}, bf16[72,384]{1,0:T(8,128)(2,1)S(1)}, bf16[72,384]{1,0:T(8,128)(2,1)S(1)}...) custom-call(f32[19,2,32,128]{3,2,1,0:T(8,128)S(1)} %copy-done, ...), custom_call_target="tpu_custom_call" | custom-call | tf_op jit(solution)/shard_map/moments/pallas_call | solution.py:527
  3.8 5.1 %collective-permute-start = (bf16[72,384]{1,0:T(8,128)(2,1)S(1)}, bf16[72,384]{1,0:T(8,128)(2,1)S(1)}, u32[]{:S(2)}, u32[]{:S(2)}) collective-permute-start(bf16[72,384]{1,0:T(8,128)(2,1)S(1)} %get-tuple-element.37), channel_id=1, source_target_pairs={{0,12},{1,13},{2,14},{3,15},{4,0},{5,1},{6,2},{7,3},{8,4},{9,5},{1... | collective-permute-start | bytes 165896 | tf_op jit(solution)/shard_map/ppermute | solution.py:545
  8.9 0.0 collective-permute-start.1
  8.9 1.0 %collective-permute-start.2 = (bf16[72,384]{1,0:T(8,128)(2,1)S(1)}, bf16[72,384]{1,0:T(8,128)(2,1)S(1)}, u32[]{:S(2)}, u32[]{:S(2)}) collective-permute-start(bf16[72,384]{1,0:T(8,128)(2,1)S(1)} %get-tuple-element.39), channel_id=1, source_target_pairs={{0,4},{1,5},{2,6},{3,7},{4,8},{5,9},{6,10},{7,11},{8,12},{9,13},{1... | collective-permute-start | bytes 165896 | tf_op jit(solution)/shard_map/ppermute | solution.py:545
  9.9 1.2 %collective-permute-done.refs_1_ = bf16[72,384]{1,0:T(8,128)(2,1)S(1)} collective-permute-done((bf16[72,384]{1,0:T(8,128)(2,1)S(1)}, bf16[72,384]{1,0:T(8,128)(2,1)S(1)}, u32[]{:S(2)}, u32[]{:S(2)}) %collective-permute-start) | collective-permute-done | bytes 55328 | tf_op jit(solution)/shard_map/ppermute | solution.py:545
  11.2 2.9 %collective-permute-done.1.refs_2_ = bf16[72,384]{1,0:T(8,128)(2,1)S(1)} collective-permute-done((bf16[72,384]{1,0:T(8,128)(2,1)S(1)}, bf16[72,384]{1,0:T(8,128)(2,1)S(1)}, u32[]{:S(2)}, u32[]{:S(2)}) %collective-permute-start.1) | collective-permute-done | bytes 55328 | tf_op jit(solution)/shard_map/ppermute | solution.py:545
  14.0 0.8 %collective-permute-done.2.refs_3_ = bf16[72,384]{1,0:T(8,128)(2,1)S(1)} collective-permute-done((bf16[72,384]{1,0:T(8,128)(2,1)S(1)}, bf16[72,384]{1,0:T(8,128)(2,1)S(1)}, u32[]{:S(2)}, u32[]{:S(2)}) %collective-permute-start.2) | collective-permute-done | bytes 55328 | tf_op jit(solution)/shard_map/ppermute | solution.py:545
  14.9 1.6 %collective-permute-start.3 = (bf16[272,384]{1,0:T(8,128)(2,1)S(1)}, bf16[272,384]{1,0:T(8,128)(2,1)S(1)}, u32[]{:S(2)}, u32[]{:S(2)}) collective-permute-start(bf16[272,384]{1,0:T(8,128)(2,1)S(1)} %pack.1.refs_0_), channel_id=1, source_target_pairs={{0,1},{1,0},{2,3},{3,2},{4,5},{5,4},{6,7},{7,6},{8,9},{9,8},{10,11... | collective-permute-start | bytes 626696 | tf_op jit(solution)/shard_map/ppermute | solution.py:556
  16.5 1.5 %collective-permute-start.4 = (bf16[272,384]{1,0:T(8,128)(2,1)S(1)}, bf16[272,384]{1,0:T(8,128)(2,1)S(1)}, u32[]{:S(2)}, u32[]{:S(2)}) collective-permute-start(bf16[272,384]{1,0:T(8,128)(2,1)S(1)} %pack.1.refs_0_), channel_id=1, source_target_pairs={{0,2},{1,3},{2,0},{3,1},{4,6},{5,7},{6,4},{7,5},{8,10},{9,11},{10,... | collective-permute-start | bytes 626696 | tf_op jit(solution)/shard_map/ppermute | solution.py:556
  18.0 0.5 collective-permute-start.5
  18.5 1.5 %collective-permute-start.6 = (f32[9,2,128]{2,1,0:T(2,128)S(1)}, f32[9,2,128]{2,1,0:T(2,128)S(1)}, u32[]{:S(2)}, u32[]{:S(2)}) collective-permute-start(f32[9,2,128]{2,1,0:T(2,128)S(1)} %get-tuple-element.40), channel_id=1, source_target_pairs={{0,1},{1,2},{2,3},{3,4},{4,5},{5,6},{6,7},{7,8},{8,9},{9,10},{10,1... | collective-permute-start | bytes 27656 | tf_op jit(solution)/shard_map/ppermute | solution.py:559
  20.0 4.1 %collective-permute-start.7 = (f32[9,2,128]{2,1,0:T(2,128)S(1)}, f32[9,2,128]{2,1,0:T(2,128)S(1)}, u32[]{:S(2)}, u32[]{:S(2)}) collective-permute-start(f32[9,2,128]{2,1,0:T(2,128)S(1)} %get-tuple-element.41), channel_id=1, source_target_pairs={{1,0},{2,1},{3,2},{4,3},{5,4},{6,5},{7,6},{8,7},{9,8},{10,9},{11,1... | collective-permute-start | bytes 27656 | tf_op jit(solution)/shard_map/ppermute | solution.py:560
  24.1 1.7 %collective-permute-done.6.refs_4_ = f32[9,2,128]{2,1,0:T(2,128)S(1)} collective-permute-done((f32[9,2,128]{2,1,0:T(2,128)S(1)}, f32[9,2,128]{2,1,0:T(2,128)S(1)}, u32[]{:S(2)}, u32[]{:S(2)}) %collective-permute-start.6) | collective-permute-done | bytes 9248 | tf_op jit(solution)/shard_map/ppermute | solution.py:559
  25.8 0.0 collective-permute-done.7.refs_5_
  25.8 0.0 collective-permute-done.3.refs_1_
  25.8 0.7 %collective-permute-done.4.refs_2_ = bf16[272,384]{1,0:T(8,128)(2,1)S(1)} collective-permute-done((bf16[272,384]{1,0:T(8,128)(2,1)S(1)}, bf16[272,384]{1,0:T(8,128)(2,1)S(1)}, u32[]{:S(2)}, u32[]{:S(2)}) %collective-permute-start.4) | collective-permute-done | bytes 208928 | tf_op jit(solution)/shard_map/ppermute | solution.py:556
  26.5 0.0 collective-permute-done.5.refs_3_
  26.6 0.6 %copy-done.8 = s32[1,1,2,8]{3,2,1,0:T(2,128)S(1)} copy-done((s32[1,1,2,8]{3,2,1,0:T(2,128)S(1)}, s32[1,1,2,8]{3,2,1,0:T(2,128)}, u32[]{:S(2)}) %copy-start.8) | copy-done | bytes 88
  27.2 7.0 %chains.1 = (f32[272,384]{1,0:T(8,128)S(1)}, bf16[272,384]{1,0:T(8,128)(2,1)S(1)}, bf16[272,384]{1,0:T(8,128)(2,1)S(1)}, bf16[272,384]{1,0:T(8,128)(2,1)S(1)}, f...) custom-call(bf16[272,384]{1,0:T(8,128)(2,1)S(1)} %pack.1.refs_0_, ...), custom_call_target="tpu_custom_call" | custom-call | tf_op jit(solution)/shard_map/chains/pallas_call | solution.py:566
  34.2 0.0 copy-start.1
  34.2 1.3 %collective-permute-start.8 = (bf16[272,384]{1,0:T(8,128)(2,1)S(1)}, bf16[272,384]{1,0:T(8,128)(2,1)S(1)}, u32[]{:S(2)}, u32[]{:S(2)}) collective-permute-start(bf16[272,384]{1,0:T(8,128)(2,1)S(1)} %get-tuple-element.48), channel_id=1, source_target_pairs={{0,1},{1,0},{2,3},{3,2},{4,5},{5,4},{6,7},{7,6},{8,9},{9,8},{10,11... | collective-permute-start | bytes 626696 | tf_op jit(solution)/shard_map/ppermute | solution.py:603
  35.6 0.6 %collective-permute-start.9 = (bf16[272,384]{1,0:T(8,128)(2,1)S(1)}, bf16[272,384]{1,0:T(8,128)(2,1)S(1)}, u32[]{:S(2)}, u32[]{:S(2)}) collective-permute-start(bf16[272,384]{1,0:T(8,128)(2,1)S(1)} %get-tuple-element.49), channel_id=1, source_target_pairs={{0,2},{1,3},{2,0},{3,1},{4,6},{5,7},{6,4},{7,5},{8,10},{9,11},{10,... | collective-permute-start | bytes 626696 | tf_op jit(solution)/shard_map/ppermute | solution.py:603
  36.2 1.6 %collective-permute-start.10 = (bf16[272,384]{1,0:T(8,128)(2,1)S(1)}, bf16[272,384]{1,0:T(8,128)(2,1)S(1)}, u32[]{:S(2)}, u32[]{:S(2)}) collective-permute-start(bf16[272,384]{1,0:T(8,128)(2,1)S(1)} %get-tuple-element.50), channel_id=1, source_target_pairs={{0,3},{1,2},{2,1},{3,0},{4,7},{5,6},{6,5},{7,4},{8,11},{9,10},{10,... | collective-permute-start | bytes 626696 | tf_op jit(solution)/shard_map/ppermute | solution.py:603
  37.8 0.0 collective-permute-start.11
  37.8 1.2 %collective-permute-done.11 = f32[8,192]{1,0:T(8,128)S(1)} collective-permute-done((f32[8,192]{1,0:T(8,128)S(1)}, f32[8,192]{1,0:T(8,128)S(1)}, u32[]{:S(2)}, u32[]{:S(2)}) %collective-permute-start.11) | collective-permute-done | bytes 6176 | tf_op jit(solution)/shard_map/ppermute | solution.py:605
  39.0 1.9 %collective-permute-done.8.refs_0_ = bf16[272,384]{1,0:T(8,128)(2,1)S(1)} collective-permute-done((bf16[272,384]{1,0:T(8,128)(2,1)S(1)}, bf16[272,384]{1,0:T(8,128)(2,1)S(1)}, u32[]{:S(2)}, u32[]{:S(2)}) %collective-permute-start.8) | collective-permute-done | bytes 208928 | tf_op jit(solution)/shard_map/ppermute | solution.py:603
  40.9 3.2 %collective-permute-done.9.refs_1_ = bf16[272,384]{1,0:T(8,128)(2,1)S(1)} collective-permute-done((bf16[272,384]{1,0:T(8,128)(2,1)S(1)}, bf16[272,384]{1,0:T(8,128)(2,1)S(1)}, u32[]{:S(2)}, u32[]{:S(2)}) %collective-permute-start.9) | collective-permute-done | bytes 208928 | tf_op jit(solution)/shard_map/ppermute | solution.py:603
  44.1 0.0 collective-permute-done.10.refs_2_
  44.1 0.1 sums.1
  44.2 1.8 %collective-permute-start.12 = (bf16[72,384]{1,0:T(8,128)(2,1)S(1)}, bf16[72,384]{1,0:T(8,128)(2,1)S(1)}, u32[]{:S(2)}, u32[]{:S(2)}) collective-permute-start(bf16[72,384]{1,0:T(8,128)(2,1)S(1)} %get-tuple-element.56), channel_id=1, source_target_pairs={{0,4},{1,5},{2,6},{3,7},{4,8},{5,9},{6,10},{7,11},{8,12},{9,13},{1... | collective-permute-start | bytes 165896 | tf_op jit(solution)/shard_map/ppermute | solution.py:618
  46.0 2.6 %collective-permute-start.13 = (bf16[72,384]{1,0:T(8,128)(2,1)S(1)}, bf16[72,384]{1,0:T(8,128)(2,1)S(1)}, u32[]{:S(2)}, u32[]{:S(2)}) collective-permute-start(bf16[72,384]{1,0:T(8,128)(2,1)S(1)} %get-tuple-element.57), channel_id=1, source_target_pairs={{0,8},{1,9},{2,10},{3,11},{4,12},{5,13},{6,14},{7,15},{8,0},{9,1},... | collective-permute-start | bytes 165896 | tf_op jit(solution)/shard_map/ppermute | solution.py:618
  48.6 2.8 %collective-permute-start.14 = (bf16[72,384]{1,0:T(8,128)(2,1)S(1)}, bf16[72,384]{1,0:T(8,128)(2,1)S(1)}, u32[]{:S(2)}, u32[]{:S(2)}) collective-permute-start(bf16[72,384]{1,0:T(8,128)(2,1)S(1)} %get-tuple-element.58), channel_id=1, source_target_pairs={{0,12},{1,13},{2,14},{3,15},{4,0},{5,1},{6,2},{7,3},{8,4},{9,5},{1... | collective-permute-start | bytes 165896 | tf_op jit(solution)/shard_map/ppermute | solution.py:618
  51.5 0.1 concatenate.24
  51.6 0.1 concatenate.25
  51.6 0.0 collective-permute-done.12.refs_1_
  51.6 0.0 collective-permute-done.13.refs_2_
  51.6 1.6 %collective-permute-done.14.refs_3_ = bf16[72,384]{1,0:T(8,128)(2,1)S(1)} collective-permute-done((bf16[72,384]{1,0:T(8,128)(2,1)S(1)}, bf16[72,384]{1,0:T(8,128)(2,1)S(1)}, u32[]{:S(2)}, u32[]{:S(2)}) %collective-permute-start.14) | collective-permute-done | bytes 55328 | tf_op jit(solution)/shard_map/ppermute | solution.py:618
  53.3 0.3 cross.1
  53.6 0.1 collective-permute-start.15
  53.7 0.6 %maximum_select_fusion = f32[1,1,2,1536]{3,2,1,0:T(2,128)} fusion(f32[1,1,1,1536]{3,2,1,0:T(1,128)S(1)} %concatenate.25, f32[1,1,1,1536]{3,2,1,0:T(1,128)S(1)} %concatenate.24, pred[]{:T(512)S(6)} %eq.3), kind=kLoop, calls=%fused_computation | loop fusion | flops 9216 | bytes 24577 | tf_op jit(solution)/shard_map/jit(_where)/select_n | solution.py:653
  54.3 1.1 %collide.1.part_ref = f32[19,2,32,128]{3,2,1,0:T(8,128)} custom-call(f32[19,2,32,128]{3,2,1,0:T(8,128)S(1)} %copy-done.1, f32[5,64,128]{2,1,0:T(8,128)S(1)} %get-tuple-element.62.state_ref, f32[19,2,128]{2,1,0:T(2,128)S(1)} %get-tuple-element.63.edge_ref), custom_call_target="tpu_custom_call" | custom-call | tf_op jit(solution)/shard_map/collide/pallas_call | solution.py:632
  55.4 0.0 collective-permute-done.15.came_ref
  55.4 0.7 %merge.1 = f32[19,2,32,128]{3,2,1,0:T(8,128)} custom-call(f32[10,32,128]{2,1,0:T(8,128)S(1)} %collective-permute-done.15.came_ref, f32[19,2,32,128]{3,2,1,0:T(8,128)} %collide.1.part_ref), custom_call_target="tpu_custom_call", output_to_operand_aliasing={{}: (1, {})} | custom-call | tf_op jit(solution)/shard_map/merge/pallas_call | solution.py:640
  (16 shorter events, 0.1 us)
Async XLA Ops:
  0.6 0.7 %copy-start.7 = (s32[1,1,4,256]{3,2,1,0:T(4,128)S(1)}, s32[1,1,4,256]{3,2,1,0:T(4,128)}, u32[]{:S(2)}) copy-start(s32[1,1,4,256]{3,2,1,0:T(4,128)} %param.13) | copy-start | bytes 12292
  0.6 0.7 %copy-start.10 = (s32[1,1,16]{2,1,0:T(1,128)S(1)}, s32[1,1,16]{2,1,0:T(1,128)}, u32[]{:S(2)}) copy-start(s32[1,1,16]{2,1,0:T(1,128)} %param.15) | copy-start | bytes 196
  1.3 1.1 %copy-start = (f32[19,2,32,128]{3,2,1,0:T(8,128)S(1)}, f32[19,2,32,128]{3,2,1,0:T(8,128)}, u32[]{:S(2)}) copy-start(f32[19,2,32,128]{3,2,1,0:T(8,128)} %pop_ref.3) | copy-start | bytes 1867780
  2.4 0.7 %copy-start.6 = (s32[1,1,16,128]{3,2,1,0:T(8,128)S(1)}, s32[1,1,16,128]{3,2,1,0:T(8,128)}, u32[]{:S(2)}) copy-start(s32[1,1,16,128]{3,2,1,0:T(8,128)} %param.14) | copy-start | bytes 24580
  3.8 7.4 %collective-permute-start = (bf16[72,384]{1,0:T(8,128)(2,1)S(1)}, bf16[72,384]{1,0:T(8,128)(2,1)S(1)}, u32[]{:S(2)}, u32[]{:S(2)}) collective-permute-start(bf16[72,384]{1,0:T(8,128)(2,1)S(1)} %get-tuple-element.37), channel_id=1, source_target_pairs={{0,12},{1,13},{2,14},{3,15},{4,0},{5,1},{6,2},{7,3},{8,4},{9,5},{1... | collective-permute-start | bytes 165896 | tf_op jit(solution)/shard_map/ppermute | solution.py:545
  8.9 5.1 %collective-permute-start.1 = (bf16[72,384]{1,0:T(8,128)(2,1)S(1)}, bf16[72,384]{1,0:T(8,128)(2,1)S(1)}, u32[]{:S(2)}, u32[]{:S(2)}) collective-permute-start(bf16[72,384]{1,0:T(8,128)(2,1)S(1)} %get-tuple-element.38), channel_id=1, source_target_pairs={{0,8},{1,9},{2,10},{3,11},{4,12},{5,13},{6,14},{7,15},{8,0},{9,1},... | collective-permute-start | bytes 165896 | tf_op jit(solution)/shard_map/ppermute | solution.py:545
  8.9 6.0 %collective-permute-start.2 = (bf16[72,384]{1,0:T(8,128)(2,1)S(1)}, bf16[72,384]{1,0:T(8,128)(2,1)S(1)}, u32[]{:S(2)}, u32[]{:S(2)}) collective-permute-start(bf16[72,384]{1,0:T(8,128)(2,1)S(1)} %get-tuple-element.39), channel_id=1, source_target_pairs={{0,4},{1,5},{2,6},{3,7},{4,8},{5,9},{6,10},{7,11},{8,12},{9,13},{1... | collective-permute-start | bytes 165896 | tf_op jit(solution)/shard_map/ppermute | solution.py:545
  14.9 11.7 %copy-start.2 = (f32[1,1,3,64,256]{4,3,2,1,0:T(8,128)S(1)}, f32[1,1,3,64,256]{4,3,2,1,0:T(8,128)}, u32[]{:S(2)}) copy-start(f32[1,1,3,64,256]{4,3,2,1,0:T(8,128)} %param.11) | copy-start | bytes 589828
  14.9 11.7 %copy-start.3 = (s32[1,1,64,256]{3,2,1,0:T(8,128)S(1)}, s32[1,1,64,256]{3,2,1,0:T(8,128)}, u32[]{:S(2)}) copy-start(s32[1,1,64,256]{3,2,1,0:T(8,128)} %param.12) | copy-start | bytes 196612
  14.9 11.7 %copy-start.4 = (f32[64,64]{1,0:T(8,128)S(1)}, f32[64,64]{1,0:T(8,128)}, u32[]{:S(2)}) copy-start(f32[64,64]{1,0:T(8,128)} %constant.12.clone.refs_9_) | copy-start | bytes 49156
  14.9 11.7 %copy-start.5 = (f32[64,1]{1,0:T(8,128)S(1)}, f32[64,1]{1,0:T(8,128)}, u32[]{:S(2)}) copy-start(f32[64,1]{1,0:T(8,128)} %constant.13.clone.refs_10_) | copy-start | bytes 772
  14.9 10.9 %collective-permute-start.3 = (bf16[272,384]{1,0:T(8,128)(2,1)S(1)}, bf16[272,384]{1,0:T(8,128)(2,1)S(1)}, u32[]{:S(2)}, u32[]{:S(2)}) collective-permute-start(bf16[272,384]{1,0:T(8,128)(2,1)S(1)} %pack.1.refs_0_), channel_id=1, source_target_pairs={{0,1},{1,0},{2,3},{3,2},{4,5},{5,4},{6,7},{7,6},{8,9},{9,8},{10,11... | collective-permute-start | bytes 626696 | tf_op jit(solution)/shard_map/ppermute | solution.py:556
  16.5 10.0 %collective-permute-start.4 = (bf16[272,384]{1,0:T(8,128)(2,1)S(1)}, bf16[272,384]{1,0:T(8,128)(2,1)S(1)}, u32[]{:S(2)}, u32[]{:S(2)}) collective-permute-start(bf16[272,384]{1,0:T(8,128)(2,1)S(1)} %pack.1.refs_0_), channel_id=1, source_target_pairs={{0,2},{1,3},{2,0},{3,1},{4,6},{5,7},{6,4},{7,5},{8,10},{9,11},{10,... | collective-permute-start | bytes 626696 | tf_op jit(solution)/shard_map/ppermute | solution.py:556
  18.0 8.5 %collective-permute-start.5 = (bf16[272,384]{1,0:T(8,128)(2,1)S(1)}, bf16[272,384]{1,0:T(8,128)(2,1)S(1)}, u32[]{:S(2)}, u32[]{:S(2)}) collective-permute-start(bf16[272,384]{1,0:T(8,128)(2,1)S(1)} %pack.1.refs_0_), channel_id=1, source_target_pairs={{0,3},{1,2},{2,1},{3,0},{4,7},{5,6},{6,5},{7,4},{8,11},{9,10},{10,... | collective-permute-start | bytes 626696 | tf_op jit(solution)/shard_map/ppermute | solution.py:556
  18.5 7.4 %collective-permute-start.6 = (f32[9,2,128]{2,1,0:T(2,128)S(1)}, f32[9,2,128]{2,1,0:T(2,128)S(1)}, u32[]{:S(2)}, u32[]{:S(2)}) collective-permute-start(f32[9,2,128]{2,1,0:T(2,128)S(1)} %get-tuple-element.40), channel_id=1, source_target_pairs={{0,1},{1,2},{2,3},{3,4},{4,5},{5,6},{6,7},{7,8},{8,9},{9,10},{10,1... | collective-permute-start | bytes 27656 | tf_op jit(solution)/shard_map/ppermute | solution.py:559
  20.0 5.9 %collective-permute-start.7 = (f32[9,2,128]{2,1,0:T(2,128)S(1)}, f32[9,2,128]{2,1,0:T(2,128)S(1)}, u32[]{:S(2)}, u32[]{:S(2)}) collective-permute-start(f32[9,2,128]{2,1,0:T(2,128)S(1)} %get-tuple-element.41), channel_id=1, source_target_pairs={{1,0},{2,1},{3,2},{4,3},{5,4},{6,5},{7,6},{8,7},{9,8},{10,9},{11,1... | collective-permute-start | bytes 27656 | tf_op jit(solution)/shard_map/ppermute | solution.py:560
  26.5 0.7 %copy-start.8 = (s32[1,1,2,8]{3,2,1,0:T(2,128)S(1)}, s32[1,1,2,8]{3,2,1,0:T(2,128)}, u32[]{:S(2)}) copy-start(s32[1,1,2,8]{3,2,1,0:T(2,128)} %param.16) | copy-start | bytes 196
  26.5 0.7 %copy-start.9 = (s32[1,1,2]{2,1,0:T(1,128)S(1)}, s32[1,1,2]{2,1,0:T(1,128)}, u32[]{:S(2)}) copy-start(s32[1,1,2]{2,1,0:T(1,128)} %param.17) | copy-start | bytes 28
  34.2 19.1 %copy-start.1 = (f32[19,2,32,128]{3,2,1,0:T(8,128)S(1)}, f32[19,2,32,128]{3,2,1,0:T(8,128)}, u32[]{:S(2)}) copy-start(f32[19,2,32,128]{3,2,1,0:T(8,128)} %pop_ref.3) | copy-start | bytes 1867780
  34.2 6.6 %collective-permute-start.8 = (bf16[272,384]{1,0:T(8,128)(2,1)S(1)}, bf16[272,384]{1,0:T(8,128)(2,1)S(1)}, u32[]{:S(2)}, u32[]{:S(2)}) collective-permute-start(bf16[272,384]{1,0:T(8,128)(2,1)S(1)} %get-tuple-element.48), channel_id=1, source_target_pairs={{0,1},{1,0},{2,3},{3,2},{4,5},{5,4},{6,7},{7,6},{8,9},{9,8},{10,11... | collective-permute-start | bytes 626696 | tf_op jit(solution)/shard_map/ppermute | solution.py:603
  35.6 8.5 %collective-permute-start.9 = (bf16[272,384]{1,0:T(8,128)(2,1)S(1)}, bf16[272,384]{1,0:T(8,128)(2,1)S(1)}, u32[]{:S(2)}, u32[]{:S(2)}) collective-permute-start(bf16[272,384]{1,0:T(8,128)(2,1)S(1)} %get-tuple-element.49), channel_id=1, source_target_pairs={{0,2},{1,3},{2,0},{3,1},{4,6},{5,7},{6,4},{7,5},{8,10},{9,11},{10,... | collective-permute-start | bytes 626696 | tf_op jit(solution)/shard_map/ppermute | solution.py:603
  36.2 7.9 %collective-permute-start.10 = (bf16[272,384]{1,0:T(8,128)(2,1)S(1)}, bf16[272,384]{1,0:T(8,128)(2,1)S(1)}, u32[]{:S(2)}, u32[]{:S(2)}) collective-permute-start(bf16[272,384]{1,0:T(8,128)(2,1)S(1)} %get-tuple-element.50), channel_id=1, source_target_pairs={{0,3},{1,2},{2,1},{3,0},{4,7},{5,6},{6,5},{7,4},{8,11},{9,10},{10,... | collective-permute-start | bytes 626696 | tf_op jit(solution)/shard_map/ppermute | solution.py:603
  37.8 1.2 %collective-permute-start.11 = (f32[8,192]{1,0:T(8,128)S(1)}, f32[8,192]{1,0:T(8,128)S(1)}, u32[]{:S(2)}, u32[]{:S(2)}) collective-permute-start(f32[8,192]{1,0:T(8,128)S(1)} %get-tuple-element.51), channel_id=1, source_target_pairs={{0,16},{16,0},{1,17},{17,1},{2,18},{18,2},{3,19},{19,3},{4,20},{20... | collective-permute-start | bytes 18440 | tf_op jit(solution)/shard_map/ppermute | solution.py:605
  44.2 7.4 %collective-permute-start.12 = (bf16[72,384]{1,0:T(8,128)(2,1)S(1)}, bf16[72,384]{1,0:T(8,128)(2,1)S(1)}, u32[]{:S(2)}, u32[]{:S(2)}) collective-permute-start(bf16[72,384]{1,0:T(8,128)(2,1)S(1)} %get-tuple-element.56), channel_id=1, source_target_pairs={{0,4},{1,5},{2,6},{3,7},{4,8},{5,9},{6,10},{7,11},{8,12},{9,13},{1... | collective-permute-start | bytes 165896 | tf_op jit(solution)/shard_map/ppermute | solution.py:618
  46.0 5.6 %collective-permute-start.13 = (bf16[72,384]{1,0:T(8,128)(2,1)S(1)}, bf16[72,384]{1,0:T(8,128)(2,1)S(1)}, u32[]{:S(2)}, u32[]{:S(2)}) collective-permute-start(bf16[72,384]{1,0:T(8,128)(2,1)S(1)} %get-tuple-element.57), channel_id=1, source_target_pairs={{0,8},{1,9},{2,10},{3,11},{4,12},{5,13},{6,14},{7,15},{8,0},{9,1},... | collective-permute-start | bytes 165896 | tf_op jit(solution)/shard_map/ppermute | solution.py:618
  48.6 4.7 %collective-permute-start.14 = (bf16[72,384]{1,0:T(8,128)(2,1)S(1)}, bf16[72,384]{1,0:T(8,128)(2,1)S(1)}, u32[]{:S(2)}, u32[]{:S(2)}) collective-permute-start(bf16[72,384]{1,0:T(8,128)(2,1)S(1)} %get-tuple-element.58), channel_id=1, source_target_pairs={{0,12},{1,13},{2,14},{3,15},{4,0},{5,1},{6,2},{7,3},{8,4},{9,5},{1... | collective-permute-start | bytes 165896 | tf_op jit(solution)/shard_map/ppermute | solution.py:618
  53.6 1.8 %collective-permute-start.15 = (f32[10,32,128]{2,1,0:T(8,128)S(1)}, f32[10,32,128]{2,1,0:T(8,128)S(1)}, u32[]{:S(2)}, u32[]{:S(2)}) collective-permute-start(f32[10,32,128]{2,1,0:T(8,128)S(1)} %get-tuple-element.61), channel_id=1, source_target_pairs={{0,16},{16,0},{1,17},{17,1},{2,18},{18,2},{3,19},{19,3},{4,20},{20... | collective-permute-start | bytes 491528 | tf_op jit(solution)/shard_map/ppermute | solution.py:631

commit v3 on v2

--- a/solution.py
+++ b/solution.py
@@ -53,7 +53,8 @@
 
 
 class Plan:
-    def __init__(self, groups, rows, size_y):
+    def __init__(self, groups, rows, size_y, length):
+        self.length = length
         self.groups = groups
         self.outer = 4
         self.inner = groups // self.outer
@@ -65,10 +66,10 @@
         self.main = self.outer * rows
         self.block = (self.main + self.outer * self.extra + 15) // 16 * 16
 
-    def outer_shift(self, k):
+    def outer_swap(self, k):
         z_count, w_count = self.outer, self.inner
         return [
-            (z * w_count + w, (z + k) % z_count * w_count + w)
+            (z * w_count + w, (z ^ k) * w_count + w)
             for z in range(z_count)
             for w in range(w_count)
         ]
@@ -107,11 +108,10 @@
     return (density, momentum)
 
 
-def moment_kernel(plan, pop_hbm, rows_hbm, count_hbm, slots_hbm, *outs):
+def moment_kernel(plan, pop_hbm, rows_hbm, count_hbm, slots_hbm, list_hbm, live_hbm, *outs):
     msg_refs = outs[: plan.outer]
-    up_ref, down_ref, state_ref, slots_ref, pop_ref, rows_ref, count_ref, sem = outs[
-        plan.outer :
-    ]
+    up_ref, down_ref, state_ref, slots_ref, leave_ref = outs[plan.outer : plan.outer + 5]
+    pop_ref, rows_ref, count_ref, list_ref, live_ref, sem = outs[plan.outer + 5 :]
     length = pop_ref.shape[3]
     size_x, size_y = plan.size_x, plan.size_y
     loads = [
@@ -122,6 +122,8 @@
         pltpu.make_async_copy(rows_hbm, rows_ref, sem.at[size_x]),
         pltpu.make_async_copy(count_hbm, count_ref, sem.at[size_x + 1]),
         pltpu.make_async_copy(slots_hbm, slots_ref, sem.at[size_x + 2]),
+        pltpu.make_async_copy(list_hbm, list_ref, sem.at[size_x + 3]),
+        pltpu.make_async_copy(live_hbm, live_ref, sem.at[size_x + 4]),
     ]
     for copy in loads + others:
         copy.start()
@@ -143,6 +145,14 @@
                 out[at + slot, x : x + 1, :] = value[row : row + 1]
     for copy in others:
         copy.wait()
+    brick = lax.axis_index("brick")
+    leaving = list_ref.shape[1]
+    for i in range(list_ref.shape[0]):
+        target = brick ^ i
+        for s in range(leaving):
+            number = jnp.where(s < live_ref[target], list_ref[target, s], -1)
+            at = i * leaving + s
+            leave_ref[at : at + 1, :] = jnp.full((1, length), number, jnp.int32)
     me = lax.axis_index("chain")
     z = me // plan.inner
     w = me % plan.inner
@@ -151,7 +161,7 @@
     for k, msg in enumerate(msg_refs):
         tables = []
         for m in range(plan.inner):
-            target = (z + plan.outer - k) % plan.outer * plan.inner + (w ^ m)
+            target = (z ^ k) * plan.inner + (w ^ m)
             row = rows_ref[pl.ds(target, 1), :]
             tables.append(jnp.where(lane < count_ref[target], row, -1).astype(f32))
         if extra > plan.inner:
@@ -174,114 +184,103 @@
     out_ref[plan.main :, :] = jnp.concatenate(tails, axis=0).astype(bf16)
 
 
+def prepare_kernel(plan, own_ref, pos_ref, site_ref, spectrum_ref, rows_ref, bead_ref, damp_ref):
+    rows_ref[...] = own_ref[...]
+    beads, chains = site_ref.shape
+    per_slot = beads * plan.length // bead_ref.shape[0]
+    step = 32
+    step_iota = lax.broadcasted_iota(jnp.int32, (step, 128), 0)
+    for r in range(beads // per_slot):
+        for tile in range(chains // 128):
+            lanes = slice(tile * 128, tile * 128 + 128)
+            for start in range(0, plan.length, step):
+                bead = jnp.full((step, 128), -1, jnp.int32)
+                for j in range(per_slot):
+                    at = slice(r * per_slot + j, r * per_slot + j + 1)
+                    bead = jnp.where(step_iota == site_ref[at, lanes] - start, j, bead)
+                first = r * plan.length + start
+                bead_ref[first : first + step, lanes] = bead
+
+    stretch = None
+    for k in range(3):
+        bond = pos_ref[k, 1:, :] - pos_ref[k, : beads - 1, :]
+        part = jnp.sum(bond * bond, axis=0, keepdims=True)
+        stretch = part if stretch is None else stretch + part
+    stretch = stretch / (beads - 1)
+    stiffness = SPRING / (1.0 - stretch / MAX_STRETCH)
+    damp_ref[...] = 1.0 / (1.0 + spectrum_ref[...] * stiffness)
+
+
+def one_hot(condition):
+    return jnp.where(condition, 1.0, 0.0).astype(bf16)
+
+
+def place_of(plan, p):
+    me = lax.axis_index("chain")
+    z = me // plan.inner
+    w = me % plan.inner
+    return ((p % plan.inner) ^ w, (p // plan.inner) ^ z)
+
+
+def pick_block(plan, capacity, m, block_ref, slot_ref, table, hot_ref):
+    outer, rows, main, extra, length = plan.outer, plan.rows, plan.main, plan.extra, plan.length
+    slots, chains = slot_ref.shape
+    tail = block_ref[main:, :length].astype(f32)
+    names = [tail[k * extra + m : k * extra + m + 1] for k in range(outer)]
+    names += [jnp.zeros((8 - outer, length), f32)] if outer < 8 else []
+    names = jnp.concatenate(names, axis=0).astype(bf16)
+    eye = lax.broadcasted_iota(jnp.int32, (length, length), 0)
+    eye = one_hot(eye == lax.broadcasted_iota(jnp.int32, (length, length), 1))
+    for k in range(3):
+        part = slice(k * length, (k + 1) * length)
+        table[part, :] = lax.dot_general(
+            eye, block_ref[:main, part], NT, preferred_element_type=f32
+        ).astype(bf16)
+    site_iota = lax.broadcasted_iota(jnp.int32, (length, chains), 0)
+    outer_iota = lax.broadcasted_iota(jnp.int32, (names.shape[0], chains), 0)
+    main_iota = lax.broadcasted_iota(jnp.int32, (main, chains), 0)
+    found = []
+    for r in range(slots):
+        slot = slot_ref[r : r + 1, :]
+        which, k = place_of(plan, slot // capacity)
+        pick = one_hot(site_iota == slot % capacity)
+        looked = jnp.dot(names, pick, preferred_element_type=f32)
+        row = jnp.sum(jnp.where(outer_iota == k, looked, 0.0), axis=0, keepdims=True)
+        row = jnp.where(which == m, row.astype(jnp.int32), -1)
+        first = jnp.where(row >= 0, k * rows + row, -1)
+        hot_ref[:, r * chains : (r + 1) * chains] = one_hot(main_iota == first)
+        found.append(row)
+    picked = jnp.dot(table[...], hot_ref[...], preferred_element_type=f32).astype(bf16)
+    return (picked, jnp.concatenate(found, axis=0))
+
+
+def pick_kernel(plan, capacity, m, block_ref, slot_ref, *refs):
+    before, (hot_ref, picked_ref, row_ref, table) = refs[:-4], refs[-4:]
+    picked, row = pick_block(plan, capacity, m, block_ref, slot_ref, table, hot_ref)
+    if before:
+        picked = picked + before[0][...]
+        row = jnp.maximum(row, before[1][...])
+    picked_ref[...] = picked
+    row_ref[...] = row
+
+
 def chain_kernel(plan, capacity, *refs):
-    block_refs = refs[: plan.inner]
-    (
-        pos_ref,
-        site_ref,
-        slot_ref,
-        list_hbm,
-        live_hbm,
-        basis_ref,
-        spectrum_ref,
-        own_ref,
-    ) = refs[plan.inner : plan.inner + 8]
-    send_refs = refs[plan.inner + 8 : 2 * plan.inner + 7]
-    (
-        moved_ref,
-        stay_ref,
-        leave_ref,
-        table,
-        turned,
-        onehot,
-        smooth,
-        velocity,
-        force,
-        spread,
-        sums,
-        list_ref,
-        live_ref,
-        sem,
-    ) = refs[2 * plan.inner + 7 :]
-    inner, outer, rows, extra = plan.inner, plan.outer, plan.rows, plan.extra
-    main, block, groups = plan.main, plan.block, plan.groups
-    length = table.shape[1] // 3
+    inner, main, block, length = plan.inner, plan.main, plan.block, plan.length
+    hot_refs, refs = list(refs[: inner - 1]), refs[inner - 1 :]
+    block_ref, slot_ref, before_ref, row_ref, pos_ref, site_ref = refs[:6]
+    bead_ref, damp_ref, basis_ref = refs[6:9]
+    send_refs, refs = refs[9 : 8 + inner], refs[8 + inner :]
+    moved_ref, spread, extras, table, last_hot, smooth, velocity, force = refs
+    hot_refs.append(last_hot)
     slots, chains = slot_ref.shape
     beads = pos_ref.shape[1]
     per_slot = beads // slots
-    me = lax.axis_index("chain")
-    z = me // inner
-    w = me % inner
-
-    loads = [
-        pltpu.make_async_copy(list_hbm, list_ref, sem.at[0]),
-        pltpu.make_async_copy(live_hbm, live_ref, sem.at[1]),
-    ]
-    for copy in loads:
-        copy.start()
-
-    table_rows = []
-    for m in range(inner):
-        table[m * block : m * block + main, :] = block_refs[m][:main, :]
-        table[m * block + main : (m + 1) * block, :] = jnp.zeros(
-            (block - main, 3 * length), bf16
-        )
-        names = block_refs[m][main:, :length].astype(f32)
-        for k in range(outer):
-            table_rows.append(names[k * extra + m : k * extra + m + 1])
-    names = jnp.concatenate(table_rows, axis=0).astype(bf16)
-
-    eye = (
-        lax.broadcasted_iota(jnp.int32, (length, length), 0)
-        == lax.broadcasted_iota(jnp.int32, (length, length), 1)
-    )
-    eye = jnp.where(eye, 1.0, 0.0).astype(bf16)
-    for k in range(3):
-        part = slice(k * length, (k + 1) * length)
-        turned[part, :] = lax.dot_general(
-            eye, table[:, part], NT, preferred_element_type=f32
-        ).astype(bf16)
-
-    site_iota = lax.broadcasted_iota(jnp.int32, (length, chains), 0)
-    group_iota = lax.broadcasted_iota(jnp.int32, (groups, chains), 0)
-    main_iota = lax.broadcasted_iota(jnp.int32, (main, chains), 0)
-    extra_iota = lax.broadcasted_iota(jnp.int32, (block - main, chains), 0)
-
-    def place_of(p):
-        return ((p % inner) ^ w, (p // inner - z + outer) % outer)
-
-    for r in range(slots):
-        slot = slot_ref[r : r + 1, :]
-        p = slot // capacity
-        s = slot % capacity
-        m, k = place_of(p)
-        pick = jnp.where(site_iota == s, 1.0, 0.0).astype(bf16)
-        looked = jnp.dot(names, pick, preferred_element_type=f32)
-        row = jnp.sum(
-            jnp.where(group_iota == m * outer + k, looked, 0.0), axis=0, keepdims=True
-        )
-        row = row.astype(jnp.int32)
-        live = row >= 0
-        y = row % plan.size_y
-        x = row // plan.size_y
-        first = jnp.where(live, m * block + k * rows + row, -1)
-        m, k = place_of((p + 1) % groups)
-        above = m * block + k * extra + x
-        m, k = place_of((p + groups - 1) % groups)
-        below = m * block + k * extra + plan.size_x + x
-        second = jnp.where(y == plan.size_y - 1, above, jnp.where(y == 0, below, -1))
-        second = jnp.where(live, second, -1)
-        lanes = slice(r * chains, (r + 1) * chains)
-        for m in range(inner):
-            base = m * block
-            onehot[base : base + main, lanes] = jnp.where(
-                main_iota == first - base, 1.0, 0.0
-            ).astype(bf16)
-            onehot[base + main : base + block, lanes] = jnp.where(
-                extra_iota == second - base, 1.0, 0.0
-            ).astype(bf16)
-
-    picked = jnp.dot(turned[...], onehot[...], preferred_element_type=f32).astype(bf16)
+    groups = plan.groups
+    tail = block - main
+
+    picked, row = pick_block(plan, capacity, inner - 1, block_ref, slot_ref, table, last_hot)
+    picked = picked + before_ref[...]
+    row = jnp.maximum(row, row_ref[...])
     near = lax.broadcasted_iota(jnp.int32, (length, length), 0)
     near = near - lax.broadcasted_iota(jnp.int32, (length, length), 1)
     around = (near == 1) | (near == -1) | (near == length - 1) | (near == 1 - length)
@@ -289,6 +288,19 @@
     for k in range(3):
         part = slice(k * length, (k + 1) * length)
         smooth[part, :] = jnp.dot(kernel, picked[part], preferred_element_type=f32)
+
+    p = slot_ref[...] // capacity
+    y = row % plan.size_y
+    x = row // plan.size_y
+    m, k = place_of(plan, (p + 1) % groups)
+    above = m * tail + k * plan.extra + x
+    m, k = place_of(plan, (p + groups - 1) % groups)
+    below = m * tail + k * plan.extra + plan.size_x + x
+    second = jnp.where(y == plan.size_y - 1, above, jnp.where(y == 0, below, -1))
+    second = jnp.where(row >= 0, second, -1)
+    extra_iota = lax.broadcasted_iota(jnp.int32, (inner * tail, chains), 0)
+    for r in range(slots):
+        extras[:, r * chains : (r + 1) * chains] = one_hot(extra_iota == second[r : r + 1])
 
     for r in range(slots):
         for octet in range(per_slot // 8):
@@ -309,14 +321,7 @@
                         value = jnp.where(which == t, got, value)
                     velocity[k, at, lanes] = value
 
-    stretch = None
-    for k in range(3):
-        bond = pos_ref[k, 1:, :] - pos_ref[k, : beads - 1, :]
-        part = jnp.sum(bond * bond, axis=0, keepdims=True)
-        stretch = part if stretch is None else stretch + part
-    stretch = stretch / (beads - 1)
-    stiffness = SPRING / (1.0 - stretch / MAX_STRETCH)
-    damping = 1.0 / (1.0 + spectrum_ref[...] * stiffness)
+    damping = damp_ref[...]
     basis = basis_ref[...]
     for k in range(3):
         amps = jnp.dot(
@@ -332,44 +337,72 @@
         moved_ref[k] = moved
         force[k] = (moved - pos_ref[k]) - velocity[k]
 
-    for copy in loads:
-        copy.wait()
-    brick = lax.axis_index("brick")
-    chain_iota = lax.broadcasted_iota(jnp.int32, (1, chains), 1)
-    leaving = list_ref.shape[1]
+    step = 32
+    octets = per_slot // 8
+    for r in range(slots):
+        for tile in range(chains // 128):
+            lanes = slice(tile * 128, tile * 128 + 128)
+            wide = slice(r * chains + tile * 128, r * chains + tile * 128 + 128)
+            mine = slice(r * per_slot, (r + 1) * per_slot)
+            site = site_ref[mine, lanes]
+            joint = [jnp.zeros((per_slot, 128), f32) for _ in range(3)]
+            for j in range(per_slot):
+                at = slice(r * per_slot + j, r * per_slot + j + 1)
+                same = site == site_ref[at, lanes]
+                for k in range(3):
+                    joint[k] = joint[k] + jnp.where(same, force[k, at, lanes], 0.0)
+            for start in range(0, length, step):
+                first = r * length + start
+                bead = bead_ref[first : first + step, lanes]
+                inside = bead & 7
+                which = bead >> 3
+                for k in range(3):
+                    out = slice(k * length + start, k * length + start + step)
+                    value = jnp.zeros((step, 128), f32)
+                    for octet in range(octets):
+                        source = joint[k][octet * 8 : octet * 8 + 8]
+                        got = jnp.concatenate(
+                            [
+                                jnp.take_along_axis(
+                                    source,
+                                    inside[t : t + 8],
+                                    axis=0,
+                                    mode="promise_in_bounds",
+                                )
+                                for t in range(0, step, 8)
+                            ],
+                            axis=0,
+                        )
+                        value = jnp.where(which == octet, got, value)
+                    spread[out, wide] = value.astype(bf16)
+
+    sides = lax.dot_general(extras[...], spread[...], NT, preferred_element_type=f32)
+    for m in range(1, inner):
+        send_refs[m - 1][:main, :] = lax.dot_general(
+            hot_refs[m][...], spread[...], NT, preferred_element_type=f32
+        ).astype(bf16)
+        send_refs[m - 1][main:, :] = sides[m * tail : (m + 1) * tail].astype(bf16)
+
+
+def own_kernel(plan, hot_ref, extras_ref, spread_ref, moved_ref, number_ref, own_ref, stay_ref, leave_ref):
+    main = plan.main
+    tail = plan.block - main
+    beads, chains = moved_ref.shape[1:]
+    leaving = number_ref.shape[0] // 2
+    chain_iota = lax.broadcasted_iota(jnp.int32, (leaving, chains), 1)
     for i, out in enumerate((stay_ref, leave_ref)):
-        target = brick ^ i
-        chosen = []
-        for s in range(leaving):
-            number = jnp.where(s < live_ref[target], list_ref[target, s], -1)
-            chosen.append(jnp.where(chain_iota == number, 1.0, 0.0))
-        chosen = jnp.concatenate(chosen, axis=0)
+        numbers = number_ref[i * leaving : (i + 1) * leaving, :1]
+        chosen = jnp.where(chain_iota == numbers, 1.0, 0.0)
         for k in range(3):
             out[:, k * beads : (k + 1) * beads] = lax.dot_general(
                 chosen, moved_ref[k], NT, precision=highest, preferred_element_type=f32
             )
-
-    step = 32
-    step_iota = lax.broadcasted_iota(jnp.int32, (step, 128), 0)
-    for r in range(slots):
-        for tile in range(chains // 128):
-            lanes = slice(tile * 128, tile * 128 + 128)
-            wide = slice(r * chains + tile * 128, r * chains + tile * 128 + 128)
-            for start in range(0, length, step):
-                parts = [jnp.zeros((step, 128), f32) for _ in range(3)]
-                for j in range(per_slot):
-                    at = slice(r * per_slot + j, r * per_slot + j + 1)
-                    here = step_iota == site_ref[at, lanes] - start
-                    for k in range(3):
-                        parts[k] = parts[k] + jnp.where(here, force[k, at, lanes], 0.0)
-                for k in range(3):
-                    out = slice(k * length + start, k * length + start + step)
-                    spread[out, wide] = parts[k].astype(bf16)
-
-    sums[...] = lax.dot_general(onehot[...], spread[...], NT, preferred_element_type=f32)
-    own_ref[...] = sums[:block, :]
-    for m in range(1, inner):
-        send_refs[m - 1][...] = sums[m * block : (m + 1) * block, :].astype(bf16)
+    own_ref[:main, :] = lax.dot_general(
+        hot_ref[...], spread_ref[...], NT, preferred_element_type=f32
+    )
+    own_ref[main:, :] = lax.dot_general(
+        extras_ref[:tail, :], spread_ref[...], NT, preferred_element_type=f32
+    )
 
 
 def sum_kernel(plan, own_ref, *refs):
@@ -515,34 +548,58 @@
     groups = lax.axis_size("chain")
     bricks = lax.axis_size("brick")
     capacity = send_rows.shape[-1]
-    plan = Plan(groups, size_x * size_y, size_y)
+    plan = Plan(groups, size_x * size_y, size_y, length)
     inner, outer = plan.inner, plan.outer
     beads, chains = positions.shape[3:]
     slots = chain_slots.shape[2]
     shape = jax.ShapeDtypeStruct
     width = 3 * length
     edge = shape((len(MOVES_UP) + 4, size_x, length), f32)
+    leaving = migrate_list.shape[-1]
 
     params = pltpu.CompilerParams
     first = pl.pallas_call(
         functools.partial(moment_kernel, plan),
         out_shape=[shape((plan.stride, width), bf16)] * outer
-        + [edge, edge, shape((4, plan.rows, length), f32), shape((slots, chains), jnp.int32)],
-        in_specs=[HBM] * 4,
-        out_specs=[VMEM] * (outer + 4),
+        + [edge, edge, shape((4, plan.rows, length), f32), shape((slots, chains), jnp.int32)]
+        + [shape((bricks * leaving, length), jnp.int32)],
+        in_specs=[HBM] * 6,
+        out_specs=[VMEM] * (outer + 5),
         scratch_shapes=[
             pltpu.VMEM(populations.shape, f32),
             pltpu.VMEM((groups, capacity), jnp.int32),
             pltpu.SMEM((groups,), jnp.int32),
-            pltpu.SemaphoreType.DMA((size_x + 3,)),
+            pltpu.SMEM((bricks, leaving), jnp.int32),
+            pltpu.SMEM((bricks,), jnp.int32),
+            pltpu.SemaphoreType.DMA((size_x + 5,)),
         ],
-        compiler_params=params(vmem_limit_bytes=6 << 20),
+        compiler_params=params(vmem_limit_bytes=62 << 20),
         name="moments",
-    )(populations, send_rows[0, 0], send_count[0, 0], chain_slots[0, 0])
-    msgs, (edge_up, edge_down, sites, slot_list) = first[:outer], first[outer:]
+    )(
+        populations,
+        send_rows[0, 0],
+        send_count[0, 0],
+        chain_slots[0, 0],
+        migrate_list[0, 0],
+        migrate_count[0, 0],
+    )
+    msgs, (edge_up, edge_down, sites, slot_list, numbers) = first[:outer], first[outer:]
     parts = [msgs[0]]
     for k in range(1, outer):
-        parts.append(lax.ppermute(msgs[k], "chain", plan.outer_shift(-k)))
+        parts.append(lax.ppermute(msgs[k], "chain", plan.outer_swap(k)))
+    basis, spectrum = rouse_tables(beads)
+    own_rows, bead, damping = pl.pallas_call(
+        functools.partial(prepare_kernel, plan),
+        out_shape=[
+            shape((plan.stride, width), bf16),
+            shape((slots * length, chains), jnp.int32),
+            shape((beads, chains), f32),
+        ],
+        in_specs=[VMEM] * 4,
+        out_specs=[VMEM] * 3,
+        compiler_params=params(vmem_limit_bytes=6 << 20),
+        name="prepare",
+    )(msgs[0], positions[0, 0], bead_site[0, 0], spectrum)
     near = pl.pallas_call(
         functools.partial(pack_kernel, plan),
         out_shape=shape((plan.block, width), bf16),
@@ -550,59 +607,74 @@
         out_specs=VMEM,
         compiler_params=params(vmem_limit_bytes=4 << 20),
         name="pack",
-    )(*parts)
+    )(own_rows, *parts[1:])
     blocks = [near]
     for m in range(1, inner):
-        blocks.append(lax.ppermute(blocks[0], "chain", plan.inner_swap(m)))
+        blocks.append(lax.ppermute(near, "chain", plan.inner_swap(m)))
     up = [(i, (i + 1) % groups) for i in range(groups)]
     down = [(j, i) for i, j in up]
     low = lax.ppermute(edge_up, "chain", up)
-    high = lax.ppermute(edge_down, "chain", down)
-    blocks, low, high = lax.optimization_barrier((blocks, low, high))
-
-    basis, spectrum = rouse_tables(beads)
-    total = inner * plan.block
-    leaving = migrate_list.shape[-1]
+
+    items = slots * chains
+    hot = shape((plan.main, items), bf16)
+    hots, before = [], []
+    for m in range(inner - 1):
+        one, *before = pl.pallas_call(
+            functools.partial(pick_kernel, plan, capacity, m),
+            out_shape=[hot, shape((width, items), bf16), shape((slots, chains), jnp.int32)],
+            in_specs=[VMEM] * (2 + len(before)),
+            out_specs=[VMEM] * 3,
+            scratch_shapes=[pltpu.VMEM((width, plan.main), bf16)],
+            compiler_params=params(vmem_limit_bytes=8 << 20),
+            name="pick",
+        )(blocks[m], slot_list, *before)
+        hots.append(one)
     second = pl.pallas_call(
         functools.partial(chain_kernel, plan, capacity),
-        out_shape=[shape((plan.block, width), f32)]
-        + [shape((plan.block, width), bf16)] * (inner - 1)
-        + [shape((3, beads, chains), f32)]
-        + [shape((leaving, 3 * beads), f32)] * 2,
-        in_specs=[VMEM] * (inner + 3) + [HBM, HBM] + [VMEM, VMEM],
-        out_specs=[VMEM] * (inner + 3),
+        out_shape=[shape((plan.block, width), bf16)] * (inner - 1)
+        + [
+            shape((3, beads, chains), f32),
+            shape((width, items), bf16),
+            shape((inner * (plan.block - plan.main), items), bf16),
+        ],
+        in_specs=[VMEM] * (inner + 8),
+        out_specs=[VMEM] * (inner + 2),
         scratch_shapes=[
-            pltpu.VMEM((total, width), bf16),
-            pltpu.VMEM((width, total), bf16),
-            pltpu.VMEM((total, slots * chains), bf16),
-            pltpu.VMEM((width, slots * chains), f32),
+            pltpu.VMEM((width, plan.main), bf16),
+            pltpu.VMEM((plan.main, items), bf16),
+            pltpu.VMEM((width, items), f32),
             pltpu.VMEM((3, beads, chains), f32),
             pltpu.VMEM((3, beads, chains), f32),
-            pltpu.VMEM((width, slots * chains), bf16),
-            pltpu.VMEM((total, width), f32),
-            pltpu.SMEM((bricks, leaving), jnp.int32),
-            pltpu.SMEM((bricks,), jnp.int32),
-            pltpu.SemaphoreType.DMA((2,)),
         ],
-        compiler_params=params(vmem_limit_bytes=(12 << 20) + total * 8192),
+        compiler_params=params(vmem_limit_bytes=16 << 20),
         name="chains",
     )(
-        *blocks,
+        *hots,
+        blocks[inner - 1],
+        slot_list,
+        *before,
         positions[0, 0],
         bead_site[0, 0],
-        slot_list,
-        migrate_list[0, 0],
-        migrate_count[0, 0],
+        bead,
+        damping,
         basis,
-        spectrum,
     )
-    own, sends = second[0], second[1:inner]
-    moved, stay, leave = second[inner:]
+    sends, (moved, spread, extras) = second[: inner - 1], second[inner - 1 :]
     came = []
     for m in range(1, inner):
         came.append(lax.ppermute(sends[m - 1], "chain", plan.inner_swap(m)))
+    own, stay, leave = pl.pallas_call(
+        functools.partial(own_kernel, plan),
+        out_shape=[shape((plan.block, width), f32)]
+        + [shape((leaving, 3 * beads), f32)] * 2,
+        in_specs=[VMEM] * 5,
+        out_specs=[VMEM] * 3,
+        compiler_params=params(vmem_limit_bytes=8 << 20),
+        name="own",
+    )(hots[0], extras, spread, moved, numbers)
     swap = [(i, (i + 1) % bricks) for i in range(bricks)]
     arrived = lax.ppermute(leave, "brick", swap)
+    high = lax.ppermute(edge_down, "chain", down)
     came, arrived = lax.optimization_barrier((came, arrived))
     kept, *outgoing = pl.pallas_call(
         functools.partial(sum_kernel, plan),
@@ -615,7 +687,7 @@
     )(own, *came)
     came = []
     for k in range(1, outer):
-        came.append(lax.ppermute(outgoing[k - 1], "chain", plan.outer_shift(k)))
+        came.append(lax.ppermute(outgoing[k - 1], "chain", plan.outer_swap(k)))
     crossing, state, edges = pl.pallas_call(
         functools.partial(cross_kernel, plan),
         out_shape=[

time: 56.4 us -> 53.9 us (0.956)
  starting transfers between devices: 26.2 us -> 23 us
  Pallas kernels: 9.94 us -> 11.2 us
  local copies, waits for them, and re-layouts: 3.27 us -> 2.04 us
  waiting for transfers between devices: 15.3 us -> 16 us
    ppermute x9, waiting for transfers between devices: 7.27 us -> 11 us  [the longest x3 6.39 us: local(): blocks.append(lax.ppermute(near, 'chain', plan.inner_swap(m)))]
    pallas_call x1, Pallas kernels: 7.03 us -> 3.37 us  [local(): pl.pallas_call(functools.partial(chain_kernel, plan, capacity), out_shape...]
    pallas_call x0 -> x5, Pallas kernels: none -> 3.53 us  [the longest x3 1.9 us: local(): pl.pallas_call(functools.partial(pick_kernel, plan, capacity, m), out_sha...]
    ppermute x9, starting transfers between devices: 16.9 us -> 13.7 us  [the longest x3 5.71 us: local(): parts.append(lax.ppermute(msgs[k], 'chain', plan.outer_swap(k)))]
    ppermute x3, waiting for transfers between devices: 5.14 us -> 2.27 us  [local(): came.append(lax.ppermute(sends[m - 1], 'chain', plan.inner_swap(m)))]
    pallas_call x1, Pallas kernels: 0.68 us -> 2.05 us  [local(): pl.pallas_call(functools.partial(moment_kernel, plan), out_shape=[shape((...]
    unnamed x22 -> x24, local copies, waits for them, and re-layouts: 3.11 us -> 1.88 us
  transfers between devices with their start and end apart: 16 -> 16, of which waited for: 9 -> 8; matrix products, arithmetic and copies ran while one was open for 1% -> 1% of each run, Pallas kernels for 2% -> 9%
where the time goes in v3:
time: 53.9 us; the launch traced here: 53.6 us
  starting transfers between devices  23 us (43%)
  waiting for transfers between devices  16 us (30%)
  Pallas kernels  11.2 us (21%)
  local copies, waits for them, and re-layouts  2.04 us (4%)
  between operations  0.82 us (2%)
  other arithmetic  0.63 us (1%)
    ppermute x3, waiting for transfers between devices, local(): blocks.append(lax.ppermute(near, 'chain', plan.inner_swap(m)))  6.39 us
    ppermute x3, starting transfers between devices, local(): parts.append(lax.ppermute(msgs[k], 'chain', plan.outer_swap(k)))  5.71 us
    ppermute x3, waiting for transfers between devices, local(): parts.append(lax.ppermute(msgs[k], 'chain', plan.outer_swap(k)))  4.64 us
    ppermute x3, starting transfers between devices, local(): came.append(lax.ppermute(outgoing[k - 1], 'chain', plan.outer_swap(k)))  4.44 us
    ppermute x1, starting transfers between devices, local(): high = lax.ppermute(edge_down, 'chain', down)  4.37 us
    ppermute x3, starting transfers between devices, local(): blocks.append(lax.ppermute(near, 'chain', plan.inner_swap(m)))  3.55 us
    ppermute x3, starting transfers between devices, local(): came.append(lax.ppermute(sends[m - 1], 'chain', plan.inner_swap(m)))  3.55 us
    pallas_call x1, Pallas kernels, local(): pl.pallas_call(functools.partial(chain_kernel, plan, capacity), out_shape...  3.37 us
  transfers between devices with their start and end apart: 16, of which 8 were waited for; matrix products, arithmetic and copies ran while one was open for 1% of the time, Pallas kernels for 9%

profile of v3, /device:TPU:0, one launch (start us, length us, event | category | flops | bytes accessed | tf_op | source)
XLA Modules:
  0.0 53.6 jit_solution(18376266000773227579)
XLA Ops:
  0.7 0.0 copy-start.8
  0.7 2.1 %moments.1 = (bf16[72,384]{1,0:T(8,128)(2,1)}, bf16[72,384]{1,0:T(8,128)(2,1)}, bf16[72,384]{1,0:T(8,128)(2,1)}, bf16[72,384]{1,0:T(8,128)(2,1)}, f32[9,2,128]{2...) custom-call(f32[19,2,32,128]{3,2,1,0:T(8,128)} %pop_ref.3, ...), custom_call_target="tpu_custom_call" | custom-call | tf_op jit(solution)/shard_map/moments/pallas_call | solution.py:561
  2.7 3.1 %collective-permute-start = (bf16[72,384]{1,0:T(8,128)(2,1)}, bf16[72,384]{1,0:T(8,128)(2,1)S(1)}, u32[]{:S(2)}, u32[]{:S(2)}) collective-permute-start(bf16[72,384]{1,0:T(8,128)(2,1)} %get-tuple-element.47), channel_id=1, source_target_pairs={{0,4},{1,5},{2,6},{3,7},{4,0},{5,1},{6,2},{7,3},{8,12},{9,13},{10,... | collective-permute-start | bytes 165896 | tf_op jit(solution)/shard_map/ppermute | solution.py:589
  5.8 2.6 %collective-permute-start.1 = (bf16[72,384]{1,0:T(8,128)(2,1)}, bf16[72,384]{1,0:T(8,128)(2,1)S(1)}, u32[]{:S(2)}, u32[]{:S(2)}) collective-permute-start(bf16[72,384]{1,0:T(8,128)(2,1)} %get-tuple-element.48), channel_id=1, source_target_pairs={{0,8},{1,9},{2,10},{3,11},{4,12},{5,13},{6,14},{7,15},{8,0},{9,1},... | collective-permute-start | bytes 165896 | tf_op jit(solution)/shard_map/ppermute | solution.py:589
  8.4 0.0 collective-permute-start.2
  8.5 0.0 copy-start.6
  8.5 0.8 %copy-done.6 = bf16[72,384]{1,0:T(8,128)(2,1)S(1)} copy-done((bf16[72,384]{1,0:T(8,128)(2,1)S(1)}, bf16[72,384]{1,0:T(8,128)(2,1)}, u32[]{:S(2)}) %copy-start.6) | copy-done | bytes 55320
  9.3 0.7 %prepare.1 = (bf16[72,384]{1,0:T(8,128)(2,1)S(1)}, s32[512,256]{1,0:T(8,128)S(1)}, f32[64,256]{1,0:T(8,128)S(1)}) custom-call(bf16[72,384]{1,0:T(8,128)(2,1)S(1)} %copy-done.6, f32[3,64,256]{2,1,0:T(8,128)S(1)} %bitcast.8, s32[64,256]{1,0:T(8,128)S(1)} %bitcast.10, f32[64,1]{1,0:T(8,128)S(1)} %copy-done.8), custom_call_target="tpu_custom_call" | custom-call | tf_op jit(solution)/shard_map/prepare/pallas_call | solution.py:591
  10.0 0.0 collective-permute-done.refs_1_
  10.0 2.2 %collective-permute-done.1.refs_2_ = bf16[72,384]{1,0:T(8,128)(2,1)S(1)} collective-permute-done((bf16[72,384]{1,0:T(8,128)(2,1)}, bf16[72,384]{1,0:T(8,128)(2,1)S(1)}, u32[]{:S(2)}, u32[]{:S(2)}) %collective-permute-start.1) | collective-permute-done | bytes 55328 | tf_op jit(solution)/shard_map/ppermute | solution.py:589
  12.2 2.4 %collective-permute-done.2.refs_3_ = bf16[72,384]{1,0:T(8,128)(2,1)S(1)} collective-permute-done((bf16[72,384]{1,0:T(8,128)(2,1)}, bf16[72,384]{1,0:T(8,128)(2,1)S(1)}, u32[]{:S(2)}, u32[]{:S(2)}) %collective-permute-start.2) | collective-permute-done | bytes 55328 | tf_op jit(solution)/shard_map/ppermute | solution.py:589
  14.6 1.6 %collective-permute-start.3 = (bf16[272,384]{1,0:T(8,128)(2,1)S(1)}, bf16[272,384]{1,0:T(8,128)(2,1)S(1)}, u32[]{:S(2)}, u32[]{:S(2)}) collective-permute-start(bf16[272,384]{1,0:T(8,128)(2,1)S(1)} %pack.1.block_ref), channel_id=1, source_target_pairs={{0,1},{1,0},{2,3},{3,2},{4,5},{5,4},{6,7},{7,6},{8,9},{9,8},{10,11... | collective-permute-start | bytes 626696 | tf_op jit(solution)/shard_map/ppermute | solution.py:613
  16.2 1.5 %collective-permute-start.4 = (bf16[272,384]{1,0:T(8,128)(2,1)S(1)}, bf16[272,384]{1,0:T(8,128)(2,1)S(1)}, u32[]{:S(2)}, u32[]{:S(2)}) collective-permute-start(bf16[272,384]{1,0:T(8,128)(2,1)S(1)} %pack.1.block_ref), channel_id=1, source_target_pairs={{0,2},{1,3},{2,0},{3,1},{4,6},{5,7},{6,4},{7,5},{8,10},{9,11},{10,... | collective-permute-start | bytes 626696 | tf_op jit(solution)/shard_map/ppermute | solution.py:613
  17.7 0.5 collective-permute-start.5
  18.2 0.6 %pick.3 = (bf16[256,1024]{1,0:T(8,128)(2,1)S(1)}, bf16[384,1024]{1,0:T(8,128)(2,1)S(1)}, s32[4,256]{1,0:T(4,128)S(1)}) custom-call(bf16[272,384]{1,0:T(8,128)(2,1)S(1)} %pack.1.block_ref, s32[4,256]{1,0:T(4,128)S(1)} %copy-done.5), custom_call_target="tpu_custom_call" | custom-call | tf_op jit(solution)/shard_map/pick/pallas_call | solution.py:622
  18.8 3.6 %collective-permute-done.3.block_ref = bf16[272,384]{1,0:T(8,128)(2,1)S(1)} collective-permute-done((bf16[272,384]{1,0:T(8,128)(2,1)S(1)}, bf16[272,384]{1,0:T(8,128)(2,1)S(1)}, u32[]{:S(2)}, u32[]{:S(2)}) %collective-permute-start.3) | collective-permute-done | bytes 208928 | tf_op jit(solution)/shard_map/ppermute | solution.py:613
  22.4 0.6 %pick.4 = (bf16[256,1024]{1,0:T(8,128)(2,1)S(1)}, bf16[384,1024]{1,0:T(8,128)(2,1)S(1)}, s32[4,256]{1,0:T(4,128)S(1)}) custom-call(bf16[272,384]{1,0:T(8,128)(2,1)S(1)} %collective-permute-done.3.block_ref, s32[4,256]{1,0:T(4,128)S(1)} %copy-done.5, bf16[384,1024]{1,0:T(8,128)(2,1)S(1)} %get-tuple-element.52.refs_0_, s32[4,256]{1,0:T(4,128)S(1)} %get-tuple-element.53.refs_1_), custom_call_target="tpu_custom_call" | custom-call | tf_op jit(solution)/shard_map/pick/pallas_call | solution.py:622
  23.0 2.8 %collective-permute-done.4.block_ref = bf16[272,384]{1,0:T(8,128)(2,1)S(1)} collective-permute-done((bf16[272,384]{1,0:T(8,128)(2,1)S(1)}, bf16[272,384]{1,0:T(8,128)(2,1)S(1)}, u32[]{:S(2)}, u32[]{:S(2)}) %collective-permute-start.4) | collective-permute-done | bytes 208928 | tf_op jit(solution)/shard_map/ppermute | solution.py:613
  25.9 0.6 %pick.5 = (bf16[256,1024]{1,0:T(8,128)(2,1)S(1)}, bf16[384,1024]{1,0:T(8,128)(2,1)S(1)}, s32[4,256]{1,0:T(4,128)S(1)}) custom-call(bf16[272,384]{1,0:T(8,128)(2,1)S(1)} %collective-permute-done.4.block_ref, s32[4,256]{1,0:T(4,128)S(1)} %copy-done.5, bf16[384,1024]{1,0:T(8,128)(2,1)S(1)} %get-tuple-element.55.refs_0_, s32[4,256]{1,0:T(4,128)S(1)} %get-tuple-element.56.refs_1_), custom_call_target="tpu_custom_call" | custom-call | tf_op jit(solution)/shard_map/pick/pallas_call | solution.py:622
  26.5 0.1 copy-done.7
  26.6 3.4 %chains.1 = (bf16[272,384]{1,0:T(8,128)(2,1)S(1)}, bf16[272,384]{1,0:T(8,128)(2,1)S(1)}, bf16[272,384]{1,0:T(8,128)(2,1)S(1)}, f32[3,64,256]{2,1,0:T(8,128)}, bf...) custom-call(bf16[256,1024]{1,0:T(8,128)(2,1)S(1)} %get-tuple-element.51.refs_0_.hot_ref, ...), custom_call_target="tpu_custom_call" | custom-call | tf_op jit(solution)/shard_map/chains/pallas_call | solution.py:632
  30.0 0.4 collective-permute-start.6
  30.4 1.6 %collective-permute-start.7 = (bf16[272,384]{1,0:T(8,128)(2,1)S(1)}, bf16[272,384]{1,0:T(8,128)(2,1)S(1)}, u32[]{:S(2)}, u32[]{:S(2)}) collective-permute-start(bf16[272,384]{1,0:T(8,128)(2,1)S(1)} %get-tuple-element.68), channel_id=1, source_target_pairs={{0,2},{1,3},{2,0},{3,1},{4,6},{5,7},{6,4},{7,5},{8,10},{9,11},{10,... | collective-permute-start | bytes 626696 | tf_op jit(solution)/shard_map/ppermute | solution.py:665
  32.0 1.6 %collective-permute-start.8 = (bf16[272,384]{1,0:T(8,128)(2,1)S(1)}, bf16[272,384]{1,0:T(8,128)(2,1)S(1)}, u32[]{:S(2)}, u32[]{:S(2)}) collective-permute-start(bf16[272,384]{1,0:T(8,128)(2,1)S(1)} %get-tuple-element.69), channel_id=1, source_target_pairs={{0,3},{1,2},{2,1},{3,0},{4,7},{5,6},{6,5},{7,4},{8,11},{9,10},{10,... | collective-permute-start | bytes 626696 | tf_op jit(solution)/shard_map/ppermute | solution.py:665
  33.6 0.9 %copy-done.3 = f32[3,64,256]{2,1,0:T(8,128)S(1)} copy-done((f32[3,64,256]{2,1,0:T(8,128)S(1)}, f32[3,64,256]{2,1,0:T(8,128)}, u32[]{:S(2)}) %copy-start.3) | copy-done | bytes 196632
  34.5 1.0 %own.1 = (f32[272,384]{1,0:T(8,128)S(1)}, f32[8,192]{1,0:T(8,128)S(1)}, f32[8,192]{1,0:T(8,128)S(1)}) custom-call(bf16[256,1024]{1,0:T(8,128)(2,1)S(1)} %get-tuple-element.51.refs_0_.hot_ref, bf16[64,1024]{1,0:T(8,128)(2,1)S(1)} %get-tuple-element.62.extras_ref, bf16[384,1024]{1,0:T(8,128)(2,1)S(1)} %get-tuple-element.63.spread_ref, ...), custom_call_target="tpu_custom_call" | custom-call | tf_op jit(solution)/shard_map/own/pallas_call | solution.py:666
  35.4 0.0 collective-permute-start.9
  35.4 1.2 %collective-permute-done.9 = f32[8,192]{1,0:T(8,128)S(1)} collective-permute-done((f32[8,192]{1,0:T(8,128)S(1)}, f32[8,192]{1,0:T(8,128)S(1)}, u32[]{:S(2)}, u32[]{:S(2)}) %collective-permute-start.9) | collective-permute-done | bytes 6176 | tf_op jit(solution)/shard_map/ppermute | solution.py:676
  36.6 0.0 collective-permute-done.6.refs_0_
  36.6 0.9 %collective-permute-done.7.refs_1_ = bf16[272,384]{1,0:T(8,128)(2,1)S(1)} collective-permute-done((bf16[272,384]{1,0:T(8,128)(2,1)S(1)}, bf16[272,384]{1,0:T(8,128)(2,1)S(1)}, u32[]{:S(2)}, u32[]{:S(2)}) %collective-permute-start.7) | collective-permute-done | bytes 208928 | tf_op jit(solution)/shard_map/ppermute | solution.py:665
  37.5 1.3 %collective-permute-done.8.refs_2_ = bf16[272,384]{1,0:T(8,128)(2,1)S(1)} collective-permute-done((bf16[272,384]{1,0:T(8,128)(2,1)S(1)}, bf16[272,384]{1,0:T(8,128)(2,1)S(1)}, u32[]{:S(2)}, u32[]{:S(2)}) %collective-permute-start.8) | collective-permute-done | bytes 208928 | tf_op jit(solution)/shard_map/ppermute | solution.py:665
  38.9 0.1 sums.1
  39.0 0.1 collective-permute-start.10
  39.1 1.7 %collective-permute-start.11 = (bf16[72,384]{1,0:T(8,128)(2,1)S(1)}, bf16[72,384]{1,0:T(8,128)(2,1)S(1)}, u32[]{:S(2)}, u32[]{:S(2)}) collective-permute-start(bf16[72,384]{1,0:T(8,128)(2,1)S(1)} %get-tuple-element.76), channel_id=1, source_target_pairs={{0,8},{1,9},{2,10},{3,11},{4,12},{5,13},{6,14},{7,15},{8,0},{9,1},... | collective-permute-start | bytes 165896 | tf_op jit(solution)/shard_map/ppermute | solution.py:690
  40.8 2.7 %collective-permute-start.12 = (bf16[72,384]{1,0:T(8,128)(2,1)S(1)}, bf16[72,384]{1,0:T(8,128)(2,1)S(1)}, u32[]{:S(2)}, u32[]{:S(2)}) collective-permute-start(bf16[72,384]{1,0:T(8,128)(2,1)S(1)} %get-tuple-element.77), channel_id=1, source_target_pairs={{0,12},{1,13},{2,14},{3,15},{4,8},{5,9},{6,10},{7,11},{8,4},{9,5},... | collective-permute-start | bytes 165896 | tf_op jit(solution)/shard_map/ppermute | solution.py:690
  43.5 1.3 %collective-permute-start.13 = (f32[9,2,128]{2,1,0:T(2,128)S(1)}, f32[9,2,128]{2,1,0:T(2,128)S(1)}, u32[]{:S(2)}, u32[]{:S(2)}) collective-permute-start(f32[9,2,128]{2,1,0:T(2,128)S(1)} %copy-done.11), channel_id=1, source_target_pairs={{0,1},{1,2},{2,3},{3,4},{4,5},{5,6},{6,7},{7,8},{8,9},{9,10},{10,1... | collective-permute-start | bytes 27656 | tf_op jit(solution)/shard_map/ppermute | solution.py:616
  44.7 4.4 %collective-permute-start.14 = (f32[9,2,128]{2,1,0:T(2,128)S(1)}, f32[9,2,128]{2,1,0:T(2,128)S(1)}, u32[]{:S(2)}, u32[]{:S(2)}) collective-permute-start(f32[9,2,128]{2,1,0:T(2,128)S(1)} %copy-done.10), channel_id=1, source_target_pairs={{1,0},{2,1},{3,2},{4,3},{5,4},{6,5},{7,6},{8,7},{9,8},{10,9},{11,1... | collective-permute-start | bytes 27656 | tf_op jit(solution)/shard_map/ppermute | solution.py:677
  49.1 0.1 concatenate.24
  49.2 0.1 concatenate.25
  49.3 1.5 %collective-permute-done.13.refs_4_ = f32[9,2,128]{2,1,0:T(2,128)S(1)} collective-permute-done((f32[9,2,128]{2,1,0:T(2,128)S(1)}, f32[9,2,128]{2,1,0:T(2,128)S(1)}, u32[]{:S(2)}, u32[]{:S(2)}) %collective-permute-start.13) | collective-permute-done | bytes 9248 | tf_op jit(solution)/shard_map/ppermute | solution.py:616
  50.7 0.0 collective-permute-done.14.refs_5_
  50.7 0.0 collective-permute-done.10.refs_1_
  50.7 0.0 collective-permute-done.11.refs_2_
  50.8 0.3 cross.1
  51.1 0.1 collective-permute-start.15
  51.1 0.6 %maximum_select_fusion = f32[1,1,2,1536]{3,2,1,0:T(2,128)} fusion(f32[1,1,1,1536]{3,2,1,0:T(1,128)S(1)} %concatenate.25, f32[1,1,1,1536]{3,2,1,0:T(1,128)S(1)} %concatenate.24, pred[]{:T(512)S(6)} %eq.3), kind=kLoop, calls=%fused_computation | loop fusion | flops 9216 | bytes 24577 | tf_op jit(solution)/shard_map/jit(_where)/select_n | solution.py:725
  51.8 1.1 %collide.1.part_ref = f32[19,2,32,128]{3,2,1,0:T(8,128)} custom-call(f32[19,2,32,128]{3,2,1,0:T(8,128)S(1)} %copy-done, f32[5,64,128]{2,1,0:T(8,128)S(1)} %get-tuple-element.81.state_ref, f32[19,2,128]{2,1,0:T(2,128)S(1)} %get-tuple-element.82.edge_ref), custom_call_target="tpu_custom_call" | custom-call | tf_op jit(solution)/shard_map/collide/pallas_call | solution.py:704
  52.8 0.7 %merge.1 = f32[19,2,32,128]{3,2,1,0:T(8,128)} custom-call(f32[10,32,128]{2,1,0:T(8,128)S(1)} %collective-permute-done.15.came_ref, f32[19,2,32,128]{3,2,1,0:T(8,128)} %collide.1.part_ref), custom_call_target="tpu_custom_call", output_to_operand_aliasing={{}: (1, {})} | custom-call | tf_op jit(solution)/shard_map/merge/pallas_call | solution.py:712
  (23 shorter events, 0.1 us)
Async XLA Ops:
  0.6 7.8 %copy-start.1 = (f32[1,1,3,64,256]{4,3,2,1,0:T(8,128)S(1)}, f32[1,1,3,64,256]{4,3,2,1,0:T(8,128)}, u32[]{:S(2)}) copy-start(f32[1,1,3,64,256]{4,3,2,1,0:T(8,128)} %param.11) | copy-start | bytes 589828
  0.6 7.8 %copy-start.2 = (s32[1,1,64,256]{3,2,1,0:T(8,128)S(1)}, s32[1,1,64,256]{3,2,1,0:T(8,128)}, u32[]{:S(2)}) copy-start(s32[1,1,64,256]{3,2,1,0:T(8,128)} %param.12) | copy-start | bytes 196612
  0.7 7.8 %copy-start.8 = (f32[64,1]{1,0:T(8,128)S(1)}, f32[64,1]{1,0:T(8,128)}, u32[]{:S(2)}) copy-start(f32[64,1]{1,0:T(8,128)} %constant.12.clone.spectrum_ref) | copy-start | bytes 772
  2.7 7.2 %collective-permute-start = (bf16[72,384]{1,0:T(8,128)(2,1)}, bf16[72,384]{1,0:T(8,128)(2,1)S(1)}, u32[]{:S(2)}, u32[]{:S(2)}) collective-permute-start(bf16[72,384]{1,0:T(8,128)(2,1)} %get-tuple-element.47), channel_id=1, source_target_pairs={{0,4},{1,5},{2,6},{3,7},{4,0},{5,1},{6,2},{7,3},{8,12},{9,13},{10,... | collective-permute-start | bytes 165896 | tf_op jit(solution)/shard_map/ppermute | solution.py:589
  5.8 6.3 %collective-permute-start.1 = (bf16[72,384]{1,0:T(8,128)(2,1)}, bf16[72,384]{1,0:T(8,128)(2,1)S(1)}, u32[]{:S(2)}, u32[]{:S(2)}) collective-permute-start(bf16[72,384]{1,0:T(8,128)(2,1)} %get-tuple-element.48), channel_id=1, source_target_pairs={{0,8},{1,9},{2,10},{3,11},{4,12},{5,13},{6,14},{7,15},{8,0},{9,1},... | collective-permute-start | bytes 165896 | tf_op jit(solution)/shard_map/ppermute | solution.py:589
  8.4 6.2 %collective-permute-start.2 = (bf16[72,384]{1,0:T(8,128)(2,1)}, bf16[72,384]{1,0:T(8,128)(2,1)S(1)}, u32[]{:S(2)}, u32[]{:S(2)}) collective-permute-start(bf16[72,384]{1,0:T(8,128)(2,1)} %get-tuple-element.49), channel_id=1, source_target_pairs={{0,12},{1,13},{2,14},{3,15},{4,8},{5,9},{6,10},{7,11},{8,4},{9,5},... | collective-permute-start | bytes 165896 | tf_op jit(solution)/shard_map/ppermute | solution.py:589
  8.5 0.8 %copy-start.6 = (bf16[72,384]{1,0:T(8,128)(2,1)S(1)}, bf16[72,384]{1,0:T(8,128)(2,1)}, u32[]{:S(2)}) copy-start(bf16[72,384]{1,0:T(8,128)(2,1)} %get-tuple-element.45.own_ref) | copy-start | bytes 165892
  14.6 3.6 %copy-start.5 = (s32[4,256]{1,0:T(4,128)S(1)}, s32[4,256]{1,0:T(4,128)}, u32[]{:S(2)}) copy-start(s32[4,256]{1,0:T(4,128)} %get-tuple-element.50.slot_ref.refs_4_) | copy-start | bytes 12292
  14.6 7.8 %collective-permute-start.3 = (bf16[272,384]{1,0:T(8,128)(2,1)S(1)}, bf16[272,384]{1,0:T(8,128)(2,1)S(1)}, u32[]{:S(2)}, u32[]{:S(2)}) collective-permute-start(bf16[272,384]{1,0:T(8,128)(2,1)S(1)} %pack.1.block_ref), channel_id=1, source_target_pairs={{0,1},{1,0},{2,3},{3,2},{4,5},{5,4},{6,7},{7,6},{8,9},{9,8},{10,11... | collective-permute-start | bytes 626696 | tf_op jit(solution)/shard_map/ppermute | solution.py:613
  16.2 9.7 %collective-permute-start.4 = (bf16[272,384]{1,0:T(8,128)(2,1)S(1)}, bf16[272,384]{1,0:T(8,128)(2,1)S(1)}, u32[]{:S(2)}, u32[]{:S(2)}) collective-permute-start(bf16[272,384]{1,0:T(8,128)(2,1)S(1)} %pack.1.block_ref), channel_id=1, source_target_pairs={{0,2},{1,3},{2,0},{3,1},{4,6},{5,7},{6,4},{7,5},{8,10},{9,11},{10,... | collective-permute-start | bytes 626696 | tf_op jit(solution)/shard_map/ppermute | solution.py:613
  17.7 8.8 %collective-permute-start.5 = (bf16[272,384]{1,0:T(8,128)(2,1)S(1)}, bf16[272,384]{1,0:T(8,128)(2,1)S(1)}, u32[]{:S(2)}, u32[]{:S(2)}) collective-permute-start(bf16[272,384]{1,0:T(8,128)(2,1)S(1)} %pack.1.block_ref), channel_id=1, source_target_pairs={{0,3},{1,2},{2,1},{3,0},{4,7},{5,6},{6,5},{7,4},{8,11},{9,10},{10,... | collective-permute-start | bytes 626696 | tf_op jit(solution)/shard_map/ppermute | solution.py:613
  25.9 0.8 %copy-start.7 = (f32[64,64]{1,0:T(8,128)S(1)}, f32[64,64]{1,0:T(8,128)}, u32[]{:S(2)}) copy-start(f32[64,64]{1,0:T(8,128)} %constant.13.clone.refs_11_) | copy-start | bytes 49156
  30.0 3.6 %copy-start.9 = (s32[16,128]{1,0:T(8,128)S(1)}, s32[16,128]{1,0:T(8,128)}, u32[]{:S(2)}) copy-start(s32[16,128]{1,0:T(8,128)} %get-tuple-element.65.number_ref) | copy-start | bytes 24580
  30.0 6.6 %collective-permute-start.6 = (bf16[272,384]{1,0:T(8,128)(2,1)S(1)}, bf16[272,384]{1,0:T(8,128)(2,1)S(1)}, u32[]{:S(2)}, u32[]{:S(2)}) collective-permute-start(bf16[272,384]{1,0:T(8,128)(2,1)S(1)} %get-tuple-element.67), channel_id=1, source_target_pairs={{0,1},{1,0},{2,3},{3,2},{4,5},{5,4},{6,7},{7,6},{8,9},{9,8},{10,11... | collective-permute-start | bytes 626696 | tf_op jit(solution)/shard_map/ppermute | solution.py:665
  30.4 7.2 %collective-permute-start.7 = (bf16[272,384]{1,0:T(8,128)(2,1)S(1)}, bf16[272,384]{1,0:T(8,128)(2,1)S(1)}, u32[]{:S(2)}, u32[]{:S(2)}) collective-permute-start(bf16[272,384]{1,0:T(8,128)(2,1)S(1)} %get-tuple-element.68), channel_id=1, source_target_pairs={{0,2},{1,3},{2,0},{3,1},{4,6},{5,7},{6,4},{7,5},{8,10},{9,11},{10,... | collective-permute-start | bytes 626696 | tf_op jit(solution)/shard_map/ppermute | solution.py:665
  32.0 6.9 %collective-permute-start.8 = (bf16[272,384]{1,0:T(8,128)(2,1)S(1)}, bf16[272,384]{1,0:T(8,128)(2,1)S(1)}, u32[]{:S(2)}, u32[]{:S(2)}) collective-permute-start(bf16[272,384]{1,0:T(8,128)(2,1)S(1)} %get-tuple-element.69), channel_id=1, source_target_pairs={{0,3},{1,2},{2,1},{3,0},{4,7},{5,6},{6,5},{7,4},{8,11},{9,10},{10,... | collective-permute-start | bytes 626696 | tf_op jit(solution)/shard_map/ppermute | solution.py:665
  33.6 0.9 %copy-start.3 = (f32[3,64,256]{2,1,0:T(8,128)S(1)}, f32[3,64,256]{2,1,0:T(8,128)}, u32[]{:S(2)}) copy-start(f32[3,64,256]{2,1,0:T(8,128)} %get-tuple-element.64.moved_ref) | copy-start | bytes 589828
  35.4 15.3 %copy-start = (f32[19,2,32,128]{3,2,1,0:T(8,128)S(1)}, f32[19,2,32,128]{3,2,1,0:T(8,128)}, u32[]{:S(2)}) copy-start(f32[19,2,32,128]{3,2,1,0:T(8,128)} %pop_ref.3) | copy-start | bytes 1867780
  35.4 1.2 %collective-permute-start.9 = (f32[8,192]{1,0:T(8,128)S(1)}, f32[8,192]{1,0:T(8,128)S(1)}, u32[]{:S(2)}, u32[]{:S(2)}) collective-permute-start(f32[8,192]{1,0:T(8,128)S(1)} %get-tuple-element.70), channel_id=1, source_target_pairs={{0,16},{16,0},{1,17},{17,1},{2,18},{18,2},{3,19},{19,3},{4,20},{20... | collective-permute-start | bytes 18440 | tf_op jit(solution)/shard_map/ppermute | solution.py:676
  38.9 4.6 %copy-start.11 = (f32[9,2,128]{2,1,0:T(2,128)S(1)}, f32[9,2,128]{2,1,0:T(2,128)}, u32[]{:S(2)}) copy-start(f32[9,2,128]{2,1,0:T(2,128)} %get-tuple-element.78) | copy-start | bytes 27652
  38.9 11.9 %copy-start.4 = (f32[4,64,128]{2,1,0:T(8,128)S(1)}, f32[4,64,128]{2,1,0:T(8,128)}, u32[]{:S(2)}) copy-start(f32[4,64,128]{2,1,0:T(8,128)} %get-tuple-element.44.sites_ref) | copy-start | bytes 393220
  39.0 5.7 %copy-start.10 = (f32[9,2,128]{2,1,0:T(2,128)S(1)}, f32[9,2,128]{2,1,0:T(2,128)}, u32[]{:S(2)}) copy-start(f32[9,2,128]{2,1,0:T(2,128)} %get-tuple-element.79) | copy-start | bytes 27652
  39.0 11.7 %collective-permute-start.10 = (bf16[72,384]{1,0:T(8,128)(2,1)S(1)}, bf16[72,384]{1,0:T(8,128)(2,1)S(1)}, u32[]{:S(2)}, u32[]{:S(2)}) collective-permute-start(bf16[72,384]{1,0:T(8,128)(2,1)S(1)} %get-tuple-element.75), channel_id=1, source_target_pairs={{0,4},{1,5},{2,6},{3,7},{4,0},{5,1},{6,2},{7,3},{8,12},{9,13},{10,... | collective-permute-start | bytes 165896 | tf_op jit(solution)/shard_map/ppermute | solution.py:690
  39.1 11.6 %collective-permute-start.11 = (bf16[72,384]{1,0:T(8,128)(2,1)S(1)}, bf16[72,384]{1,0:T(8,128)(2,1)S(1)}, u32[]{:S(2)}, u32[]{:S(2)}) collective-permute-start(bf16[72,384]{1,0:T(8,128)(2,1)S(1)} %get-tuple-element.76), channel_id=1, source_target_pairs={{0,8},{1,9},{2,10},{3,11},{4,12},{5,13},{6,14},{7,15},{8,0},{9,1},... | collective-permute-start | bytes 165896 | tf_op jit(solution)/shard_map/ppermute | solution.py:690
  40.8 10.0 %collective-permute-start.12 = (bf16[72,384]{1,0:T(8,128)(2,1)S(1)}, bf16[72,384]{1,0:T(8,128)(2,1)S(1)}, u32[]{:S(2)}, u32[]{:S(2)}) collective-permute-start(bf16[72,384]{1,0:T(8,128)(2,1)S(1)} %get-tuple-element.77), channel_id=1, source_target_pairs={{0,12},{1,13},{2,14},{3,15},{4,8},{5,9},{6,10},{7,11},{8,4},{9,5},... | collective-permute-start | bytes 165896 | tf_op jit(solution)/shard_map/ppermute | solution.py:690
  43.5 7.3 %collective-permute-start.13 = (f32[9,2,128]{2,1,0:T(2,128)S(1)}, f32[9,2,128]{2,1,0:T(2,128)S(1)}, u32[]{:S(2)}, u32[]{:S(2)}) collective-permute-start(f32[9,2,128]{2,1,0:T(2,128)S(1)} %copy-done.11), channel_id=1, source_target_pairs={{0,1},{1,2},{2,3},{3,4},{4,5},{5,6},{6,7},{7,8},{8,9},{9,10},{10,1... | collective-permute-start | bytes 27656 | tf_op jit(solution)/shard_map/ppermute | solution.py:616
  44.7 6.0 %collective-permute-start.14 = (f32[9,2,128]{2,1,0:T(2,128)S(1)}, f32[9,2,128]{2,1,0:T(2,128)S(1)}, u32[]{:S(2)}, u32[]{:S(2)}) collective-permute-start(f32[9,2,128]{2,1,0:T(2,128)S(1)} %copy-done.10), channel_id=1, source_target_pairs={{1,0},{2,1},{3,2},{4,3},{5,4},{6,5},{7,6},{8,7},{9,8},{10,9},{11,1... | collective-permute-start | bytes 27656 | tf_op jit(solution)/shard_map/ppermute | solution.py:677
  51.1 1.8 %collective-permute-start.15 = (f32[10,32,128]{2,1,0:T(8,128)S(1)}, f32[10,32,128]{2,1,0:T(8,128)S(1)}, u32[]{:S(2)}, u32[]{:S(2)}) collective-permute-start(f32[10,32,128]{2,1,0:T(8,128)S(1)} %get-tuple-element.80), channel_id=1, source_target_pairs={{0,16},{16,0},{1,17},{17,1},{2,18},{18,2},{3,19},{19,3},{4,20},{20... | collective-permute-start | bytes 491528 | tf_op jit(solution)/shard_map/ppermute | solution.py:703
